TPU v7x, 32 devices: a whole 2x2x4 slice. The times are simulated.
32 devices in a mesh: view: 8 (over z, y), mp: 4 (over x, core).
Axes of the slice: x: 2, y: 2, z: 4, core: 2. Of those that a mesh axis runs over, the one named last changes fastest.
Arguments:
- tokens: bfloat16 [32, 384, 1024], P('view', None, 'mp'), may hold values from -6 to 6
- pairs: int32 [64, 2], P('view'), may hold values from 0 to 31, as said below
- w_embed: bfloat16 [1024, 768], replicated, may hold values from -0.1875 to 0.1875
- w_query: bfloat16 [2, 768, 768], replicated, may hold values from -8 to 8
- w_keyval: bfloat16 [2, 768, 1536], replicated, may hold values from -0.21875 to 0.21875
- w_out: bfloat16 [2, 768, 768], replicated, may hold values from -0.21875 to 0.21875
- w_head: bfloat16 [2, 4, 768], replicated, may hold values from -0.21875 to 0.21875
- gains: float32 [2, 3, 768], replicated, may hold values from 0.1 to 1.9
Outputs:
- view_sums: float32 [32, 4, 384], P('view')
Inputs may be any that keep to these rules, and one draw needn't show every extreme that they name: Owner of a view: view // 4. Among the 16 sides of the pairs of one index of view, at most 2 name views of one owner, and in every such block some owner is named exactly 2 times. The two views of a pair differ.
All inputs are finite; a program needn't handle non-finite values.
Results may differ from a plain program's by a relative error of at most 0.012.
Values may be sent and summed in bfloat16 or wider, within the bound.
No kernel may reach another device: no remote copies, remote signals or barrier semaphores. Data moves between devices by JAX's collectives and lax.ppermute only.
A program may use at most 128 MiB of HBM per device.

v0:
```python
import functools

import jax
import jax.numpy as jnp
from jax import lax
from jax.experimental import pallas as pl
from jax.experimental.pallas import tpu as pltpu
from jax.sharding import PartitionSpec as P

HEADS = 12
EPS = 1e-06
LOG2_E = 1.4426950408889634
HBM = pl.BlockSpec(memory_space=pltpu.HBM)
SMEM = pl.BlockSpec(memory_space=pltpu.SMEM)
VMEM = pl.BlockSpec(memory_space=pltpu.VMEM)


def xor_pairs(count, step):
    return [(i, i ^ step) for i in range(count)]


def load_kernel(*refs):
    count = len(refs) // 2
    copies = [pltpu.make_async_copy(refs[i], refs[count + i], refs[-1].at[i]) for i in range(count)]
    for copy in copies:
        copy.start()
    for copy in copies:
        copy.wait()


def embed_kernel(parts, cuts, me_ref, w_vmem, *refs):
    pieces, outs, whole = refs[:parts], refs[parts : parts + len(cuts)], refs[parts + len(cuts)]
    x_ref, emb_ref, in_sem, out_sem = refs[parts + len(cuts) + 1 :]
    views, _, feat = pieces[0].shape
    width = w_vmem.shape[1]
    column = me_ref[1]
    copies = []
    for j in range(parts):
        start = pl.multiple_of((column ^ j) * feat, feat)
        copies.append(
            pltpu.make_async_copy(pieces[j], x_ref.at[:, :, pl.ds(start, feat)], in_sem.at[j])
        )
        copies[-1].start()
    for copy in copies:
        copy.wait()
    copies = []
    for q, (first, size) in enumerate(cuts):
        emb = jnp.dot(
            x_ref[:, first : first + size, :].reshape(views * size, parts * feat),
            w_vmem[...],
            preferred_element_type=jnp.float32,
        )
        emb_ref[:, first : first + size, :] = emb.astype(jnp.bfloat16).reshape(views, size, width)
        copies.append(
            pltpu.make_async_copy(
                emb_ref.at[:, pl.ds(first, size), :], outs[q], out_sem.at[q]
            )
        )
        copies[-1].start()
    copies.append(pltpu.make_async_copy(emb_ref, whole, out_sem.at[len(cuts)]))
    copies[-1].start()
    for copy in copies:
        copy.wait()


def pick_kernel(lanes, reach, slots, cap, me_ref, line_ref, want_ref, *refs):
    count = 1 + 2 * reach
    own, below, above = refs[0], refs[1 : 1 + reach], refs[1 + reach : count]
    outs = refs[count : count + lanes]
    stage_ref, in_sem, out_sem = refs[count + lanes :]
    place, lane = me_ref[0] // lanes, me_ref[0] % lanes
    rows = line_ref.shape[0] * lanes

    def sources(act):
        for n, i in enumerate(slots):
            at = line_ref[i]
            if i == 0:
                act(pltpu.make_async_copy(own, stage_ref.at[n], in_sem.at[n]))
            for p in range(1, i + 1):
                for want, source in ((place - p, below[p - 1]), (place + p, above[p - 1])):

                    @pl.when(at == want)
                    def _():
                        act(pltpu.make_async_copy(source, stage_ref.at[n], in_sem.at[n]))

    sources(lambda copy: copy.start())
    sources(lambda copy: copy.wait())
    copies = []
    for j in range(lanes):
        for n, i in enumerate(slots):
            for c in range(cap):
                view = want_ref[(j * rows + line_ref[i] * lanes + lane) * cap + c]
                copies.append(
                    pltpu.make_async_copy(
                        stage_ref.at[n, jnp.maximum(view, 0)], outs[j].at[n, c], out_sem.at[len(copies)]
                    )
                )
                copies[-1].start()
    for copy in copies:
        copy.wait()


def route_kernel(lanes, parts, cap, base, cuts, groups, me_ref, line_ref, side_ref, *refs):
    count = len(cuts) * len(groups) * lanes
    fetched, outs = refs[:count], refs[count : count + parts]
    stage_ref, in_sem, out_sem = refs[count + parts :]
    lane, column = me_ref[0] % lanes, me_ref[1]

    def slots(act):
        number = 0
        for q, (first, size) in enumerate(cuts):
            for g, group in enumerate(groups):
                for j in range(lanes):
                    source = fetched[(q * len(groups) + g) * lanes + j]
                    for n, i in enumerate(group):
                        for c in range(cap):
                            side = side_ref[(line_ref[i] * lanes + (lane ^ j)) * cap + c]
                            part = source.at[n, c]
                            if source.shape[2] > size:
                                part = source.at[n, c, pl.ds(base + first, size)]

                            @pl.when(side >= 0)
                            def _():
                                act(
                                    pltpu.make_async_copy(
                                        part,
                                        stage_ref.at[side, pl.ds(first, size), :],
                                        in_sem.at[number],
                                    )
                                )

                            number += 1

    slots(lambda copy: copy.start())
    slots(lambda copy: copy.wait())
    copies = []
    for j in range(parts):
        copies.append(
            pltpu.make_async_copy(
                stage_ref.at[pl.ds(2 * (column ^ j), 2)], outs[j], out_sem.at[j]
            )
        )
        copies[-1].start()
    for copy in copies:
        copy.wait()


def normed(values):
    mean = jnp.mean(values, axis=-1, keepdims=True)
    centred = values - mean
    var = jnp.mean(centred * centred, axis=-1, keepdims=True)
    return centred * lax.rsqrt(var + EPS)


def decode_kernel(parts, cuts, me_ref, gains_ref, whead_ref, wkv, wq, wo, *refs):
    pieces, out_ref = refs[: parts * len(cuts)], refs[parts * len(cuts)]
    scratch = refs[parts * len(cuts) + 1 :]
    emb_ref, qin_ref, min_ref, q_ref, kv_ref, ctx_ref, sem = scratch
    tokv, width = emb_ref.shape[1:]
    rows = tokv // parts
    column = me_ref[1]
    copies = []
    for q, (first, size) in enumerate(cuts):
        for j in range(parts):
            i = q * parts + j
            start = pl.multiple_of((column ^ j) * rows + first, size)
            copies.append(
                pltpu.make_async_copy(pieces[i], emb_ref.at[:, pl.ds(start, size), :], sem.at[i])
            )
            copies[-1].start()
    for copy in copies:
        copy.wait()
    for side in range(2):
        xhat = normed(emb_ref[side].astype(jnp.float32))
        qin_ref[side] = (xhat * gains_ref[side, 0:1, :]).astype(jnp.bfloat16)
        min_ref[1 - side] = (xhat * gains_ref[1 - side, 1:2, :]).astype(jnp.bfloat16)
    for side in range(2):
        q_ref[side] = jnp.dot(
            qin_ref[side], wq[side], preferred_element_type=jnp.float32
        ).astype(jnp.bfloat16)
    for side in range(2):
        kv_ref[side] = jnp.dot(
            min_ref[side], wkv[side], preferred_element_type=jnp.float32
        ).astype(jnp.bfloat16)

    head_size = width // HEADS
    lanes = 2 * head_size
    low = lax.broadcasted_iota(jnp.int32, (tokv, lanes), 1) < head_size

    def split(values):
        zero = jnp.zeros_like(values)
        return jnp.concatenate([jnp.where(low, values, zero), jnp.where(low, zero, values)], axis=0)

    def soft(scores):
        top = jnp.max(scores, axis=-1, keepdims=True)
        e = jnp.exp2((scores - top) * (LOG2_E / head_size**0.5))
        return (e * (1.0 / jnp.sum(e, axis=-1, keepdims=True))).astype(jnp.bfloat16)

    def two_heads(i, carry):
        start = pl.multiple_of(i * lanes, lanes)
        for side in range(2):
            query = q_ref[side, :, pl.ds(start, lanes)]
            keys = split(kv_ref[side, :, pl.ds(start, lanes)])
            values = split(kv_ref[side, :, pl.ds(width + start, lanes)])
            scores = lax.dot_general(
                query, keys, (((1,), (1,)), ((), ())), preferred_element_type=jnp.float32
            )
            probs = jnp.concatenate([soft(scores[:, :tokv]), soft(scores[:, tokv:])], axis=1)
            ctx_ref[side, :, pl.ds(start, lanes)] = jnp.dot(
                probs, values, preferred_element_type=jnp.float32
            ).astype(jnp.bfloat16)
        return carry

    for i in range(HEADS // 2):
        two_heads(i, 0)
    for side in range(2):
        updated = emb_ref[side].astype(jnp.float32) + jnp.dot(
            ctx_ref[side], wo[side], preferred_element_type=jnp.float32
        )
        final = (normed(updated) * gains_ref[side, 2:3, :]).astype(jnp.bfloat16)
        head = lax.dot_general(
            whead_ref[side], final, (((1,), (1,)), ((), ())), preferred_element_type=jnp.float32
        )
        conf = 1.0 + jnp.exp(head[3:4, :])
        out_ref[side, 0:3, :] = head[0:3, :] * conf
        out_ref[side, 3:4, :] = conf


def load(*weights):
    return pl.pallas_call(
        load_kernel,
        out_shape=[jax.ShapeDtypeStruct(w.shape, w.dtype) for w in weights],
        in_specs=[HBM] * len(weights),
        out_specs=[VMEM] * len(weights),
        scratch_shapes=[pltpu.SemaphoreType.DMA((len(weights),))],
        compiler_params=pltpu.CompilerParams(vmem_limit_bytes=50 * 1024 * 1024),
        name="load",
    )(*weights)


def embed(parts, cuts, me, w_embed, pieces):
    views, rows, _ = pieces[0].shape
    full, width = w_embed.shape
    return pl.pallas_call(
        functools.partial(embed_kernel, parts, cuts),
        out_shape=[
            jax.ShapeDtypeStruct((views, size, width), jnp.bfloat16)
            for size in [size for _, size in cuts] + [rows]
        ],
        in_specs=[SMEM, VMEM] + [HBM] * parts,
        out_specs=[HBM] * (len(cuts) + 1),
        scratch_shapes=[
            pltpu.VMEM((views, rows, full), jnp.bfloat16),
            pltpu.VMEM((views, rows, width), jnp.bfloat16),
            pltpu.SemaphoreType.DMA((parts,)),
            pltpu.SemaphoreType.DMA((len(cuts) + 1,)),
        ],
        compiler_params=pltpu.CompilerParams(vmem_limit_bytes=16 * 1024 * 1024),
        cost_estimate=pl.CostEstimate(
            flops=2 * views * rows * full * width,
            bytes_accessed=2 * (full * width + 2 * views * rows * full),
            transcendentals=0,
        ),
        name="embed",
    )(me, w_embed, *pieces)


def pick(lanes, slots, cap, me, line, wants, own, below, above):
    views, size, width = own.shape
    reach = len(below)
    return pl.pallas_call(
        functools.partial(pick_kernel, lanes, reach, slots, cap),
        out_shape=[jax.ShapeDtypeStruct((len(slots), cap, size, width), jnp.bfloat16)] * lanes,
        in_specs=[SMEM, SMEM, SMEM] + [HBM] * (1 + 2 * reach),
        out_specs=[HBM] * lanes,
        scratch_shapes=[
            pltpu.VMEM((len(slots), views, size, width), jnp.bfloat16),
            pltpu.SemaphoreType.DMA((len(slots),)),
            pltpu.SemaphoreType.DMA((lanes * len(slots) * cap,)),
        ],
        compiler_params=pltpu.CompilerParams(vmem_limit_bytes=16 * 1024 * 1024),
        cost_estimate=pl.CostEstimate(
            flops=0,
            bytes_accessed=4 * lanes * len(slots) * cap * size * width,
            transcendentals=0,
        ),
        name="pick",
    )(me, line, wants, own, *below, *above)


def route(lanes, parts, cap, cuts, groups, me, line, sides, fetched):
    width = fetched[0].shape[-1]
    size = sum(size for _, size in cuts)
    base = cuts[0][0]
    cuts = tuple((first - base, each) for first, each in cuts)
    copies = len(cuts) * sum(len(group) for group in groups) * lanes * cap
    return pl.pallas_call(
        functools.partial(route_kernel, lanes, parts, cap, base, cuts, groups),
        out_shape=[jax.ShapeDtypeStruct((2, size, width), jnp.bfloat16)] * parts,
        in_specs=[SMEM, SMEM, SMEM] + [HBM] * len(fetched),
        out_specs=[HBM] * parts,
        scratch_shapes=[
            pltpu.VMEM((2 * parts, size, width), jnp.bfloat16),
            pltpu.SemaphoreType.DMA((copies,)),
            pltpu.SemaphoreType.DMA((parts,)),
        ],
        compiler_params=pltpu.CompilerParams(vmem_limit_bytes=16 * 1024 * 1024),
        cost_estimate=pl.CostEstimate(
            flops=0, bytes_accessed=8 * parts * size * width, transcendentals=0
        ),
        name="route",
    )(me, line, sides, *fetched)


def decode(parts, cuts, me, gains, w_head, w_query, w_keyval, w_out, pieces):
    width = pieces[0].shape[2]
    tokv = parts * sum(size for _, size in cuts)
    flops = 2 * 2 * tokv * width * (5 * width + 2 * tokv)
    return pl.pallas_call(
        functools.partial(decode_kernel, parts, cuts),
        out_shape=jax.ShapeDtypeStruct((2, 4, tokv), jnp.float32),
        in_specs=[SMEM, VMEM, VMEM, VMEM, VMEM, VMEM] + [HBM] * (parts * len(cuts)),
        out_specs=VMEM,
        scratch_shapes=[
            pltpu.VMEM((2, tokv, width), jnp.bfloat16),
            pltpu.VMEM((2, tokv, width), jnp.bfloat16),
            pltpu.VMEM((2, tokv, width), jnp.bfloat16),
            pltpu.VMEM((2, tokv, width), jnp.bfloat16),
            pltpu.VMEM((2, tokv, 2 * width), jnp.bfloat16),
            pltpu.VMEM((2, tokv, width), jnp.bfloat16),
            pltpu.SemaphoreType.DMA((parts * len(cuts),)),
        ],
        compiler_params=pltpu.CompilerParams(vmem_limit_bytes=40 * 1024 * 1024),
        cost_estimate=pl.CostEstimate(
            flops=flops, bytes_accessed=20 * width * width, transcendentals=2 * HEADS * tokv * tokv
        ),
        name="decode",
    )(me, gains, w_head, w_keyval, w_query, w_out, *pieces)


def on_device(tokens, pairs, w_embed, w_query, w_keyval, w_out, w_head, gains):
    count = lax.axis_size("view")
    parts = lax.axis_size("mp")
    row = lax.axis_index("view")
    column = lax.axis_index("mp")
    me = jnp.stack([row, column]).astype(jnp.int32)
    view_dev, tokv, _ = tokens.shape
    rows = tokv // parts
    block_pairs = pairs.shape[0]
    pair_dev = block_pairs // parts
    side_count = 2 * block_pairs
    cap = max(2, (side_count + count - 1) // count)
    slot_total = count * cap
    lanes = 1 << ((count.bit_length() - 1) // 2)
    length = count // lanes
    cuts = ((0, rows // 2), (rows // 2, rows // 2)) if rows % 32 == 0 else ((0, rows),)

    pieces = []
    for j in range(parts):
        piece = lax.dynamic_slice_in_dim(tokens, (column ^ j) * rows, rows, axis=1)
        pieces.append(lax.ppermute(piece, "mp", xor_pairs(parts, j)) if j else piece)

    pairs, pieces[1] = lax.optimization_barrier((pairs, pieces[1]))
    side_views = pairs.reshape(side_count)
    owners = side_views // view_dev
    local_ids = side_views % view_dev
    positions = jnp.arange(side_count, dtype=jnp.int32)
    same_owner = owners[:, None] == owners[None, :]
    slot_rank = jnp.sum(
        jnp.logical_and(same_owner, positions[None, :] < positions[:, None]), axis=1
    )
    slot_index = owners * cap + slot_rank
    slot_match = jnp.arange(slot_total, dtype=jnp.int32)[:, None] == slot_index[None, :]
    wanted = jnp.sum(jnp.where(slot_match, local_ids[None, :], 0), axis=1)
    used = jnp.any(slot_match, axis=1)
    slot_side = jnp.where(used, jnp.sum(jnp.where(slot_match, positions[None, :], 0), axis=1), -1)
    slot_side = slot_side.astype(jnp.int32)
    wanted = jnp.where(used, wanted, -1).astype(jnp.int32)
    wants = jnp.concatenate(
        [lax.ppermute(wanted, "view", xor_pairs(count, j)) if j else wanted for j in range(lanes)]
    )
    nearest = [sorted(range(length), key=lambda at: (abs(at - z), at)) for z in range(length)]
    line = jnp.asarray(nearest, jnp.int32)[row // lanes]

    weights = load(w_embed, w_query, w_keyval, w_out)
    pieces, weights = lax.optimization_barrier((pieces, weights))
    w_embed, w_query, w_keyval, w_out = weights
    *embedded, whole = embed(parts, cuts, me, w_embed, pieces)
    embedded, wants = lax.optimization_barrier((embedded, wants))
    groups = ((0,), tuple(range(1, length - 1)), (length - 1,))

    def swap(picked):
        return [
            lax.ppermute(picked[j], "view", xor_pairs(count, j)) if j else picked[j]
            for j in range(lanes)
        ]

    shared = pick(lanes, groups[0], cap, me, line, wants, whole, [], [])
    below, above = [[] for _ in cuts], [[] for _ in cuts]
    for p in range(1, length):
        up = [
            (z * lanes + y, (z + 1) * lanes + y) for z in range(p - 1, length - 1) for y in range(lanes)
        ]
        down = [
            (z * lanes + y, (z - 1) * lanes + y) for z in range(1, length - p + 1) for y in range(lanes)
        ]
        for q in range(len(cuts)):
            below[q].append(lax.ppermute((below[q] or [embedded[q]])[-1], "view", up))
            above[q].append(lax.ppermute((above[q] or [embedded[q]])[-1], "view", down))
        if p == 1:
            below[0], above[0], shared = lax.optimization_barrier((below[0], above[0], shared))
            shared = swap(shared)
        if p == 2:
            below[0], above[0], shared = lax.optimization_barrier((below[0], above[0], shared))
    fetched = []
    for q in range(len(cuts)):
        picked = [
            pick(
                lanes,
                group,
                cap,
                me,
                line,
                wants,
                embedded[q],
                below[q][: group[-1]],
                above[q][: group[-1]],
            )
            for group in groups[1:]
        ]
        fetched.append(list(shared))
        for group in picked:
            fetched[-1] += swap(group)
    slot_pair = slot_side // 2
    results, arrived = [], None
    for c in range(pair_dev):
        mine = jnp.logical_and(slot_side >= 0, slot_pair % pair_dev == c)
        place = jnp.where(mine, 2 * (slot_pair // pair_dev) + slot_side % 2, -1).astype(jnp.int32)
        steps = [(cut,) for cut in cuts] if c == 0 else [cuts]
        parcels = []
        for q, step in enumerate(steps):
            wave = fetched[q : q + 1] if c == 0 else fetched
            parcels += route(
                lanes, parts, cap, step, groups, me, line, place, [each for g in wave for each in g]
            )
        if c:
            parcels, arrived = lax.optimization_barrier((parcels, arrived))
        arrived = [
            lax.ppermute(parcel, "mp", xor_pairs(parts, i % parts)) if i % parts else parcel
            for i, parcel in enumerate(parcels)
        ]
        results.append(
            decode(
                parts,
                cuts if c == 0 else ((0, rows),),
                me,
                gains,
                w_head,
                w_query,
                w_keyval,
                w_out,
                arrived,
            )
        )
    results = jnp.stack(results)

    every = lax.all_gather(results, "mp", axis=0, tiled=True).reshape(side_count, 4 * tokv)
    slotted = jnp.dot(slot_match.astype(jnp.float32), every, precision=lax.Precision.HIGHEST)
    tags = jnp.broadcast_to(wanted.astype(jnp.float32)[:, None], (slot_total, 128))
    slotted = jnp.concatenate([slotted, tags], axis=1).reshape(count, cap, 4 * tokv + 128)
    returned = lax.all_to_all(slotted, "view", split_axis=0, concat_axis=0, tiled=True)
    picker = returned[:, :, 4 * tokv :][:, :, :1] == jnp.arange(view_dev, dtype=jnp.float32)
    summed = jnp.einsum(
        "rcv,rcx->vx",
        picker.astype(jnp.float32),
        returned[:, :, : 4 * tokv],
        precision=lax.Precision.HIGHEST,
    )
    return summed.reshape(view_dev, 4, tokv)


def solution(mesh):
    return jax.shard_map(
        on_device,
        mesh=mesh,
        in_specs=(P("view", None, "mp"), P("view", None), P(), P(), P(), P(), P(), P()),
        out_specs=P("view", None, None),
        check_vma=False,
    )
```

profile of v0, /device:TPU:0, one launch (start us, length us, event | category | flops | bytes accessed | tf_op | source)
XLA Modules:
  0.0 137.5 jit_solution(9764999843025872313)
XLA Ops:
  0.0 2.2 %constant_dynamic-slice_fusion.1 = (bf16[4,96,256]{2,1,0:T(8,128)(2,1)}, bf16[4,96,256]{2,1,0:T(8,128)(2,1)S(1)}, bf16[4,96,256]{2,1,0:T(8,128)(2,1)}, bf16[4,96,256]{2,1,0:T(8,128)(2,1)}) fusion(bf16[4,384,256]{2,1,0:T(8,128)(2,1)} %param.9, s32[]{:T(128)S(6)} %select_n.93, s32[]{:T(128)S(6)} %select_n.91, s32[]{:T(128)S(6)} %select_n.89, s32[]{:T(128)S(6)} %select_n.92), kind=kLoop, calls=%fused_computation.24 | loop fusion | bytes 1572880 | tf_op jit(solution)/shard_map/dynamic_slice | solution.py:360
  2.7 2.6 %collective-permute-start.2 = (bf16[4,96,256]{2,1,0:T(8,128)(2,1)}, bf16[4,96,256]{2,1,0:T(8,128)(2,1)}, u32[]{:S(2)}, u32[]{:S(2)}) collective-permute-start(bf16[4,96,256]{2,1,0:T(8,128)(2,1)} %get-tuple-element.125), channel_id=1, source_target_pairs={{0,3},{1,2},{2,1},{3,0},{4,7},{5,6},{6,5},{7,4},{8,11},{9,10},{10,... | collective-permute-start | bytes 589832 | tf_op jit(solution)/shard_map/ppermute | solution.py:361
  5.3 7.5 %load.1 = (bf16[1024,768]{1,0:T(8,128)(2,1)S(1)}, bf16[2,768,768]{2,1,0:T(8,128)(2,1)}, bf16[2,768,1536]{2,1,0:T(8,128)(2,1)}, bf16[2,768,768]{2,1,0:T(8,128)(2,1)}) custom-call(bf16[1024,768]{1,0:T(8,128)(2,1)S(1)} %copy-done, bf16[2,768,768]{2,1,0:T(8,128)(2,1)} %refs_1_.1, bf16[2,768,1536]{2,1,0:T(8,128)(2,1)} %refs_2_.1, bf16[2,768,768]{2,1,0:T(8,128)(2,1)} %refs_3_.1), custom_call_target="tpu_custom_call" | custom-call | tf_op jit(solution)/shard_map/load/pallas_call | solution.py:230
  13.5 2.1 %collective-permute-start.3 = (s32[16]{0:T(128)S(1)}, s32[16]{0:T(128)S(1)}, u32[]{:S(2)}, u32[]{:S(2)}) collective-permute-start(s32[16]{0:T(128)S(1)} %get-tuple-element.130), channel_id=1, source_target_pairs={{0,4},{4,0},{8,12},{12,8},{16,20},{20,16},{24,28},{28,24},{1,5},{5... | collective-permute-start | bytes 200 | tf_op jit(solution)/shard_map/ppermute | solution.py:380
  15.6 3.0 %embed.1 = (bf16[4,48,768]{2,1,0:T(8,128)(2,1)S(1)}, bf16[4,48,768]{2,1,0:T(8,128)(2,1)S(1)}, bf16[4,96,768]{2,1,0:T(8,128)(2,1)S(1)}) custom-call(s32[2]{0:T(128)S(1)} %pad_add_fusion.me_ref, bf16[1024,768]{1,0:T(8,128)(2,1)S(1)} %get-tuple-element.70.w_vmem, bf16[4,96,256]{2,1,0:T(8,128)(2,1)S(1)} %get-tuple-element.71.refs_0_, ...), custom_call_target="tpu_custom_call" | custom-call | flops 603979776 | bytes 3145728 | tf_op jit(solution)/shard_map/embed/pallas_call | solution.py:244
  20.0 4.6 %collective-permute-start.16 = (bf16[4,48,768]{2,1,0:T(8,128)(2,1)S(1)}, bf16[4,48,768]{2,1,0:T(8,128)(2,1)S(1)}, u32[]{:S(2)}, u32[]{:S(2)}) collective-permute-start(bf16[4,48,768]{2,1,0:T(8,128)(2,1)S(1)} %get-tuple-element.100.refs_0_), channel_id=1, source_target_pairs={{0,8},{4,12},{8,16},{12,20},{16,24},{20,28},{1,9},{5,13},{9,17},{1... | collective-permute-start | bytes 884744 | tf_op jit(solution)/shard_map/ppermute | solution.py:408
  24.6 1.3 collective-permute-start.5
  25.9 4.6 %collective-permute-start.4 = (bf16[4,48,768]{2,1,0:T(8,128)(2,1)S(1)}, bf16[4,48,768]{2,1,0:T(8,128)(2,1)S(1)}, u32[]{:S(2)}, u32[]{:S(2)}) collective-permute-start(bf16[4,48,768]{2,1,0:T(8,128)(2,1)S(1)} %get-tuple-element.77.refs_0_), channel_id=1, source_target_pairs={{0,8},{4,12},{8,16},{12,20},{16,24},{20,28},{1,9},{5,13},{9,17},{1... | collective-permute-start | bytes 884744 | tf_op jit(solution)/shard_map/ppermute | solution.py:408
  30.5 1.3 collective-permute-start.19
  33.2 1.5 %pick.5 = (bf16[1,2,96,768]{3,2,1,0:T(8,128)(2,1)S(1)}, bf16[1,2,96,768]{3,2,1,0:T(8,128)(2,1)S(1)}) custom-call(s32[2]{0:T(128)S(1)} %pad_add_fusion.me_ref, s32[4]{0:T(128)S(1)} %fusion.7.line_ref, s32[32]{0:T(128)S(1)} %pad_add_fusion.1.want_ref, bf16[4,96,768]{2,1,0:T(8,128)(2,1)S(1)} %get-tuple-element.79.refs_0_), custom_call_target="tpu_custom_call" | custom-call | bytes 1179648 | tf_op jit(solution)/shard_map/pick/pallas_call | solution.py:271
  34.7 1.7 %collective-permute-done.5.refs_3_.refs_4_ = bf16[4,48,768]{2,1,0:T(8,128)(2,1)S(1)} collective-permute-done((bf16[4,48,768]{2,1,0:T(8,128)(2,1)S(1)}, bf16[4,48,768]{2,1,0:T(8,128)(2,1)S(1)}, u32[]{:S(2)}, u32[]{:S(2)}) %collective-permute-start.5) | collective-permute-done | bytes 294944 | tf_op jit(solution)/shard_map/ppermute | solution.py:409
  38.4 1.3 collective-permute-start.7
  39.7 2.0 %collective-permute-done.19.refs_4_.refs_5_ = bf16[4,48,768]{2,1,0:T(8,128)(2,1)S(1)} collective-permute-done((bf16[4,48,768]{2,1,0:T(8,128)(2,1)S(1)}, bf16[4,48,768]{2,1,0:T(8,128)(2,1)S(1)}, u32[]{:S(2)}, u32[]{:S(2)}) %collective-permute-start.19) | collective-permute-done | bytes 294944 | tf_op jit(solution)/shard_map/ppermute | solution.py:409
  44.3 10.5 %collective-permute-done.7.refs_4_.refs_5_ = bf16[4,48,768]{2,1,0:T(8,128)(2,1)S(1)} collective-permute-done((bf16[4,48,768]{2,1,0:T(8,128)(2,1)S(1)}, bf16[4,48,768]{2,1,0:T(8,128)(2,1)S(1)}, u32[]{:S(2)}, u32[]{:S(2)}) %collective-permute-start.7) | collective-permute-done | bytes 294944 | tf_op jit(solution)/shard_map/ppermute | solution.py:409
  55.5 1.3 collective-permute-start.11
  56.8 1.7 %pick.8 = (bf16[2,2,48,768]{3,2,1,0:T(8,128)(2,1)S(1)}, bf16[2,2,48,768]{3,2,1,0:T(8,128)(2,1)S(1)}) custom-call(s32[2]{0:T(128)S(1)} %pad_add_fusion.me_ref, s32[4]{0:T(128)S(1)} %fusion.7.line_ref, s32[32]{0:T(128)S(1)} %pad_add_fusion.1.want_ref, bf16[4,48,768]{2,1,0:T(8,128)(2,1)S(1)} %get-tuple-element.100.refs_0_, ...), custom_call_target="tpu_custom_call" | custom-call | bytes 1179648 | tf_op jit(solution)/shard_map/pick/pallas_call | solution.py:271
  59.3 1.7 %pick.6 = (bf16[2,2,48,768]{3,2,1,0:T(8,128)(2,1)S(1)}, bf16[2,2,48,768]{3,2,1,0:T(8,128)(2,1)S(1)}) custom-call(s32[2]{0:T(128)S(1)} %pad_add_fusion.me_ref, s32[4]{0:T(128)S(1)} %fusion.7.line_ref, s32[32]{0:T(128)S(1)} %pad_add_fusion.1.want_ref, bf16[4,48,768]{2,1,0:T(8,128)(2,1)S(1)} %get-tuple-element.77.refs_0_, ...), custom_call_target="tpu_custom_call" | custom-call | bytes 1179648 | tf_op jit(solution)/shard_map/pick/pallas_call | solution.py:271
  61.0 1.3 collective-permute-start.9
  65.5 1.3 collective-permute-start.12
  66.8 4.7 %collective-permute-done.23.refs_5_.refs_11_ = bf16[1,2,48,768]{3,2,1,0:T(8,128)(2,1)S(1)} collective-permute-done((bf16[1,2,48,768]{3,2,1,0:T(8,128)(2,1)S(1)}, bf16[1,2,48,768]{3,2,1,0:T(8,128)(2,1)S(1)}, u32[]{:S(2)}, u32[]{:S(2)}) %collective-permute-start.23) | collective-permute-done | bytes 147488 | tf_op jit(solution)/shard_map/ppermute | solution.py:394
  71.6 2.6 %route.4 = (bf16[2,48,768]{2,1,0:T(8,128)(2,1)S(1)}, bf16[2,48,768]{2,1,0:T(8,128)(2,1)S(1)}, bf16[2,48,768]{2,1,0:T(8,128)(2,1)S(1)}, bf16[2,48,768]{2,1,0:T(8,128)(2,1)S(1)}) custom-call(s32[2]{0:T(128)S(1)} %pad_add_fusion.me_ref, s32[4]{0:T(128)S(1)} %fusion.7.line_ref, s32[16]{0:T(128)S(1)} %get-tuple-element.119.side_ref, ...), custom_call_target="tpu_custom_call" | custom-call | bytes 1179648 | tf_op jit(solution)/shard_map/route/pallas_call | solution.py:297
  74.3 1.6 %collective-permute-start.25 = (bf16[2,48,768]{2,1,0:T(8,128)(2,1)S(1)}, bf16[2,48,768]{2,1,0:T(8,128)(2,1)S(1)}, u32[]{:S(2)}, u32[]{:S(2)}) collective-permute-start(bf16[2,48,768]{2,1,0:T(8,128)(2,1)S(1)} %get-tuple-element.107), channel_id=1, source_target_pairs={{0,2},{1,3},{2,0},{3,1},{4,6},{5,7},{6,4},{7,5},{8,10},{9,11},{10,... | collective-permute-start | bytes 442376 | tf_op jit(solution)/shard_map/ppermute | solution.py:449
  76.2 2.6 %route.3 = (bf16[2,48,768]{2,1,0:T(8,128)(2,1)S(1)}, bf16[2,48,768]{2,1,0:T(8,128)(2,1)S(1)}, bf16[2,48,768]{2,1,0:T(8,128)(2,1)S(1)}, bf16[2,48,768]{2,1,0:T(8,128)(2,1)S(1)}) custom-call(s32[2]{0:T(128)S(1)} %pad_add_fusion.me_ref, s32[4]{0:T(128)S(1)} %fusion.7.line_ref, s32[16]{0:T(128)S(1)} %get-tuple-element.119.side_ref, ...), custom_call_target="tpu_custom_call" | custom-call | bytes 1179648 | tf_op jit(solution)/shard_map/route/pallas_call | solution.py:297
  79.2 1.5 %collective-permute-start.14 = (bf16[2,48,768]{2,1,0:T(8,128)(2,1)S(1)}, bf16[2,48,768]{2,1,0:T(8,128)(2,1)S(1)}, u32[]{:S(2)}, u32[]{:S(2)}) collective-permute-start(bf16[2,48,768]{2,1,0:T(8,128)(2,1)S(1)} %get-tuple-element.98), channel_id=1, source_target_pairs={{0,2},{1,3},{2,0},{3,1},{4,6},{5,7},{6,4},{7,5},{8,10},{9,11},{10,... | collective-permute-start | bytes 442376 | tf_op jit(solution)/shard_map/ppermute | solution.py:449
  80.8 3.5 %route.5 = (bf16[2,96,768]{2,1,0:T(8,128)(2,1)S(1)}, bf16[2,96,768]{2,1,0:T(8,128)(2,1)S(1)}, bf16[2,96,768]{2,1,0:T(8,128)(2,1)S(1)}, bf16[2,96,768]{2,1,0:T(8,128)(2,1)S(1)}) custom-call(s32[2]{0:T(128)S(1)} %pad_add_fusion.me_ref, s32[4]{0:T(128)S(1)} %fusion.7.line_ref, s32[16]{0:T(128)S(1)} %and_select_fusion.side_ref, ...), custom_call_target="tpu_custom_call" | custom-call | bytes 2359296 | tf_op jit(solution)/shard_map/route/pallas_call | solution.py:297
  84.4 3.1 %collective-permute-done.14.refs_2_ = bf16[2,48,768]{2,1,0:T(8,128)(2,1)S(1)} collective-permute-done((bf16[2,48,768]{2,1,0:T(8,128)(2,1)S(1)}, bf16[2,48,768]{2,1,0:T(8,128)(2,1)S(1)}, u32[]{:S(2)}, u32[]{:S(2)}) %collective-permute-start.14) | collective-permute-done | bytes 147488 | tf_op jit(solution)/shard_map/ppermute | solution.py:449
  87.4 2.2 %collective-permute-done.15.refs_3_ = bf16[2,48,768]{2,1,0:T(8,128)(2,1)S(1)} collective-permute-done((bf16[2,48,768]{2,1,0:T(8,128)(2,1)S(1)}, bf16[2,48,768]{2,1,0:T(8,128)(2,1)S(1)}, u32[]{:S(2)}, u32[]{:S(2)}) %collective-permute-start.15) | collective-permute-done | bytes 147488 | tf_op jit(solution)/shard_map/ppermute | solution.py:449
  89.9 1.5 %collective-permute-start.28 = (bf16[2,96,768]{2,1,0:T(8,128)(2,1)S(1)}, bf16[2,96,768]{2,1,0:T(8,128)(2,1)S(1)}, u32[]{:S(2)}, u32[]{:S(2)}) collective-permute-start(bf16[2,96,768]{2,1,0:T(8,128)(2,1)S(1)} %get-tuple-element.115), channel_id=1, source_target_pairs={{0,2},{1,3},{2,0},{3,1},{4,6},{5,7},{6,4},{7,5},{8,10},{9,11},{10,... | collective-permute-start | bytes 884744 | tf_op jit(solution)/shard_map/ppermute | solution.py:449
  91.5 12.4 %decode.2 = f32[2,4,384]{2,1,0:T(4,128)S(1)} custom-call(s32[2]{0:T(128)S(1)} %pad_add_fusion.me_ref, f32[2,3,768]{2,1,0:T(4,128)S(1)} %copy.24.gains_ref, bf16[2,4,768]{2,1,0:T(4,128)(2,1)S(1)} %copy-done.3, bf16[2,768,1536]{2,1,0:T(8,128)(2,1)S(1)} %bitcast.16, bf16[2,768,768]{2,1,0:T(8,128)(2,1)S(1)} %copy-done.1, bf16[2,768,768]{2,1,0:T(8,128)(2,1)S(1)} %copy-done.2, ...), custom_call_target="tpu_custom_call" | custom-call | flops 5435817984 | bytes 11796480 | tf_op jit(solution)/shard_map/decode/pallas_call | solution.py:319
  104.6 11.9 %decode.3 = f32[2,4,384]{2,1,0:T(4,128)S(1)} custom-call(s32[2]{0:T(128)S(1)} %pad_add_fusion.me_ref, f32[2,3,768]{2,1,0:T(4,128)S(1)} %copy.24.gains_ref, bf16[2,4,768]{2,1,0:T(4,128)(2,1)S(1)} %copy-done.3, bf16[2,768,1536]{2,1,0:T(8,128)(2,1)S(1)} %bitcast.16, bf16[2,768,768]{2,1,0:T(8,128)(2,1)S(1)} %copy-done.1, bf16[2,768,768]{2,1,0:T(8,128)(2,1)S(1)} %copy-done.2, ...), custom_call_target="tpu_custom_call" | custom-call | flops 5435817984 | bytes 11796480 | tf_op jit(solution)/shard_map/decode/pallas_call | solution.py:319
  116.5 5.4 %all_gather.3 = f32[8,2,4,384]{3,2,1,0:T(4,128)S(1)} all-gather(f32[2,2,4,384]{3,2,1,0:T(4,128)S(1)} %pad_maximum_fusion.1), channel_id=1, replica_groups=mesh['view'=8,'mp'=4] {'mp'}, dimensions={0}, use_global_device_ids=true | all-gather | bytes 122880 | tf_op jit(solution)/shard_map/all_gather | solution.py:467
  122.2 14.4 %all_to_all.5 = f32[8,2,1664]{2,1,0:T(2,128)S(1)} all-to-all(f32[8,2,1664]{2,1,0:T(2,128)S(1)} %reshape.110), channel_id=1, replica_groups=mesh['view'=8,'mp'=4] {'view'}, dimensions={0} | all-to-all | bytes 212992 | tf_op jit(solution)/shard_map/all_to_all | solution.py:471
  (84 shorter events, 16.5 us)
Async XLA Ops:
  2.2 10.7 %collective-permute-start = (bf16[4,96,256]{2,1,0:T(8,128)(2,1)}, bf16[4,96,256]{2,1,0:T(8,128)(2,1)S(1)}, u32[]{:S(2)}, u32[]{:S(2)}) collective-permute-start(bf16[4,96,256]{2,1,0:T(8,128)(2,1)} %get-tuple-element.127), channel_id=1, source_target_pairs={{0,1},{1,0},{2,3},{3,2},{4,5},{5,4},{6,7},{7,6},{8,9},{9,8},{10,11... | collective-permute-start | bytes 589832 | tf_op jit(solution)/shard_map/ppermute | solution.py:361
  2.7 13.0 %collective-permute-start.2 = (bf16[4,96,256]{2,1,0:T(8,128)(2,1)}, bf16[4,96,256]{2,1,0:T(8,128)(2,1)}, u32[]{:S(2)}, u32[]{:S(2)}) collective-permute-start(bf16[4,96,256]{2,1,0:T(8,128)(2,1)} %get-tuple-element.125), channel_id=1, source_target_pairs={{0,3},{1,2},{2,1},{3,0},{4,7},{5,6},{6,5},{7,4},{8,11},{9,10},{10,... | collective-permute-start | bytes 589832 | tf_op jit(solution)/shard_map/ppermute | solution.py:361
  5.2 10.4 %collective-permute-start.1 = (bf16[4,96,256]{2,1,0:T(8,128)(2,1)}, bf16[4,96,256]{2,1,0:T(8,128)(2,1)}, u32[]{:S(2)}, u32[]{:S(2)}) collective-permute-start(bf16[4,96,256]{2,1,0:T(8,128)(2,1)} %get-tuple-element.128), channel_id=1, source_target_pairs={{0,2},{1,3},{2,0},{3,1},{4,6},{5,7},{6,4},{7,5},{8,10},{9,11},{10,... | collective-permute-start | bytes 589832 | tf_op jit(solution)/shard_map/ppermute | solution.py:361
  13.5 5.1 %collective-permute-start.3 = (s32[16]{0:T(128)S(1)}, s32[16]{0:T(128)S(1)}, u32[]{:S(2)}, u32[]{:S(2)}) collective-permute-start(s32[16]{0:T(128)S(1)} %get-tuple-element.130), channel_id=1, source_target_pairs={{0,4},{4,0},{8,12},{12,8},{16,20},{20,16},{24,28},{28,24},{1,5},{5... | collective-permute-start | bytes 200 | tf_op jit(solution)/shard_map/ppermute | solution.py:380
  18.7 11.7 %collective-permute-start.18 = (bf16[4,48,768]{2,1,0:T(8,128)(2,1)S(1)}, bf16[4,48,768]{2,1,0:T(8,128)(2,1)S(1)}, u32[]{:S(2)}, u32[]{:S(2)}) collective-permute-start(bf16[4,48,768]{2,1,0:T(8,128)(2,1)S(1)} %get-tuple-element.100.refs_0_), channel_id=1, source_target_pairs={{8,0},{12,4},{16,8},{20,12},{24,16},{28,20},{9,1},{13,5},{17,9},{2... | collective-permute-start | bytes 884744 | tf_op jit(solution)/shard_map/ppermute | solution.py:409
  20.0 11.8 %collective-permute-start.16 = (bf16[4,48,768]{2,1,0:T(8,128)(2,1)S(1)}, bf16[4,48,768]{2,1,0:T(8,128)(2,1)S(1)}, u32[]{:S(2)}, u32[]{:S(2)}) collective-permute-start(bf16[4,48,768]{2,1,0:T(8,128)(2,1)S(1)} %get-tuple-element.100.refs_0_), channel_id=1, source_target_pairs={{0,8},{4,12},{8,16},{12,20},{16,24},{20,28},{1,9},{5,13},{9,17},{1... | collective-permute-start | bytes 884744 | tf_op jit(solution)/shard_map/ppermute | solution.py:408
  24.6 11.8 %collective-permute-start.5 = (bf16[4,48,768]{2,1,0:T(8,128)(2,1)S(1)}, bf16[4,48,768]{2,1,0:T(8,128)(2,1)S(1)}, u32[]{:S(2)}, u32[]{:S(2)}) collective-permute-start(bf16[4,48,768]{2,1,0:T(8,128)(2,1)S(1)} %get-tuple-element.77.refs_0_), channel_id=1, source_target_pairs={{8,0},{12,4},{16,8},{20,12},{24,16},{28,20},{9,1},{13,5},{17,9},{2... | collective-permute-start | bytes 884744 | tf_op jit(solution)/shard_map/ppermute | solution.py:409
  25.9 10.7 %collective-permute-start.4 = (bf16[4,48,768]{2,1,0:T(8,128)(2,1)S(1)}, bf16[4,48,768]{2,1,0:T(8,128)(2,1)S(1)}, u32[]{:S(2)}, u32[]{:S(2)}) collective-permute-start(bf16[4,48,768]{2,1,0:T(8,128)(2,1)S(1)} %get-tuple-element.77.refs_0_), channel_id=1, source_target_pairs={{0,8},{4,12},{8,16},{12,20},{16,24},{20,28},{1,9},{5,13},{9,17},{1... | collective-permute-start | bytes 884744 | tf_op jit(solution)/shard_map/ppermute | solution.py:408
  30.5 11.2 %collective-permute-start.19 = (bf16[4,48,768]{2,1,0:T(8,128)(2,1)S(1)}, bf16[4,48,768]{2,1,0:T(8,128)(2,1)S(1)}, u32[]{:S(2)}, u32[]{:S(2)}) collective-permute-start(bf16[4,48,768]{2,1,0:T(8,128)(2,1)S(1)} %collective-permute-done.18.refs_3_.refs_4_), channel_id=1, source_target_pairs={{8,0},{12,4},{16,8},{20,12},{9,1},{13,5},{17,9},{21,13},{10,2},{14... | collective-permute-start | bytes 884744 | tf_op jit(solution)/shard_map/ppermute | solution.py:409
  31.8 11.2 %collective-permute-start.17 = (bf16[4,48,768]{2,1,0:T(8,128)(2,1)S(1)}, bf16[4,48,768]{2,1,0:T(8,128)(2,1)S(1)}, u32[]{:S(2)}, u32[]{:S(2)}) collective-permute-start(bf16[4,48,768]{2,1,0:T(8,128)(2,1)S(1)} %collective-permute-done.16.refs_1_), channel_id=1, source_target_pairs={{8,16},{12,20},{16,24},{20,28},{9,17},{13,21},{17,25},{21,29},{10,... | collective-permute-start | bytes 884744 | tf_op jit(solution)/shard_map/ppermute | solution.py:408
  36.6 7.8 %collective-permute-start.8 = (bf16[1,2,96,768]{3,2,1,0:T(8,128)(2,1)S(1)}, bf16[1,2,96,768]{3,2,1,0:T(8,128)(2,1)S(1)}, u32[]{:S(2)}, u32[]{:S(2)}) collective-permute-start(bf16[1,2,96,768]{3,2,1,0:T(8,128)(2,1)S(1)} %get-tuple-element.85), channel_id=1, source_target_pairs={{0,4},{4,0},{8,12},{12,8},{16,20},{20,16},{24,28},{28,24},{1,5},{5... | collective-permute-start | bytes 884744 | tf_op jit(solution)/shard_map/ppermute | solution.py:394
  37.7 6.6 %collective-permute-start.6 = (bf16[4,48,768]{2,1,0:T(8,128)(2,1)S(1)}, bf16[4,48,768]{2,1,0:T(8,128)(2,1)S(1)}, u32[]{:S(2)}, u32[]{:S(2)}) collective-permute-start(bf16[4,48,768]{2,1,0:T(8,128)(2,1)S(1)} %collective-permute-done.4.refs_1_), channel_id=1, source_target_pairs={{8,16},{12,20},{16,24},{20,28},{9,17},{13,21},{17,25},{21,29},{10,... | collective-permute-start | bytes 884744 | tf_op jit(solution)/shard_map/ppermute | solution.py:408
  38.4 16.4 %collective-permute-start.7 = (bf16[4,48,768]{2,1,0:T(8,128)(2,1)S(1)}, bf16[4,48,768]{2,1,0:T(8,128)(2,1)S(1)}, u32[]{:S(2)}, u32[]{:S(2)}) collective-permute-start(bf16[4,48,768]{2,1,0:T(8,128)(2,1)S(1)} %collective-permute-done.5.refs_3_.refs_4_), channel_id=1, source_target_pairs={{8,0},{12,4},{16,8},{20,12},{9,1},{13,5},{17,9},{21,13},{10,2},{14... | collective-permute-start | bytes 884744 | tf_op jit(solution)/shard_map/ppermute | solution.py:409
  41.7 19.3 %collective-permute-start.22 = (bf16[4,48,768]{2,1,0:T(8,128)(2,1)S(1)}, bf16[4,48,768]{2,1,0:T(8,128)(2,1)S(1)}, u32[]{:S(2)}, u32[]{:S(2)}) collective-permute-start(bf16[4,48,768]{2,1,0:T(8,128)(2,1)S(1)} %collective-permute-done.19.refs_4_.refs_5_), channel_id=1, source_target_pairs={{8,0},{12,4},{9,1},{13,5},{10,2},{14,6},{11,3},{15,7}} | collective-permute-start | bytes 884744 | tf_op jit(solution)/shard_map/ppermute | solution.py:409
  43.0 19.3 %collective-permute-start.21 = (bf16[4,48,768]{2,1,0:T(8,128)(2,1)S(1)}, bf16[4,48,768]{2,1,0:T(8,128)(2,1)S(1)}, u32[]{:S(2)}, u32[]{:S(2)}) collective-permute-start(bf16[4,48,768]{2,1,0:T(8,128)(2,1)S(1)} %collective-permute-done.17.refs_2_), channel_id=1, source_target_pairs={{16,24},{20,28},{17,25},{21,29},{18,26},{22,30},{19,27},{23,31}} | collective-permute-start | bytes 884744 | tf_op jit(solution)/shard_map/ppermute | solution.py:408
  54.8 9.5 %collective-permute-start.10 = (bf16[4,48,768]{2,1,0:T(8,128)(2,1)S(1)}, bf16[4,48,768]{2,1,0:T(8,128)(2,1)S(1)}, u32[]{:S(2)}, u32[]{:S(2)}) collective-permute-start(bf16[4,48,768]{2,1,0:T(8,128)(2,1)S(1)} %collective-permute-done.6.refs_2_), channel_id=1, source_target_pairs={{16,24},{20,28},{17,25},{21,29},{18,26},{22,30},{19,27},{23,31}} | collective-permute-start | bytes 884744 | tf_op jit(solution)/shard_map/ppermute | solution.py:408
  55.5 8.8 %collective-permute-start.11 = (bf16[4,48,768]{2,1,0:T(8,128)(2,1)S(1)}, bf16[4,48,768]{2,1,0:T(8,128)(2,1)S(1)}, u32[]{:S(2)}, u32[]{:S(2)}) collective-permute-start(bf16[4,48,768]{2,1,0:T(8,128)(2,1)S(1)} %collective-permute-done.7.refs_4_.refs_5_), channel_id=1, source_target_pairs={{8,0},{12,4},{9,1},{13,5},{10,2},{14,6},{11,3},{15,7}} | collective-permute-start | bytes 884744 | tf_op jit(solution)/shard_map/ppermute | solution.py:409
  56.8 34.7 %slice-start = ((s8[4718592]{0:T(1024)(128)(4,1)}), s8[4194304]{0:T(1024)(128)(4,1)S(1)}, s32[]{:S(2)}) async-start(s8[4718592]{0:T(1024)(128)(4,1)} %bitcast.15), calls=%async_computation.1 | async-start | bytes 8388608
  58.5 8.4 %collective-permute-start.20 = (bf16[2,2,48,768]{3,2,1,0:T(8,128)(2,1)S(1)}, bf16[2,2,48,768]{3,2,1,0:T(8,128)(2,1)S(1)}, u32[]{:S(2)}, u32[]{:S(2)}) collective-permute-start(bf16[2,2,48,768]{3,2,1,0:T(8,128)(2,1)S(1)} %get-tuple-element.102), channel_id=1, source_target_pairs={{0,4},{4,0},{8,12},{12,8},{16,20},{20,16},{24,28},{28,24},{1,5},{5... | collective-permute-start | bytes 884744 | tf_op jit(solution)/shard_map/ppermute | solution.py:394
  61.0 15.2 %collective-permute-start.9 = (bf16[2,2,48,768]{3,2,1,0:T(8,128)(2,1)S(1)}, bf16[2,2,48,768]{3,2,1,0:T(8,128)(2,1)S(1)}, u32[]{:S(2)}, u32[]{:S(2)}) collective-permute-start(bf16[2,2,48,768]{3,2,1,0:T(8,128)(2,1)S(1)} %get-tuple-element.93), channel_id=1, source_target_pairs={{0,4},{4,0},{8,12},{12,8},{16,20},{20,16},{24,28},{28,24},{1,5},{5... | collective-permute-start | bytes 884744 | tf_op jit(solution)/shard_map/ppermute | solution.py:394
  63.5 28.0 %slice-start.1 = ((s8[4718592]{0:T(1024)(128)(4,1)}), s8[524288]{0:T(1024)(128)(4,1)S(1)}, s32[]{:S(2)}) async-start(s8[4718592]{0:T(1024)(128)(4,1)} %bitcast.15), calls=%async_computation.2 | async-start | bytes 1048576
  63.5 8.1 %collective-permute-start.23 = (bf16[1,2,48,768]{3,2,1,0:T(8,128)(2,1)S(1)}, bf16[1,2,48,768]{3,2,1,0:T(8,128)(2,1)S(1)}, u32[]{:S(2)}, u32[]{:S(2)}) collective-permute-start(bf16[1,2,48,768]{3,2,1,0:T(8,128)(2,1)S(1)} %get-tuple-element.104), channel_id=1, source_target_pairs={{0,4},{4,0},{8,12},{12,8},{16,20},{20,16},{24,28},{28,24},{1,5},{5... | collective-permute-start | bytes 442376 | tf_op jit(solution)/shard_map/ppermute | solution.py:394
  65.5 10.8 %collective-permute-start.12 = (bf16[1,2,48,768]{3,2,1,0:T(8,128)(2,1)S(1)}, bf16[1,2,48,768]{3,2,1,0:T(8,128)(2,1)S(1)}, u32[]{:S(2)}, u32[]{:S(2)}) collective-permute-start(bf16[1,2,48,768]{3,2,1,0:T(8,128)(2,1)S(1)} %get-tuple-element.95), channel_id=1, source_target_pairs={{0,4},{4,0},{8,12},{12,8},{16,20},{20,16},{24,28},{28,24},{1,5},{5... | collective-permute-start | bytes 442376 | tf_op jit(solution)/shard_map/ppermute | solution.py:394
  74.2 6.5 %collective-permute-start.24 = (bf16[2,48,768]{2,1,0:T(8,128)(2,1)S(1)}, bf16[2,48,768]{2,1,0:T(8,128)(2,1)S(1)}, u32[]{:S(2)}, u32[]{:S(2)}) collective-permute-start(bf16[2,48,768]{2,1,0:T(8,128)(2,1)S(1)} %get-tuple-element.106), channel_id=1, source_target_pairs={{0,1},{1,0},{2,3},{3,2},{4,5},{5,4},{6,7},{7,6},{8,9},{9,8},{10,11... | collective-permute-start | bytes 442376 | tf_op jit(solution)/shard_map/ppermute | solution.py:449
  74.3 10.0 %collective-permute-start.25 = (bf16[2,48,768]{2,1,0:T(8,128)(2,1)S(1)}, bf16[2,48,768]{2,1,0:T(8,128)(2,1)S(1)}, u32[]{:S(2)}, u32[]{:S(2)}) collective-permute-start(bf16[2,48,768]{2,1,0:T(8,128)(2,1)S(1)} %get-tuple-element.107), channel_id=1, source_target_pairs={{0,2},{1,3},{2,0},{3,1},{4,6},{5,7},{6,4},{7,5},{8,10},{9,11},{10,... | collective-permute-start | bytes 442376 | tf_op jit(solution)/shard_map/ppermute | solution.py:449
  75.9 8.5 %collective-permute-start.26 = (bf16[2,48,768]{2,1,0:T(8,128)(2,1)S(1)}, bf16[2,48,768]{2,1,0:T(8,128)(2,1)S(1)}, u32[]{:S(2)}, u32[]{:S(2)}) collective-permute-start(bf16[2,48,768]{2,1,0:T(8,128)(2,1)S(1)} %get-tuple-element.108), channel_id=1, source_target_pairs={{0,3},{1,2},{2,1},{3,0},{4,7},{5,6},{6,5},{7,4},{8,11},{9,10},{10,... | collective-permute-start | bytes 442376 | tf_op jit(solution)/shard_map/ppermute | solution.py:449
  78.8 5.5 %collective-permute-start.13 = (bf16[2,48,768]{2,1,0:T(8,128)(2,1)S(1)}, bf16[2,48,768]{2,1,0:T(8,128)(2,1)S(1)}, u32[]{:S(2)}, u32[]{:S(2)}) collective-permute-start(bf16[2,48,768]{2,1,0:T(8,128)(2,1)S(1)} %get-tuple-element.97), channel_id=1, source_target_pairs={{0,1},{1,0},{2,3},{3,2},{4,5},{5,4},{6,7},{7,6},{8,9},{9,8},{10,11... | collective-permute-start | bytes 442376 | tf_op jit(solution)/shard_map/ppermute | solution.py:449
  79.2 8.2 %collective-permute-start.14 = (bf16[2,48,768]{2,1,0:T(8,128)(2,1)S(1)}, bf16[2,48,768]{2,1,0:T(8,128)(2,1)S(1)}, u32[]{:S(2)}, u32[]{:S(2)}) collective-permute-start(bf16[2,48,768]{2,1,0:T(8,128)(2,1)S(1)} %get-tuple-element.98), channel_id=1, source_target_pairs={{0,2},{1,3},{2,0},{3,1},{4,6},{5,7},{6,4},{7,5},{8,10},{9,11},{10,... | collective-permute-start | bytes 442376 | tf_op jit(solution)/shard_map/ppermute | solution.py:449
  80.7 8.9 %collective-permute-start.15 = (bf16[2,48,768]{2,1,0:T(8,128)(2,1)S(1)}, bf16[2,48,768]{2,1,0:T(8,128)(2,1)S(1)}, u32[]{:S(2)}, u32[]{:S(2)}) collective-permute-start(bf16[2,48,768]{2,1,0:T(8,128)(2,1)S(1)} %get-tuple-element.99), channel_id=1, source_target_pairs={{0,3},{1,2},{2,1},{3,0},{4,7},{5,6},{6,5},{7,4},{8,11},{9,10},{10,... | collective-permute-start | bytes 442376 | tf_op jit(solution)/shard_map/ppermute | solution.py:449
  89.6 14.3 %collective-permute-start.27 = (bf16[2,96,768]{2,1,0:T(8,128)(2,1)S(1)}, bf16[2,96,768]{2,1,0:T(8,128)(2,1)S(1)}, u32[]{:S(2)}, u32[]{:S(2)}) collective-permute-start(bf16[2,96,768]{2,1,0:T(8,128)(2,1)S(1)} %get-tuple-element.114), channel_id=1, source_target_pairs={{0,1},{1,0},{2,3},{3,2},{4,5},{5,4},{6,7},{7,6},{8,9},{9,8},{10,11... | collective-permute-start | bytes 884744 | tf_op jit(solution)/shard_map/ppermute | solution.py:449
  89.9 14.0 %collective-permute-start.28 = (bf16[2,96,768]{2,1,0:T(8,128)(2,1)S(1)}, bf16[2,96,768]{2,1,0:T(8,128)(2,1)S(1)}, u32[]{:S(2)}, u32[]{:S(2)}) collective-permute-start(bf16[2,96,768]{2,1,0:T(8,128)(2,1)S(1)} %get-tuple-element.115), channel_id=1, source_target_pairs={{0,2},{1,3},{2,0},{3,1},{4,6},{5,7},{6,4},{7,5},{8,10},{9,11},{10,... | collective-permute-start | bytes 884744 | tf_op jit(solution)/shard_map/ppermute | solution.py:449
  91.4 13.2 %collective-permute-start.29 = (bf16[2,96,768]{2,1,0:T(8,128)(2,1)S(1)}, bf16[2,96,768]{2,1,0:T(8,128)(2,1)S(1)}, u32[]{:S(2)}, u32[]{:S(2)}) collective-permute-start(bf16[2,96,768]{2,1,0:T(8,128)(2,1)S(1)} %get-tuple-element.116), channel_id=1, source_target_pairs={{0,3},{1,2},{2,1},{3,0},{4,7},{5,6},{6,5},{7,4},{8,11},{9,10},{10,... | collective-permute-start | bytes 884744 | tf_op jit(solution)/shard_map/ppermute | solution.py:449
  (6 other events, 80.7 us)
where the time goes:
time: 138 us
  Pallas kernels  50.7 us (37%)
  starting transfers between devices  36 us (26%)
  waiting for transfers between devices  25.8 us (19%)
  blocking collectives  19.7 us (14%)
  local copies, waits for them, and re-layouts  3.94 us (3%)
    pallas_call x2, Pallas kernels, decode(): pl.pallas_call(functools.partial(decode_kernel, parts, cuts), out_shape=j...  24.3 us
    all_to_all x1, blocking collectives, on_device(): lax.all_to_all(slotted, 'view', split_axis=0, concat_axis=0, tiled=True)  14.4 us
    ppermute x6, waiting for transfers between devices, on_device(): above[q].append(lax.ppermute((above[q] or [embedded[q]])[-1], 'view', down))  14.2 us
    ppermute x6, starting transfers between devices, on_device(): below[q].append(lax.ppermute((below[q] or [embedded[q]])[-1], 'view', up))  11.8 us
    pallas_call x3, Pallas kernels, route(): pl.pallas_call(functools.partial(route_kernel, lanes, parts, cap, base, c...  8.75 us
    ppermute x6, starting transfers between devices, on_device(): above[q].append(lax.ppermute((above[q] or [embedded[q]])[-1], 'view', down))  7.73 us
    pallas_call x1, Pallas kernels, load(): pl.pallas_call(load_kernel, out_shape=[jax.ShapeDtypeStruct(w.shape, w.dt...  7.5 us
    pallas_call x5, Pallas kernels, pick(): pl.pallas_call(functools.partial(pick_kernel, lanes, reach, slots, cap),...  7.15 us
  transfers between devices with their start and end apart: 30, of which 9 were waited for; matrix products, arithmetic and copies ran while one was open for 1% of the time, Pallas kernels for 28%

commit v1 on v0

--- a/solution.py
+++ b/solution.py
@@ -170,17 +170,20 @@
             copies[-1].start()
     for copy in copies:
         copy.wait()
-    for side in range(2):
+
+    def normalise(side):
         xhat = normed(emb_ref[side].astype(jnp.float32))
         qin_ref[side] = (xhat * gains_ref[side, 0:1, :]).astype(jnp.bfloat16)
         min_ref[1 - side] = (xhat * gains_ref[1 - side, 1:2, :]).astype(jnp.bfloat16)
-    for side in range(2):
-        q_ref[side] = jnp.dot(
-            qin_ref[side], wq[side], preferred_element_type=jnp.float32
+
+    def project_query(side, start, size):
+        q_ref[side, :, start : start + size] = jnp.dot(
+            qin_ref[side], wq[side, :, start : start + size], preferred_element_type=jnp.float32
         ).astype(jnp.bfloat16)
-    for side in range(2):
-        kv_ref[side] = jnp.dot(
-            min_ref[side], wkv[side], preferred_element_type=jnp.float32
+
+    def project_keyval(side, start, size):
+        kv_ref[side, :, start : start + size] = jnp.dot(
+            min_ref[side], wkv[side, :, start : start + size], preferred_element_type=jnp.float32
         ).astype(jnp.bfloat16)
 
     head_size = width // HEADS
@@ -196,27 +199,24 @@
         e = jnp.exp2((scores - top) * (LOG2_E / head_size**0.5))
         return (e * (1.0 / jnp.sum(e, axis=-1, keepdims=True))).astype(jnp.bfloat16)
 
-    def two_heads(i, carry):
-        start = pl.multiple_of(i * lanes, lanes)
-        for side in range(2):
-            query = q_ref[side, :, pl.ds(start, lanes)]
-            keys = split(kv_ref[side, :, pl.ds(start, lanes)])
-            values = split(kv_ref[side, :, pl.ds(width + start, lanes)])
-            scores = lax.dot_general(
-                query, keys, (((1,), (1,)), ((), ())), preferred_element_type=jnp.float32
-            )
-            probs = jnp.concatenate([soft(scores[:, :tokv]), soft(scores[:, tokv:])], axis=1)
-            ctx_ref[side, :, pl.ds(start, lanes)] = jnp.dot(
-                probs, values, preferred_element_type=jnp.float32
-            ).astype(jnp.bfloat16)
-        return carry
-
-    for i in range(HEADS // 2):
-        two_heads(i, 0)
-    for side in range(2):
-        updated = emb_ref[side].astype(jnp.float32) + jnp.dot(
-            ctx_ref[side], wo[side], preferred_element_type=jnp.float32
-        )
+    def two_heads_scores(side, i):
+        start = i * lanes
+        query = q_ref[side, :, start : start + lanes]
+        keys = split(kv_ref[side, :, start : start + lanes])
+        return lax.dot_general(
+            query, keys, (((1,), (1,)), ((), ())), preferred_element_type=jnp.float32
+        )
+
+    def two_heads(side, i, scores):
+        start = i * lanes
+        values = split(kv_ref[side, :, width + start : width + start + lanes])
+        probs = jnp.concatenate([soft(scores[:, :tokv]), soft(scores[:, tokv:])], axis=1)
+        ctx_ref[side, :, start : start + lanes] = jnp.dot(
+            probs, values, preferred_element_type=jnp.float32
+        ).astype(jnp.bfloat16)
+
+    def finish(side, product):
+        updated = emb_ref[side].astype(jnp.float32) + product
         final = (normed(updated) * gains_ref[side, 2:3, :]).astype(jnp.bfloat16)
         head = lax.dot_general(
             whead_ref[side], final, (((1,), (1,)), ((), ())), preferred_element_type=jnp.float32
@@ -224,6 +224,30 @@
         conf = 1.0 + jnp.exp(head[3:4, :])
         out_ref[side, 0:3, :] = head[0:3, :] * conf
         out_ref[side, 3:4, :] = conf
+
+    def project_out(side):
+        return jnp.dot(ctx_ref[side], wo[side], preferred_element_type=jnp.float32)
+
+    steps = HEADS // 2
+    block = 2 * width // steps
+    normalise(1)
+    project_keyval(0, 0, 2 * width)
+    normalise(0)
+    project_query(0, 0, width)
+    scores = two_heads_scores(0, 0)
+    for i in range(2 * steps):
+        side, at = i // steps, i % steps
+        now = scores
+        if side == 0:
+            project_keyval(1, at * block, block)
+            if at % 2:
+                project_query(1, at // 2 * block, block)
+        if i + 1 < 2 * steps:
+            scores = two_heads_scores((i + 1) // steps, (i + 1) % steps)
+        two_heads(side, at, now)
+        if i == steps:
+            finish(0, project_out(0))
+    finish(1, project_out(1))
 
 
 def load(*weights):
@@ -414,20 +438,10 @@
             below[0], above[0], shared = lax.optimization_barrier((below[0], above[0], shared))
     fetched = []
     for q in range(len(cuts)):
-        picked = [
-            pick(
-                lanes,
-                group,
-                cap,
-                me,
-                line,
-                wants,
-                embedded[q],
-                below[q][: group[-1]],
-                above[q][: group[-1]],
-            )
-            for group in groups[1:]
-        ]
+        picked = []
+        for group in groups[1:]:
+            near = below[q][: group[-1]], above[q][: group[-1]]
+            picked.append(pick(lanes, group, cap, me, line, wants, embedded[q], *near))
         fetched.append(list(shared))
         for group in picked:
             fetched[-1] += swap(group)

time: 138 us -> 137 us (level)
  Pallas kernels: 50.7 us -> 48.4 us
    pallas_call x2, Pallas kernels: 24.3 us -> 22 us  [decode(): pl.pallas_call(functools.partial(decode_kernel, parts, cuts), out_shape=j...]
where the time goes in v1:
time: 137 us; the launch traced here: 136 us
  Pallas kernels  48.4 us (35%)
  starting transfers between devices  36 us (26%)
  waiting for transfers between devices  26.9 us (20%)
  blocking collectives  19.7 us (14%)
  local copies, waits for them, and re-layouts  3.94 us (3%)
    pallas_call x2, Pallas kernels, decode(): pl.pallas_call(functools.partial(decode_kernel, parts, cuts), out_shape=j...  22 us
    all_to_all x1, blocking collectives, on_device(): lax.all_to_all(slotted, 'view', split_axis=0, concat_axis=0, tiled=True)  14.3 us
    ppermute x6, waiting for transfers between devices, on_device(): above[q].append(lax.ppermute((above[q] or [embedded[q]])[-1], 'view', down))  14.2 us
    ppermute x6, starting transfers between devices, on_device(): below[q].append(lax.ppermute((below[q] or [embedded[q]])[-1], 'view', up))  11.8 us
    pallas_call x3, Pallas kernels, route(): pl.pallas_call(functools.partial(route_kernel, lanes, parts, cap, base, c...  8.75 us
    ppermute x6, starting transfers between devices, on_device(): above[q].append(lax.ppermute((above[q] or [embedded[q]])[-1], 'view', down))  7.73 us
    pallas_call x1, Pallas kernels, load(): pl.pallas_call(load_kernel, out_shape=[jax.ShapeDtypeStruct(w.shape, w.dt...  7.5 us
    pallas_call x5, Pallas kernels, pick(): pl.pallas_call(functools.partial(pick_kernel, lanes, reach, slots, cap),...  7.15 us
  transfers between devices with their start and end apart: 30, of which 9 were waited for; matrix products, arithmetic and copies ran while one was open for 1% of the time, Pallas kernels for 28%

profile of v1, /device:TPU:0, one launch (start us, length us, event | category | flops | bytes accessed | tf_op | source)
XLA Modules:
  0.0 136.4 jit_solution(6996219080771544738)
XLA Ops:
  0.0 2.2 %constant_dynamic-slice_fusion.1 = (bf16[4,96,256]{2,1,0:T(8,128)(2,1)}, bf16[4,96,256]{2,1,0:T(8,128)(2,1)S(1)}, bf16[4,96,256]{2,1,0:T(8,128)(2,1)}, bf16[4,96,256]{2,1,0:T(8,128)(2,1)}) fusion(bf16[4,384,256]{2,1,0:T(8,128)(2,1)} %param.9, s32[]{:T(128)S(6)} %select_n.93, s32[]{:T(128)S(6)} %select_n.91, s32[]{:T(128)S(6)} %select_n.89, s32[]{:T(128)S(6)} %select_n.92), kind=kLoop, calls=%fused_computation.24 | loop fusion | bytes 1572880 | tf_op jit(solution)/shard_map/dynamic_slice | solution.py:384
  2.7 2.6 %collective-permute-start.2 = (bf16[4,96,256]{2,1,0:T(8,128)(2,1)}, bf16[4,96,256]{2,1,0:T(8,128)(2,1)}, u32[]{:S(2)}, u32[]{:S(2)}) collective-permute-start(bf16[4,96,256]{2,1,0:T(8,128)(2,1)} %get-tuple-element.125), channel_id=1, source_target_pairs={{0,3},{1,2},{2,1},{3,0},{4,7},{5,6},{6,5},{7,4},{8,11},{9,10},{10,... | collective-permute-start | bytes 589832 | tf_op jit(solution)/shard_map/ppermute | solution.py:385
  5.3 7.5 %load.1 = (bf16[1024,768]{1,0:T(8,128)(2,1)S(1)}, bf16[2,768,768]{2,1,0:T(8,128)(2,1)}, bf16[2,768,1536]{2,1,0:T(8,128)(2,1)}, bf16[2,768,768]{2,1,0:T(8,128)(2,1)}) custom-call(bf16[1024,768]{1,0:T(8,128)(2,1)S(1)} %copy-done, bf16[2,768,768]{2,1,0:T(8,128)(2,1)} %refs_1_.1, bf16[2,768,1536]{2,1,0:T(8,128)(2,1)} %refs_2_.1, bf16[2,768,768]{2,1,0:T(8,128)(2,1)} %refs_3_.1), custom_call_target="tpu_custom_call" | custom-call | tf_op jit(solution)/shard_map/load/pallas_call | solution.py:254
  13.5 2.1 %collective-permute-start.3 = (s32[16]{0:T(128)S(1)}, s32[16]{0:T(128)S(1)}, u32[]{:S(2)}, u32[]{:S(2)}) collective-permute-start(s32[16]{0:T(128)S(1)} %get-tuple-element.130), channel_id=1, source_target_pairs={{0,4},{4,0},{8,12},{12,8},{16,20},{20,16},{24,28},{28,24},{1,5},{5... | collective-permute-start | bytes 200 | tf_op jit(solution)/shard_map/ppermute | solution.py:404
  15.6 3.0 %embed.1 = (bf16[4,48,768]{2,1,0:T(8,128)(2,1)S(1)}, bf16[4,48,768]{2,1,0:T(8,128)(2,1)S(1)}, bf16[4,96,768]{2,1,0:T(8,128)(2,1)S(1)}) custom-call(s32[2]{0:T(128)S(1)} %pad_add_fusion.me_ref, bf16[1024,768]{1,0:T(8,128)(2,1)S(1)} %get-tuple-element.70.w_vmem, bf16[4,96,256]{2,1,0:T(8,128)(2,1)S(1)} %get-tuple-element.71.refs_0_, ...), custom_call_target="tpu_custom_call" | custom-call | flops 603979776 | bytes 3145728 | tf_op jit(solution)/shard_map/embed/pallas_call | solution.py:268
  20.0 4.6 %collective-permute-start.16 = (bf16[4,48,768]{2,1,0:T(8,128)(2,1)S(1)}, bf16[4,48,768]{2,1,0:T(8,128)(2,1)S(1)}, u32[]{:S(2)}, u32[]{:S(2)}) collective-permute-start(bf16[4,48,768]{2,1,0:T(8,128)(2,1)S(1)} %get-tuple-element.100.refs_0_), channel_id=1, source_target_pairs={{0,8},{4,12},{8,16},{12,20},{16,24},{20,28},{1,9},{5,13},{9,17},{1... | collective-permute-start | bytes 884744 | tf_op jit(solution)/shard_map/ppermute | solution.py:432
  24.6 1.3 collective-permute-start.5
  25.9 4.6 %collective-permute-start.4 = (bf16[4,48,768]{2,1,0:T(8,128)(2,1)S(1)}, bf16[4,48,768]{2,1,0:T(8,128)(2,1)S(1)}, u32[]{:S(2)}, u32[]{:S(2)}) collective-permute-start(bf16[4,48,768]{2,1,0:T(8,128)(2,1)S(1)} %get-tuple-element.77.refs_0_), channel_id=1, source_target_pairs={{0,8},{4,12},{8,16},{12,20},{16,24},{20,28},{1,9},{5,13},{9,17},{1... | collective-permute-start | bytes 884744 | tf_op jit(solution)/shard_map/ppermute | solution.py:432
  30.5 1.3 collective-permute-start.19
  33.2 1.5 %pick.5 = (bf16[1,2,96,768]{3,2,1,0:T(8,128)(2,1)S(1)}, bf16[1,2,96,768]{3,2,1,0:T(8,128)(2,1)S(1)}) custom-call(s32[2]{0:T(128)S(1)} %pad_add_fusion.me_ref, s32[4]{0:T(128)S(1)} %fusion.7.line_ref, s32[32]{0:T(128)S(1)} %pad_add_fusion.1.want_ref, bf16[4,96,768]{2,1,0:T(8,128)(2,1)S(1)} %get-tuple-element.79.refs_0_), custom_call_target="tpu_custom_call" | custom-call | bytes 1179648 | tf_op jit(solution)/shard_map/pick/pallas_call | solution.py:295
  34.7 1.7 %collective-permute-done.5.refs_3_.refs_4_ = bf16[4,48,768]{2,1,0:T(8,128)(2,1)S(1)} collective-permute-done((bf16[4,48,768]{2,1,0:T(8,128)(2,1)S(1)}, bf16[4,48,768]{2,1,0:T(8,128)(2,1)S(1)}, u32[]{:S(2)}, u32[]{:S(2)}) %collective-permute-start.5) | collective-permute-done | bytes 294944 | tf_op jit(solution)/shard_map/ppermute | solution.py:433
  38.4 1.3 collective-permute-start.7
  39.7 2.0 %collective-permute-done.19.refs_4_.refs_5_ = bf16[4,48,768]{2,1,0:T(8,128)(2,1)S(1)} collective-permute-done((bf16[4,48,768]{2,1,0:T(8,128)(2,1)S(1)}, bf16[4,48,768]{2,1,0:T(8,128)(2,1)S(1)}, u32[]{:S(2)}, u32[]{:S(2)}) %collective-permute-start.19) | collective-permute-done | bytes 294944 | tf_op jit(solution)/shard_map/ppermute | solution.py:433
  44.3 10.5 %collective-permute-done.7.refs_4_.refs_5_ = bf16[4,48,768]{2,1,0:T(8,128)(2,1)S(1)} collective-permute-done((bf16[4,48,768]{2,1,0:T(8,128)(2,1)S(1)}, bf16[4,48,768]{2,1,0:T(8,128)(2,1)S(1)}, u32[]{:S(2)}, u32[]{:S(2)}) %collective-permute-start.7) | collective-permute-done | bytes 294944 | tf_op jit(solution)/shard_map/ppermute | solution.py:433
  56.8 1.7 %pick.8 = (bf16[2,2,48,768]{3,2,1,0:T(8,128)(2,1)S(1)}, bf16[2,2,48,768]{3,2,1,0:T(8,128)(2,1)S(1)}) custom-call(s32[2]{0:T(128)S(1)} %pad_add_fusion.me_ref, s32[4]{0:T(128)S(1)} %fusion.7.line_ref, s32[32]{0:T(128)S(1)} %pad_add_fusion.1.want_ref, bf16[4,48,768]{2,1,0:T(8,128)(2,1)S(1)} %get-tuple-element.100.refs_0_, ...), custom_call_target="tpu_custom_call" | custom-call | bytes 1179648 | tf_op jit(solution)/shard_map/pick/pallas_call | solution.py:295
  59.3 1.7 %pick.6 = (bf16[2,2,48,768]{3,2,1,0:T(8,128)(2,1)S(1)}, bf16[2,2,48,768]{3,2,1,0:T(8,128)(2,1)S(1)}) custom-call(s32[2]{0:T(128)S(1)} %pad_add_fusion.me_ref, s32[4]{0:T(128)S(1)} %fusion.7.line_ref, s32[32]{0:T(128)S(1)} %pad_add_fusion.1.want_ref, bf16[4,48,768]{2,1,0:T(8,128)(2,1)S(1)} %get-tuple-element.77.refs_0_, ...), custom_call_target="tpu_custom_call" | custom-call | bytes 1179648 | tf_op jit(solution)/shard_map/pick/pallas_call | solution.py:295
  61.0 1.3 collective-permute-start.9
  65.5 1.3 collective-permute-start.12
  66.8 4.7 %collective-permute-done.23.refs_5_.refs_11_ = bf16[1,2,48,768]{3,2,1,0:T(8,128)(2,1)S(1)} collective-permute-done((bf16[1,2,48,768]{3,2,1,0:T(8,128)(2,1)S(1)}, bf16[1,2,48,768]{3,2,1,0:T(8,128)(2,1)S(1)}, u32[]{:S(2)}, u32[]{:S(2)}) %collective-permute-start.23) | collective-permute-done | bytes 147488 | tf_op jit(solution)/shard_map/ppermute | solution.py:418
  71.6 2.6 %route.4 = (bf16[2,48,768]{2,1,0:T(8,128)(2,1)S(1)}, bf16[2,48,768]{2,1,0:T(8,128)(2,1)S(1)}, bf16[2,48,768]{2,1,0:T(8,128)(2,1)S(1)}, bf16[2,48,768]{2,1,0:T(8,128)(2,1)S(1)}) custom-call(s32[2]{0:T(128)S(1)} %pad_add_fusion.me_ref, s32[4]{0:T(128)S(1)} %fusion.7.line_ref, s32[16]{0:T(128)S(1)} %get-tuple-element.119.side_ref, ...), custom_call_target="tpu_custom_call" | custom-call | bytes 1179648 | tf_op jit(solution)/shard_map/route/pallas_call | solution.py:321
  74.3 1.6 %collective-permute-start.25 = (bf16[2,48,768]{2,1,0:T(8,128)(2,1)S(1)}, bf16[2,48,768]{2,1,0:T(8,128)(2,1)S(1)}, u32[]{:S(2)}, u32[]{:S(2)}) collective-permute-start(bf16[2,48,768]{2,1,0:T(8,128)(2,1)S(1)} %get-tuple-element.107), channel_id=1, source_target_pairs={{0,2},{1,3},{2,0},{3,1},{4,6},{5,7},{6,4},{7,5},{8,10},{9,11},{10,... | collective-permute-start | bytes 442376 | tf_op jit(solution)/shard_map/ppermute | solution.py:463
  76.2 2.6 %route.3 = (bf16[2,48,768]{2,1,0:T(8,128)(2,1)S(1)}, bf16[2,48,768]{2,1,0:T(8,128)(2,1)S(1)}, bf16[2,48,768]{2,1,0:T(8,128)(2,1)S(1)}, bf16[2,48,768]{2,1,0:T(8,128)(2,1)S(1)}) custom-call(s32[2]{0:T(128)S(1)} %pad_add_fusion.me_ref, s32[4]{0:T(128)S(1)} %fusion.7.line_ref, s32[16]{0:T(128)S(1)} %get-tuple-element.119.side_ref, ...), custom_call_target="tpu_custom_call" | custom-call | bytes 1179648 | tf_op jit(solution)/shard_map/route/pallas_call | solution.py:321
  79.2 1.5 %collective-permute-start.14 = (bf16[2,48,768]{2,1,0:T(8,128)(2,1)S(1)}, bf16[2,48,768]{2,1,0:T(8,128)(2,1)S(1)}, u32[]{:S(2)}, u32[]{:S(2)}) collective-permute-start(bf16[2,48,768]{2,1,0:T(8,128)(2,1)S(1)} %get-tuple-element.98), channel_id=1, source_target_pairs={{0,2},{1,3},{2,0},{3,1},{4,6},{5,7},{6,4},{7,5},{8,10},{9,11},{10,... | collective-permute-start | bytes 442376 | tf_op jit(solution)/shard_map/ppermute | solution.py:463
  80.8 3.5 %route.5 = (bf16[2,96,768]{2,1,0:T(8,128)(2,1)S(1)}, bf16[2,96,768]{2,1,0:T(8,128)(2,1)S(1)}, bf16[2,96,768]{2,1,0:T(8,128)(2,1)S(1)}, bf16[2,96,768]{2,1,0:T(8,128)(2,1)S(1)}) custom-call(s32[2]{0:T(128)S(1)} %pad_add_fusion.me_ref, s32[4]{0:T(128)S(1)} %fusion.7.line_ref, s32[16]{0:T(128)S(1)} %and_select_fusion.side_ref, ...), custom_call_target="tpu_custom_call" | custom-call | bytes 2359296 | tf_op jit(solution)/shard_map/route/pallas_call | solution.py:321
  84.4 3.1 %collective-permute-done.14.refs_2_ = bf16[2,48,768]{2,1,0:T(8,128)(2,1)S(1)} collective-permute-done((bf16[2,48,768]{2,1,0:T(8,128)(2,1)S(1)}, bf16[2,48,768]{2,1,0:T(8,128)(2,1)S(1)}, u32[]{:S(2)}, u32[]{:S(2)}) %collective-permute-start.14) | collective-permute-done | bytes 147488 | tf_op jit(solution)/shard_map/ppermute | solution.py:463
  87.4 2.2 %collective-permute-done.15.refs_3_ = bf16[2,48,768]{2,1,0:T(8,128)(2,1)S(1)} collective-permute-done((bf16[2,48,768]{2,1,0:T(8,128)(2,1)S(1)}, bf16[2,48,768]{2,1,0:T(8,128)(2,1)S(1)}, u32[]{:S(2)}, u32[]{:S(2)}) %collective-permute-start.15) | collective-permute-done | bytes 147488 | tf_op jit(solution)/shard_map/ppermute | solution.py:463
  89.9 1.5 %collective-permute-start.28 = (bf16[2,96,768]{2,1,0:T(8,128)(2,1)S(1)}, bf16[2,96,768]{2,1,0:T(8,128)(2,1)S(1)}, u32[]{:S(2)}, u32[]{:S(2)}) collective-permute-start(bf16[2,96,768]{2,1,0:T(8,128)(2,1)S(1)} %get-tuple-element.115), channel_id=1, source_target_pairs={{0,2},{1,3},{2,0},{3,1},{4,6},{5,7},{6,4},{7,5},{8,10},{9,11},{10,... | collective-permute-start | bytes 884744 | tf_op jit(solution)/shard_map/ppermute | solution.py:463
  91.5 11.2 %decode.2 = f32[2,4,384]{2,1,0:T(4,128)S(1)} custom-call(s32[2]{0:T(128)S(1)} %pad_add_fusion.me_ref, f32[2,3,768]{2,1,0:T(4,128)S(1)} %copy.24.gains_ref, bf16[2,4,768]{2,1,0:T(4,128)(2,1)S(1)} %copy-done.3, bf16[2,768,1536]{2,1,0:T(8,128)(2,1)S(1)} %bitcast.16, bf16[2,768,768]{2,1,0:T(8,128)(2,1)S(1)} %copy-done.1, bf16[2,768,768]{2,1,0:T(8,128)(2,1)S(1)} %copy-done.2, ...), custom_call_target="tpu_custom_call" | custom-call | flops 5435817984 | bytes 11796480 | tf_op jit(solution)/shard_map/decode/pallas_call | solution.py:343
  102.7 1.8 %collective-permute-done.29.refs_3_ = bf16[2,96,768]{2,1,0:T(8,128)(2,1)S(1)} collective-permute-done((bf16[2,96,768]{2,1,0:T(8,128)(2,1)S(1)}, bf16[2,96,768]{2,1,0:T(8,128)(2,1)S(1)}, u32[]{:S(2)}, u32[]{:S(2)}) %collective-permute-start.29) | collective-permute-done | bytes 294944 | tf_op jit(solution)/shard_map/ppermute | solution.py:463
  104.6 10.8 %decode.3 = f32[2,4,384]{2,1,0:T(4,128)S(1)} custom-call(s32[2]{0:T(128)S(1)} %pad_add_fusion.me_ref, f32[2,3,768]{2,1,0:T(4,128)S(1)} %copy.24.gains_ref, bf16[2,4,768]{2,1,0:T(4,128)(2,1)S(1)} %copy-done.3, bf16[2,768,1536]{2,1,0:T(8,128)(2,1)S(1)} %bitcast.16, bf16[2,768,768]{2,1,0:T(8,128)(2,1)S(1)} %copy-done.1, bf16[2,768,768]{2,1,0:T(8,128)(2,1)S(1)} %copy-done.2, ...), custom_call_target="tpu_custom_call" | custom-call | flops 5435817984 | bytes 11796480 | tf_op jit(solution)/shard_map/decode/pallas_call | solution.py:343
  115.4 5.4 %all_gather.3 = f32[8,2,4,384]{3,2,1,0:T(4,128)S(1)} all-gather(f32[2,2,4,384]{3,2,1,0:T(4,128)S(1)} %pad_maximum_fusion.1), channel_id=1, replica_groups=mesh['view'=8,'mp'=4] {'mp'}, dimensions={0}, use_global_device_ids=true | all-gather | bytes 122880 | tf_op jit(solution)/shard_map/all_gather | solution.py:481
  121.1 14.3 %all_to_all.5 = f32[8,2,1664]{2,1,0:T(2,128)S(1)} all-to-all(f32[8,2,1664]{2,1,0:T(2,128)S(1)} %reshape.110), channel_id=1, replica_groups=mesh['view'=8,'mp'=4] {'view'}, dimensions={0} | all-to-all | bytes 212992 | tf_op jit(solution)/shard_map/all_to_all | solution.py:485
  (84 shorter events, 17.1 us)
Async XLA Ops:
  2.2 10.7 %collective-permute-start = (bf16[4,96,256]{2,1,0:T(8,128)(2,1)}, bf16[4,96,256]{2,1,0:T(8,128)(2,1)S(1)}, u32[]{:S(2)}, u32[]{:S(2)}) collective-permute-start(bf16[4,96,256]{2,1,0:T(8,128)(2,1)} %get-tuple-element.127), channel_id=1, source_target_pairs={{0,1},{1,0},{2,3},{3,2},{4,5},{5,4},{6,7},{7,6},{8,9},{9,8},{10,11... | collective-permute-start | bytes 589832 | tf_op jit(solution)/shard_map/ppermute | solution.py:385
  2.7 13.0 %collective-permute-start.2 = (bf16[4,96,256]{2,1,0:T(8,128)(2,1)}, bf16[4,96,256]{2,1,0:T(8,128)(2,1)}, u32[]{:S(2)}, u32[]{:S(2)}) collective-permute-start(bf16[4,96,256]{2,1,0:T(8,128)(2,1)} %get-tuple-element.125), channel_id=1, source_target_pairs={{0,3},{1,2},{2,1},{3,0},{4,7},{5,6},{6,5},{7,4},{8,11},{9,10},{10,... | collective-permute-start | bytes 589832 | tf_op jit(solution)/shard_map/ppermute | solution.py:385
  5.2 10.4 %collective-permute-start.1 = (bf16[4,96,256]{2,1,0:T(8,128)(2,1)}, bf16[4,96,256]{2,1,0:T(8,128)(2,1)}, u32[]{:S(2)}, u32[]{:S(2)}) collective-permute-start(bf16[4,96,256]{2,1,0:T(8,128)(2,1)} %get-tuple-element.128), channel_id=1, source_target_pairs={{0,2},{1,3},{2,0},{3,1},{4,6},{5,7},{6,4},{7,5},{8,10},{9,11},{10,... | collective-permute-start | bytes 589832 | tf_op jit(solution)/shard_map/ppermute | solution.py:385
  13.5 5.1 %collective-permute-start.3 = (s32[16]{0:T(128)S(1)}, s32[16]{0:T(128)S(1)}, u32[]{:S(2)}, u32[]{:S(2)}) collective-permute-start(s32[16]{0:T(128)S(1)} %get-tuple-element.130), channel_id=1, source_target_pairs={{0,4},{4,0},{8,12},{12,8},{16,20},{20,16},{24,28},{28,24},{1,5},{5... | collective-permute-start | bytes 200 | tf_op jit(solution)/shard_map/ppermute | solution.py:404
  18.7 11.7 %collective-permute-start.18 = (bf16[4,48,768]{2,1,0:T(8,128)(2,1)S(1)}, bf16[4,48,768]{2,1,0:T(8,128)(2,1)S(1)}, u32[]{:S(2)}, u32[]{:S(2)}) collective-permute-start(bf16[4,48,768]{2,1,0:T(8,128)(2,1)S(1)} %get-tuple-element.100.refs_0_), channel_id=1, source_target_pairs={{8,0},{12,4},{16,8},{20,12},{24,16},{28,20},{9,1},{13,5},{17,9},{2... | collective-permute-start | bytes 884744 | tf_op jit(solution)/shard_map/ppermute | solution.py:433
  20.0 11.8 %collective-permute-start.16 = (bf16[4,48,768]{2,1,0:T(8,128)(2,1)S(1)}, bf16[4,48,768]{2,1,0:T(8,128)(2,1)S(1)}, u32[]{:S(2)}, u32[]{:S(2)}) collective-permute-start(bf16[4,48,768]{2,1,0:T(8,128)(2,1)S(1)} %get-tuple-element.100.refs_0_), channel_id=1, source_target_pairs={{0,8},{4,12},{8,16},{12,20},{16,24},{20,28},{1,9},{5,13},{9,17},{1... | collective-permute-start | bytes 884744 | tf_op jit(solution)/shard_map/ppermute | solution.py:432
  24.6 11.8 %collective-permute-start.5 = (bf16[4,48,768]{2,1,0:T(8,128)(2,1)S(1)}, bf16[4,48,768]{2,1,0:T(8,128)(2,1)S(1)}, u32[]{:S(2)}, u32[]{:S(2)}) collective-permute-start(bf16[4,48,768]{2,1,0:T(8,128)(2,1)S(1)} %get-tuple-element.77.refs_0_), channel_id=1, source_target_pairs={{8,0},{12,4},{16,8},{20,12},{24,16},{28,20},{9,1},{13,5},{17,9},{2... | collective-permute-start | bytes 884744 | tf_op jit(solution)/shard_map/ppermute | solution.py:433
  25.9 10.7 %collective-permute-start.4 = (bf16[4,48,768]{2,1,0:T(8,128)(2,1)S(1)}, bf16[4,48,768]{2,1,0:T(8,128)(2,1)S(1)}, u32[]{:S(2)}, u32[]{:S(2)}) collective-permute-start(bf16[4,48,768]{2,1,0:T(8,128)(2,1)S(1)} %get-tuple-element.77.refs_0_), channel_id=1, source_target_pairs={{0,8},{4,12},{8,16},{12,20},{16,24},{20,28},{1,9},{5,13},{9,17},{1... | collective-permute-start | bytes 884744 | tf_op jit(solution)/shard_map/ppermute | solution.py:432
  30.5 11.2 %collective-permute-start.19 = (bf16[4,48,768]{2,1,0:T(8,128)(2,1)S(1)}, bf16[4,48,768]{2,1,0:T(8,128)(2,1)S(1)}, u32[]{:S(2)}, u32[]{:S(2)}) collective-permute-start(bf16[4,48,768]{2,1,0:T(8,128)(2,1)S(1)} %collective-permute-done.18.refs_3_.refs_4_), channel_id=1, source_target_pairs={{8,0},{12,4},{16,8},{20,12},{9,1},{13,5},{17,9},{21,13},{10,2},{14... | collective-permute-start | bytes 884744 | tf_op jit(solution)/shard_map/ppermute | solution.py:433
  31.8 11.2 %collective-permute-start.17 = (bf16[4,48,768]{2,1,0:T(8,128)(2,1)S(1)}, bf16[4,48,768]{2,1,0:T(8,128)(2,1)S(1)}, u32[]{:S(2)}, u32[]{:S(2)}) collective-permute-start(bf16[4,48,768]{2,1,0:T(8,128)(2,1)S(1)} %collective-permute-done.16.refs_1_), channel_id=1, source_target_pairs={{8,16},{12,20},{16,24},{20,28},{9,17},{13,21},{17,25},{21,29},{10,... | collective-permute-start | bytes 884744 | tf_op jit(solution)/shard_map/ppermute | solution.py:432
  36.6 7.8 %collective-permute-start.8 = (bf16[1,2,96,768]{3,2,1,0:T(8,128)(2,1)S(1)}, bf16[1,2,96,768]{3,2,1,0:T(8,128)(2,1)S(1)}, u32[]{:S(2)}, u32[]{:S(2)}) collective-permute-start(bf16[1,2,96,768]{3,2,1,0:T(8,128)(2,1)S(1)} %get-tuple-element.85), channel_id=1, source_target_pairs={{0,4},{4,0},{8,12},{12,8},{16,20},{20,16},{24,28},{28,24},{1,5},{5... | collective-permute-start | bytes 884744 | tf_op jit(solution)/shard_map/ppermute | solution.py:418
  37.7 6.6 %collective-permute-start.6 = (bf16[4,48,768]{2,1,0:T(8,128)(2,1)S(1)}, bf16[4,48,768]{2,1,0:T(8,128)(2,1)S(1)}, u32[]{:S(2)}, u32[]{:S(2)}) collective-permute-start(bf16[4,48,768]{2,1,0:T(8,128)(2,1)S(1)} %collective-permute-done.4.refs_1_), channel_id=1, source_target_pairs={{8,16},{12,20},{16,24},{20,28},{9,17},{13,21},{17,25},{21,29},{10,... | collective-permute-start | bytes 884744 | tf_op jit(solution)/shard_map/ppermute | solution.py:432
  38.4 16.4 %collective-permute-start.7 = (bf16[4,48,768]{2,1,0:T(8,128)(2,1)S(1)}, bf16[4,48,768]{2,1,0:T(8,128)(2,1)S(1)}, u32[]{:S(2)}, u32[]{:S(2)}) collective-permute-start(bf16[4,48,768]{2,1,0:T(8,128)(2,1)S(1)} %collective-permute-done.5.refs_3_.refs_4_), channel_id=1, source_target_pairs={{8,0},{12,4},{16,8},{20,12},{9,1},{13,5},{17,9},{21,13},{10,2},{14... | collective-permute-start | bytes 884744 | tf_op jit(solution)/shard_map/ppermute | solution.py:433
  41.7 19.3 %collective-permute-start.22 = (bf16[4,48,768]{2,1,0:T(8,128)(2,1)S(1)}, bf16[4,48,768]{2,1,0:T(8,128)(2,1)S(1)}, u32[]{:S(2)}, u32[]{:S(2)}) collective-permute-start(bf16[4,48,768]{2,1,0:T(8,128)(2,1)S(1)} %collective-permute-done.19.refs_4_.refs_5_), channel_id=1, source_target_pairs={{8,0},{12,4},{9,1},{13,5},{10,2},{14,6},{11,3},{15,7}} | collective-permute-start | bytes 884744 | tf_op jit(solution)/shard_map/ppermute | solution.py:433
  43.0 19.3 %collective-permute-start.21 = (bf16[4,48,768]{2,1,0:T(8,128)(2,1)S(1)}, bf16[4,48,768]{2,1,0:T(8,128)(2,1)S(1)}, u32[]{:S(2)}, u32[]{:S(2)}) collective-permute-start(bf16[4,48,768]{2,1,0:T(8,128)(2,1)S(1)} %collective-permute-done.17.refs_2_), channel_id=1, source_target_pairs={{16,24},{20,28},{17,25},{21,29},{18,26},{22,30},{19,27},{23,31}} | collective-permute-start | bytes 884744 | tf_op jit(solution)/shard_map/ppermute | solution.py:432
  54.8 9.5 %collective-permute-start.10 = (bf16[4,48,768]{2,1,0:T(8,128)(2,1)S(1)}, bf16[4,48,768]{2,1,0:T(8,128)(2,1)S(1)}, u32[]{:S(2)}, u32[]{:S(2)}) collective-permute-start(bf16[4,48,768]{2,1,0:T(8,128)(2,1)S(1)} %collective-permute-done.6.refs_2_), channel_id=1, source_target_pairs={{16,24},{20,28},{17,25},{21,29},{18,26},{22,30},{19,27},{23,31}} | collective-permute-start | bytes 884744 | tf_op jit(solution)/shard_map/ppermute | solution.py:432
  55.5 8.8 %collective-permute-start.11 = (bf16[4,48,768]{2,1,0:T(8,128)(2,1)S(1)}, bf16[4,48,768]{2,1,0:T(8,128)(2,1)S(1)}, u32[]{:S(2)}, u32[]{:S(2)}) collective-permute-start(bf16[4,48,768]{2,1,0:T(8,128)(2,1)S(1)} %collective-permute-done.7.refs_4_.refs_5_), channel_id=1, source_target_pairs={{8,0},{12,4},{9,1},{13,5},{10,2},{14,6},{11,3},{15,7}} | collective-permute-start | bytes 884744 | tf_op jit(solution)/shard_map/ppermute | solution.py:433
  56.8 34.7 %slice-start = ((s8[4718592]{0:T(1024)(128)(4,1)}), s8[4194304]{0:T(1024)(128)(4,1)S(1)}, s32[]{:S(2)}) async-start(s8[4718592]{0:T(1024)(128)(4,1)} %bitcast.15), calls=%async_computation.1 | async-start | bytes 8388608
  58.5 8.4 %collective-permute-start.20 = (bf16[2,2,48,768]{3,2,1,0:T(8,128)(2,1)S(1)}, bf16[2,2,48,768]{3,2,1,0:T(8,128)(2,1)S(1)}, u32[]{:S(2)}, u32[]{:S(2)}) collective-permute-start(bf16[2,2,48,768]{3,2,1,0:T(8,128)(2,1)S(1)} %get-tuple-element.102), channel_id=1, source_target_pairs={{0,4},{4,0},{8,12},{12,8},{16,20},{20,16},{24,28},{28,24},{1,5},{5... | collective-permute-start | bytes 884744 | tf_op jit(solution)/shard_map/ppermute | solution.py:418
  61.0 15.2 %collective-permute-start.9 = (bf16[2,2,48,768]{3,2,1,0:T(8,128)(2,1)S(1)}, bf16[2,2,48,768]{3,2,1,0:T(8,128)(2,1)S(1)}, u32[]{:S(2)}, u32[]{:S(2)}) collective-permute-start(bf16[2,2,48,768]{3,2,1,0:T(8,128)(2,1)S(1)} %get-tuple-element.93), channel_id=1, source_target_pairs={{0,4},{4,0},{8,12},{12,8},{16,20},{20,16},{24,28},{28,24},{1,5},{5... | collective-permute-start | bytes 884744 | tf_op jit(solution)/shard_map/ppermute | solution.py:418
  63.5 28.0 %slice-start.1 = ((s8[4718592]{0:T(1024)(128)(4,1)}), s8[524288]{0:T(1024)(128)(4,1)S(1)}, s32[]{:S(2)}) async-start(s8[4718592]{0:T(1024)(128)(4,1)} %bitcast.15), calls=%async_computation.2 | async-start | bytes 1048576
  63.5 8.1 %collective-permute-start.23 = (bf16[1,2,48,768]{3,2,1,0:T(8,128)(2,1)S(1)}, bf16[1,2,48,768]{3,2,1,0:T(8,128)(2,1)S(1)}, u32[]{:S(2)}, u32[]{:S(2)}) collective-permute-start(bf16[1,2,48,768]{3,2,1,0:T(8,128)(2,1)S(1)} %get-tuple-element.104), channel_id=1, source_target_pairs={{0,4},{4,0},{8,12},{12,8},{16,20},{20,16},{24,28},{28,24},{1,5},{5... | collective-permute-start | bytes 442376 | tf_op jit(solution)/shard_map/ppermute | solution.py:418
  65.5 10.8 %collective-permute-start.12 = (bf16[1,2,48,768]{3,2,1,0:T(8,128)(2,1)S(1)}, bf16[1,2,48,768]{3,2,1,0:T(8,128)(2,1)S(1)}, u32[]{:S(2)}, u32[]{:S(2)}) collective-permute-start(bf16[1,2,48,768]{3,2,1,0:T(8,128)(2,1)S(1)} %get-tuple-element.95), channel_id=1, source_target_pairs={{0,4},{4,0},{8,12},{12,8},{16,20},{20,16},{24,28},{28,24},{1,5},{5... | collective-permute-start | bytes 442376 | tf_op jit(solution)/shard_map/ppermute | solution.py:418
  74.2 6.5 %collective-permute-start.24 = (bf16[2,48,768]{2,1,0:T(8,128)(2,1)S(1)}, bf16[2,48,768]{2,1,0:T(8,128)(2,1)S(1)}, u32[]{:S(2)}, u32[]{:S(2)}) collective-permute-start(bf16[2,48,768]{2,1,0:T(8,128)(2,1)S(1)} %get-tuple-element.106), channel_id=1, source_target_pairs={{0,1},{1,0},{2,3},{3,2},{4,5},{5,4},{6,7},{7,6},{8,9},{9,8},{10,11... | collective-permute-start | bytes 442376 | tf_op jit(solution)/shard_map/ppermute | solution.py:463
  74.3 10.0 %collective-permute-start.25 = (bf16[2,48,768]{2,1,0:T(8,128)(2,1)S(1)}, bf16[2,48,768]{2,1,0:T(8,128)(2,1)S(1)}, u32[]{:S(2)}, u32[]{:S(2)}) collective-permute-start(bf16[2,48,768]{2,1,0:T(8,128)(2,1)S(1)} %get-tuple-element.107), channel_id=1, source_target_pairs={{0,2},{1,3},{2,0},{3,1},{4,6},{5,7},{6,4},{7,5},{8,10},{9,11},{10,... | collective-permute-start | bytes 442376 | tf_op jit(solution)/shard_map/ppermute | solution.py:463
  75.9 8.5 %collective-permute-start.26 = (bf16[2,48,768]{2,1,0:T(8,128)(2,1)S(1)}, bf16[2,48,768]{2,1,0:T(8,128)(2,1)S(1)}, u32[]{:S(2)}, u32[]{:S(2)}) collective-permute-start(bf16[2,48,768]{2,1,0:T(8,128)(2,1)S(1)} %get-tuple-element.108), channel_id=1, source_target_pairs={{0,3},{1,2},{2,1},{3,0},{4,7},{5,6},{6,5},{7,4},{8,11},{9,10},{10,... | collective-permute-start | bytes 442376 | tf_op jit(solution)/shard_map/ppermute | solution.py:463
  78.8 5.5 %collective-permute-start.13 = (bf16[2,48,768]{2,1,0:T(8,128)(2,1)S(1)}, bf16[2,48,768]{2,1,0:T(8,128)(2,1)S(1)}, u32[]{:S(2)}, u32[]{:S(2)}) collective-permute-start(bf16[2,48,768]{2,1,0:T(8,128)(2,1)S(1)} %get-tuple-element.97), channel_id=1, source_target_pairs={{0,1},{1,0},{2,3},{3,2},{4,5},{5,4},{6,7},{7,6},{8,9},{9,8},{10,11... | collective-permute-start | bytes 442376 | tf_op jit(solution)/shard_map/ppermute | solution.py:463
  79.2 8.2 %collective-permute-start.14 = (bf16[2,48,768]{2,1,0:T(8,128)(2,1)S(1)}, bf16[2,48,768]{2,1,0:T(8,128)(2,1)S(1)}, u32[]{:S(2)}, u32[]{:S(2)}) collective-permute-start(bf16[2,48,768]{2,1,0:T(8,128)(2,1)S(1)} %get-tuple-element.98), channel_id=1, source_target_pairs={{0,2},{1,3},{2,0},{3,1},{4,6},{5,7},{6,4},{7,5},{8,10},{9,11},{10,... | collective-permute-start | bytes 442376 | tf_op jit(solution)/shard_map/ppermute | solution.py:463
  80.7 8.9 %collective-permute-start.15 = (bf16[2,48,768]{2,1,0:T(8,128)(2,1)S(1)}, bf16[2,48,768]{2,1,0:T(8,128)(2,1)S(1)}, u32[]{:S(2)}, u32[]{:S(2)}) collective-permute-start(bf16[2,48,768]{2,1,0:T(8,128)(2,1)S(1)} %get-tuple-element.99), channel_id=1, source_target_pairs={{0,3},{1,2},{2,1},{3,0},{4,7},{5,6},{6,5},{7,4},{8,11},{9,10},{10,... | collective-permute-start | bytes 442376 | tf_op jit(solution)/shard_map/ppermute | solution.py:463
  89.6 13.1 %collective-permute-start.27 = (bf16[2,96,768]{2,1,0:T(8,128)(2,1)S(1)}, bf16[2,96,768]{2,1,0:T(8,128)(2,1)S(1)}, u32[]{:S(2)}, u32[]{:S(2)}) collective-permute-start(bf16[2,96,768]{2,1,0:T(8,128)(2,1)S(1)} %get-tuple-element.114), channel_id=1, source_target_pairs={{0,1},{1,0},{2,3},{3,2},{4,5},{5,4},{6,7},{7,6},{8,9},{9,8},{10,11... | collective-permute-start | bytes 884744 | tf_op jit(solution)/shard_map/ppermute | solution.py:463
  89.9 12.8 %collective-permute-start.28 = (bf16[2,96,768]{2,1,0:T(8,128)(2,1)S(1)}, bf16[2,96,768]{2,1,0:T(8,128)(2,1)S(1)}, u32[]{:S(2)}, u32[]{:S(2)}) collective-permute-start(bf16[2,96,768]{2,1,0:T(8,128)(2,1)S(1)} %get-tuple-element.115), channel_id=1, source_target_pairs={{0,2},{1,3},{2,0},{3,1},{4,6},{5,7},{6,4},{7,5},{8,10},{9,11},{10,... | collective-permute-start | bytes 884744 | tf_op jit(solution)/shard_map/ppermute | solution.py:463
  91.4 13.2 %collective-permute-start.29 = (bf16[2,96,768]{2,1,0:T(8,128)(2,1)S(1)}, bf16[2,96,768]{2,1,0:T(8,128)(2,1)S(1)}, u32[]{:S(2)}, u32[]{:S(2)}) collective-permute-start(bf16[2,96,768]{2,1,0:T(8,128)(2,1)S(1)} %get-tuple-element.116), channel_id=1, source_target_pairs={{0,3},{1,2},{2,1},{3,0},{4,7},{5,6},{6,5},{7,4},{8,11},{9,10},{10,... | collective-permute-start | bytes 884744 | tf_op jit(solution)/shard_map/ppermute | solution.py:463
  (6 other events, 80.7 us)

commit v2 on v1

--- a/solution.py
+++ b/solution.py
@@ -63,28 +63,19 @@
         copy.wait()
 
 
-def pick_kernel(lanes, reach, slots, cap, me_ref, line_ref, want_ref, *refs):
-    count = 1 + 2 * reach
-    own, below, above = refs[0], refs[1 : 1 + reach], refs[1 + reach : count]
-    outs = refs[count : count + lanes]
+def pick_kernel(lanes, slots, cap, me_ref, line_ref, want_ref, *refs):
+    count = len(slots)
+    sources, outs = refs[:count], refs[count : count + lanes]
     stage_ref, in_sem, out_sem = refs[count + lanes :]
-    place, lane = me_ref[0] // lanes, me_ref[0] % lanes
+    lane = me_ref[0] % lanes
     rows = line_ref.shape[0] * lanes
-
-    def sources(act):
-        for n, i in enumerate(slots):
-            at = line_ref[i]
-            if i == 0:
-                act(pltpu.make_async_copy(own, stage_ref.at[n], in_sem.at[n]))
-            for p in range(1, i + 1):
-                for want, source in ((place - p, below[p - 1]), (place + p, above[p - 1])):
-
-                    @pl.when(at == want)
-                    def _():
-                        act(pltpu.make_async_copy(source, stage_ref.at[n], in_sem.at[n]))
-
-    sources(lambda copy: copy.start())
-    sources(lambda copy: copy.wait())
+    copies = [
+        pltpu.make_async_copy(sources[n], stage_ref.at[n], in_sem.at[n]) for n in range(count)
+    ]
+    for copy in copies:
+        copy.start()
+    for copy in copies:
+        copy.wait()
     copies = []
     for j in range(lanes):
         for n, i in enumerate(slots):
@@ -289,13 +280,12 @@
     )(me, w_embed, *pieces)
 
 
-def pick(lanes, slots, cap, me, line, wants, own, below, above):
-    views, size, width = own.shape
-    reach = len(below)
+def pick(lanes, slots, cap, me, line, wants, sources):
+    views, size, width = sources[0].shape
     return pl.pallas_call(
-        functools.partial(pick_kernel, lanes, reach, slots, cap),
+        functools.partial(pick_kernel, lanes, slots, cap),
         out_shape=[jax.ShapeDtypeStruct((len(slots), cap, size, width), jnp.bfloat16)] * lanes,
-        in_specs=[SMEM, SMEM, SMEM] + [HBM] * (1 + 2 * reach),
+        in_specs=[SMEM, SMEM, SMEM] + [HBM] * len(sources),
         out_specs=[HBM] * lanes,
         scratch_shapes=[
             pltpu.VMEM((len(slots), views, size, width), jnp.bfloat16),
@@ -309,7 +299,7 @@
             transcendentals=0,
         ),
         name="pick",
-    )(me, line, wants, own, *below, *above)
+    )(me, line, wants, *sources)
 
 
 def route(lanes, parts, cap, cuts, groups, me, line, sides, fetched):
@@ -403,7 +393,13 @@
     wants = jnp.concatenate(
         [lax.ppermute(wanted, "view", xor_pairs(count, j)) if j else wanted for j in range(lanes)]
     )
-    nearest = [sorted(range(length), key=lambda at: (abs(at - z), at)) for z in range(length)]
+    ring = [0] + list(range(1, length, 2)) + list(range(2, length, 2))[::-1]
+    nearest = [[ring[(ring.index(z) - i) % length] for i in range(length)] for z in range(length)]
+    hop = [
+        (ring[k] * lanes + y, ring[(k + 1) % length] * lanes + y)
+        for k in range(length)
+        for y in range(lanes)
+    ]
     line = jnp.asarray(nearest, jnp.int32)[row // lanes]
 
     weights = load(w_embed, w_query, w_keyval, w_out)
@@ -419,34 +415,27 @@
             for j in range(lanes)
         ]
 
-    shared = pick(lanes, groups[0], cap, me, line, wants, whole, [], [])
-    below, above = [[] for _ in cuts], [[] for _ in cuts]
+    shared = pick(lanes, groups[0], cap, me, line, wants, [whole])
+    passed = [[part] for part in embedded]
     for p in range(1, length):
-        up = [
-            (z * lanes + y, (z + 1) * lanes + y) for z in range(p - 1, length - 1) for y in range(lanes)
-        ]
-        down = [
-            (z * lanes + y, (z - 1) * lanes + y) for z in range(1, length - p + 1) for y in range(lanes)
-        ]
         for q in range(len(cuts)):
-            below[q].append(lax.ppermute((below[q] or [embedded[q]])[-1], "view", up))
-            above[q].append(lax.ppermute((above[q] or [embedded[q]])[-1], "view", down))
+            passed[q].append(lax.ppermute(passed[q][-1], "view", hop))
         if p == 1:
-            below[0], above[0], shared = lax.optimization_barrier((below[0], above[0], shared))
+            passed[0][1], shared = lax.optimization_barrier((passed[0][1], shared))
             shared = swap(shared)
         if p == 2:
-            below[0], above[0], shared = lax.optimization_barrier((below[0], above[0], shared))
+            passed[0][2], shared = lax.optimization_barrier((passed[0][2], shared))
     fetched = []
     for q in range(len(cuts)):
         picked = []
         for group in groups[1:]:
-            near = below[q][: group[-1]], above[q][: group[-1]]
-            picked.append(pick(lanes, group, cap, me, line, wants, embedded[q], *near))
+            near = [passed[q][i] for i in group]
+            picked.append(pick(lanes, group, cap, me, line, wants, near))
         fetched.append(list(shared))
         for group in picked:
             fetched[-1] += swap(group)
     slot_pair = slot_side // 2
-    results, arrived = [], None
+    results = []
     for c in range(pair_dev):
         mine = jnp.logical_and(slot_side >= 0, slot_pair % pair_dev == c)
         place = jnp.where(mine, 2 * (slot_pair // pair_dev) + slot_side % 2, -1).astype(jnp.int32)
@@ -457,12 +446,11 @@
             parcels += route(
                 lanes, parts, cap, step, groups, me, line, place, [each for g in wave for each in g]
             )
-        if c:
-            parcels, arrived = lax.optimization_barrier((parcels, arrived))
-        arrived = [
-            lax.ppermute(parcel, "mp", xor_pairs(parts, i % parts)) if i % parts else parcel
-            for i, parcel in enumerate(parcels)
-        ]
+        arrived = []
+        for i, parcel in enumerate(parcels):
+            arrived.append(
+                lax.ppermute(parcel, "mp", xor_pairs(parts, i % parts)) if i % parts else parcel
+            )
         results.append(
             decode(
                 parts,

time: 137 us -> 131 us (0.956)
  starting transfers between devices: 36 us -> 21.8 us
  waiting for transfers between devices: 26.9 us -> 36.6 us
  blocking collectives: 19.7 us -> 17.2 us
  local copies, waits for them, and re-layouts: 3.94 us -> 5.58 us
    ppermute x12 -> x6, starting transfers between devices: 19.6 us -> 7.3 us  [on_device(): passed[q].append(lax.ppermute(passed[q][-1], 'view', hop))]
    ppermute x12 -> x6, waiting for transfers between devices: 14.4 us -> 24.2 us  [on_device(): passed[q].append(lax.ppermute(passed[q][-1], 'view', hop))]
    ppermute x9, waiting for transfers between devices: 7.11 us -> 3.13 us  [on_device(): lax.ppermute(parcel, 'mp', xor_pairs(parts, i % parts))]
    all_to_all x1, blocking collectives: 14.3 us -> 11.6 us  [on_device(): lax.all_to_all(slotted, 'view', split_axis=0, concat_axis=0, tiled=True)]
    ppermute x3, waiting for transfers between devices: 0.01 us -> 2.18 us  [on_device(): lax.ppermute(piece, 'mp', xor_pairs(parts, j))]
    ppermute x5, starting transfers between devices: 5.47 us -> 3.81 us  [swap(): lax.ppermute(picked[j], 'view', xor_pairs(count, j))]
    unnamed x18 -> x16, local copies, waits for them, and re-layouts: 0.05 us -> 1.7 us
    ppermute x5, waiting for transfers between devices: 5.44 us -> 7.08 us  [swap(): lax.ppermute(picked[j], 'view', xor_pairs(count, j))]
  transfers between devices with their start and end apart: 30 -> 24, of which waited for: 9 -> 10; matrix products, arithmetic and copies ran while one was open for 1% -> 1% of each run, Pallas kernels for 28% -> 29%
where the time goes in v2:
time: 131 us
  Pallas kernels  48.2 us (37%)
  waiting for transfers between devices  36.6 us (28%)
  starting transfers between devices  21.8 us (17%)
  blocking collectives  17.2 us (13%)
  local copies, waits for them, and re-layouts  5.58 us (4%)
    ppermute x6, waiting for transfers between devices, on_device(): passed[q].append(lax.ppermute(passed[q][-1], 'view', hop))  24.2 us
    pallas_call x2, Pallas kernels, decode(): pl.pallas_call(functools.partial(decode_kernel, parts, cuts), out_shape=j...  22 us
    all_to_all x1, blocking collectives, on_device(): lax.all_to_all(slotted, 'view', split_axis=0, concat_axis=0, tiled=True)  11.6 us
    pallas_call x3, Pallas kernels, route(): pl.pallas_call(functools.partial(route_kernel, lanes, parts, cap, base, c...  8.75 us
    pallas_call x1, Pallas kernels, load(): pl.pallas_call(load_kernel, out_shape=[jax.ShapeDtypeStruct(w.shape, w.dt...  7.52 us
    ppermute x6, starting transfers between devices, on_device(): passed[q].append(lax.ppermute(passed[q][-1], 'view', hop))  7.3 us
    ppermute x5, waiting for transfers between devices, swap(): lax.ppermute(picked[j], 'view', xor_pairs(count, j))  7.08 us
    pallas_call x5, Pallas kernels, pick(): pl.pallas_call(functools.partial(pick_kernel, lanes, slots, cap), out_sha...  6.97 us
  transfers between devices with their start and end apart: 24, of which 10 were waited for; matrix products, arithmetic and copies ran while one was open for 1% of the time, Pallas kernels for 29%

profile of v2, /device:TPU:0, one launch (start us, length us, event | category | flops | bytes accessed | tf_op | source)
XLA Modules:
  0.0 130.8 jit_solution(3235096270974239190)
XLA Ops:
  0.0 2.2 %constant_dynamic-slice_fusion.1 = (bf16[4,96,256]{2,1,0:T(8,128)(2,1)}, bf16[4,96,256]{2,1,0:T(8,128)(2,1)S(1)}, bf16[4,96,256]{2,1,0:T(8,128)(2,1)}, bf16[4,96,256]{2,1,0:T(8,128)(2,1)}) fusion(bf16[4,384,256]{2,1,0:T(8,128)(2,1)} %param.9, s32[]{:T(128)S(6)} %select_n.93, s32[]{:T(128)S(6)} %select_n.91, s32[]{:T(128)S(6)} %select_n.89, s32[]{:T(128)S(6)} %select_n.92), kind=kLoop, calls=%fused_computation.24 | loop fusion | bytes 1572880 | tf_op jit(solution)/shard_map/dynamic_slice | solution.py:374
  2.7 2.5 %collective-permute-start.1 = (bf16[4,96,256]{2,1,0:T(8,128)(2,1)}, bf16[4,96,256]{2,1,0:T(8,128)(2,1)}, u32[]{:S(2)}, u32[]{:S(2)}) collective-permute-start(bf16[4,96,256]{2,1,0:T(8,128)(2,1)} %get-tuple-element.112), channel_id=1, source_target_pairs={{0,2},{1,3},{2,0},{3,1},{4,6},{5,7},{6,4},{7,5},{8,10},{9,11},{10,... | collective-permute-start | bytes 589832 | tf_op jit(solution)/shard_map/ppermute | solution.py:375
  5.2 7.5 %load.1 = (bf16[1024,768]{1,0:T(8,128)(2,1)S(1)}, bf16[2,768,768]{2,1,0:T(8,128)(2,1)}, bf16[2,768,1536]{2,1,0:T(8,128)(2,1)}, bf16[2,768,768]{2,1,0:T(8,128)(2,1)}) custom-call(bf16[1024,768]{1,0:T(8,128)(2,1)S(1)} %copy-done, bf16[2,768,768]{2,1,0:T(8,128)(2,1)} %refs_1_.1, bf16[2,768,1536]{2,1,0:T(8,128)(2,1)} %refs_2_.1, bf16[2,768,768]{2,1,0:T(8,128)(2,1)} %refs_3_.1), custom_call_target="tpu_custom_call" | custom-call | tf_op jit(solution)/shard_map/load/pallas_call | solution.py:245
  12.9 2.2 %collective-permute-done.2.refs_3_ = bf16[4,96,256]{2,1,0:T(8,128)(2,1)} collective-permute-done((bf16[4,96,256]{2,1,0:T(8,128)(2,1)}, bf16[4,96,256]{2,1,0:T(8,128)(2,1)}, u32[]{:S(2)}, u32[]{:S(2)}) %collective-permute-start.2) | collective-permute-done | bytes 196640 | tf_op jit(solution)/shard_map/ppermute | solution.py:375
  15.7 1.6 %collective-permute-start.3 = (s32[16]{0:T(128)S(1)}, s32[16]{0:T(128)S(1)}, u32[]{:S(2)}, u32[]{:S(2)}) collective-permute-start(s32[16]{0:T(128)S(1)} %get-tuple-element.114), channel_id=1, source_target_pairs={{0,4},{4,0},{8,12},{12,8},{16,20},{20,16},{24,28},{28,24},{1,5},{5... | collective-permute-start | bytes 200 | tf_op jit(solution)/shard_map/ppermute | solution.py:394
  17.2 3.0 %embed.1 = (bf16[4,48,768]{2,1,0:T(8,128)(2,1)S(1)}, bf16[4,48,768]{2,1,0:T(8,128)(2,1)S(1)}, bf16[4,96,768]{2,1,0:T(8,128)(2,1)S(1)}) custom-call(s32[2]{0:T(128)S(1)} %pad_add_fusion.me_ref, bf16[1024,768]{1,0:T(8,128)(2,1)S(1)} %get-tuple-element.62.w_vmem, bf16[4,96,256]{2,1,0:T(8,128)(2,1)S(1)} %get-tuple-element.63.refs_0_, ...), custom_call_target="tpu_custom_call" | custom-call | flops 603979776 | bytes 3145728 | tf_op jit(solution)/shard_map/embed/pallas_call | solution.py:259
  20.4 1.6 %collective-permute-start.13 = (bf16[4,48,768]{2,1,0:T(8,128)(2,1)S(1)}, bf16[4,48,768]{2,1,0:T(8,128)(2,1)S(1)}, u32[]{:S(2)}, u32[]{:S(2)}) collective-permute-start(bf16[4,48,768]{2,1,0:T(8,128)(2,1)S(1)} %get-tuple-element.88), channel_id=1, source_target_pairs={{0,8},{4,12},{8,24},{12,28},{24,16},{28,20},{16,0},{20,4},{1,9},{5... | collective-permute-start | bytes 884744 | tf_op jit(solution)/shard_map/ppermute | solution.py:422
  21.9 2.6 %collective-permute-start.4 = (bf16[4,48,768]{2,1,0:T(8,128)(2,1)S(1)}, bf16[4,48,768]{2,1,0:T(8,128)(2,1)S(1)}, u32[]{:S(2)}, u32[]{:S(2)}) collective-permute-start(bf16[4,48,768]{2,1,0:T(8,128)(2,1)S(1)} %get-tuple-element.69), channel_id=1, source_target_pairs={{0,8},{4,12},{8,24},{12,28},{24,16},{28,20},{16,0},{20,4},{1,9},{5... | collective-permute-start | bytes 884744 | tf_op jit(solution)/shard_map/ppermute | solution.py:422
  24.5 6.6 %collective-permute-done.13.refs_0_ = bf16[4,48,768]{2,1,0:T(8,128)(2,1)S(1)} collective-permute-done((bf16[4,48,768]{2,1,0:T(8,128)(2,1)S(1)}, bf16[4,48,768]{2,1,0:T(8,128)(2,1)S(1)}, u32[]{:S(2)}, u32[]{:S(2)}) %collective-permute-start.13) | collective-permute-done | bytes 294944 | tf_op jit(solution)/shard_map/ppermute | solution.py:422
  32.6 1.5 %pick.5 = (bf16[1,2,96,768]{3,2,1,0:T(8,128)(2,1)S(1)}, bf16[1,2,96,768]{3,2,1,0:T(8,128)(2,1)S(1)}) custom-call(s32[2]{0:T(128)S(1)} %pad_add_fusion.me_ref, s32[4]{0:T(128)S(1)} %fusion.7.line_ref, s32[32]{0:T(128)S(1)} %pad_add_fusion.1.want_ref, bf16[4,96,768]{2,1,0:T(8,128)(2,1)S(1)} %get-tuple-element.71.refs_0_), custom_call_target="tpu_custom_call" | custom-call | bytes 1179648 | tf_op jit(solution)/shard_map/pick/pallas_call | solution.py:285
  34.1 3.3 %collective-permute-done.4.refs_0_ = bf16[4,48,768]{2,1,0:T(8,128)(2,1)S(1)} collective-permute-done((bf16[4,48,768]{2,1,0:T(8,128)(2,1)S(1)}, bf16[4,48,768]{2,1,0:T(8,128)(2,1)S(1)}, u32[]{:S(2)}, u32[]{:S(2)}) %collective-permute-start.4) | collective-permute-done | bytes 294944 | tf_op jit(solution)/shard_map/ppermute | solution.py:422
  38.8 5.0 %collective-permute-done.14.refs_1_ = bf16[4,48,768]{2,1,0:T(8,128)(2,1)S(1)} collective-permute-done((bf16[4,48,768]{2,1,0:T(8,128)(2,1)S(1)}, bf16[4,48,768]{2,1,0:T(8,128)(2,1)S(1)}, u32[]{:S(2)}, u32[]{:S(2)}) %collective-permute-start.14) | collective-permute-done | bytes 294944 | tf_op jit(solution)/shard_map/ppermute | solution.py:422
  44.6 5.5 %collective-permute-done.5.refs_1_ = bf16[4,48,768]{2,1,0:T(8,128)(2,1)S(1)} collective-permute-done((bf16[4,48,768]{2,1,0:T(8,128)(2,1)S(1)}, bf16[4,48,768]{2,1,0:T(8,128)(2,1)S(1)}, u32[]{:S(2)}, u32[]{:S(2)}) %collective-permute-start.5) | collective-permute-done | bytes 294944 | tf_op jit(solution)/shard_map/ppermute | solution.py:422
  50.9 1.6 %pick.8 = (bf16[2,2,48,768]{3,2,1,0:T(8,128)(2,1)S(1)}, bf16[2,2,48,768]{3,2,1,0:T(8,128)(2,1)S(1)}) custom-call(s32[2]{0:T(128)S(1)} %pad_add_fusion.me_ref, s32[4]{0:T(128)S(1)} %fusion.7.line_ref, s32[32]{0:T(128)S(1)} %pad_add_fusion.1.want_ref, bf16[4,48,768]{2,1,0:T(8,128)(2,1)S(1)} %collective-permute-done.13.refs_0_, ...), custom_call_target="tpu_custom_call" | custom-call | bytes 1179648 | tf_op jit(solution)/shard_map/pick/pallas_call | solution.py:285
  53.1 1.6 %pick.6 = (bf16[2,2,48,768]{3,2,1,0:T(8,128)(2,1)S(1)}, bf16[2,2,48,768]{3,2,1,0:T(8,128)(2,1)S(1)}) custom-call(s32[2]{0:T(128)S(1)} %pad_add_fusion.me_ref, s32[4]{0:T(128)S(1)} %fusion.7.line_ref, s32[32]{0:T(128)S(1)} %pad_add_fusion.1.want_ref, bf16[4,48,768]{2,1,0:T(8,128)(2,1)S(1)} %collective-permute-done.4.refs_0_, ...), custom_call_target="tpu_custom_call" | custom-call | bytes 1179648 | tf_op jit(solution)/shard_map/pick/pallas_call | solution.py:285
  54.8 1.6 %collective-permute-start.7 = (bf16[2,2,48,768]{3,2,1,0:T(8,128)(2,1)S(1)}, bf16[2,2,48,768]{3,2,1,0:T(8,128)(2,1)S(1)}, u32[]{:S(2)}, u32[]{:S(2)}) collective-permute-start(bf16[2,2,48,768]{3,2,1,0:T(8,128)(2,1)S(1)} %get-tuple-element.81), channel_id=1, source_target_pairs={{0,4},{4,0},{8,12},{12,8},{16,20},{20,16},{24,28},{28,24},{1,5},{5... | collective-permute-start | bytes 884744 | tf_op jit(solution)/shard_map/ppermute | solution.py:414
  56.4 1.1 pick.9
  58.1 3.7 %collective-permute-done.8.refs_0_ = bf16[4,48,768]{2,1,0:T(8,128)(2,1)S(1)} collective-permute-done((bf16[4,48,768]{2,1,0:T(8,128)(2,1)S(1)}, bf16[4,48,768]{2,1,0:T(8,128)(2,1)S(1)}, u32[]{:S(2)}, u32[]{:S(2)}) %collective-permute-start.8) | collective-permute-done | bytes 294944 | tf_op jit(solution)/shard_map/ppermute | solution.py:422
  61.8 1.1 pick.7
  63.4 7.1 %collective-permute-done.17.refs_5_.refs_11_ = bf16[1,2,48,768]{3,2,1,0:T(8,128)(2,1)S(1)} collective-permute-done((bf16[1,2,48,768]{3,2,1,0:T(8,128)(2,1)S(1)}, bf16[1,2,48,768]{3,2,1,0:T(8,128)(2,1)S(1)}, u32[]{:S(2)}, u32[]{:S(2)}) %collective-permute-start.17) | collective-permute-done | bytes 147488 | tf_op jit(solution)/shard_map/ppermute | solution.py:414
  70.5 2.6 %route.4 = (bf16[2,48,768]{2,1,0:T(8,128)(2,1)S(1)}, bf16[2,48,768]{2,1,0:T(8,128)(2,1)S(1)}, bf16[2,48,768]{2,1,0:T(8,128)(2,1)S(1)}, bf16[2,48,768]{2,1,0:T(8,128)(2,1)S(1)}) custom-call(s32[2]{0:T(128)S(1)} %pad_add_fusion.me_ref, s32[4]{0:T(128)S(1)} %fusion.7.line_ref, s32[16]{0:T(128)S(1)} %get-tuple-element.103.side_ref, ...), custom_call_target="tpu_custom_call" | custom-call | bytes 1179648 | tf_op jit(solution)/shard_map/route/pallas_call | solution.py:311
  73.2 1.6 %collective-permute-start.19 = (bf16[2,48,768]{2,1,0:T(8,128)(2,1)S(1)}, bf16[2,48,768]{2,1,0:T(8,128)(2,1)S(1)}, u32[]{:S(2)}, u32[]{:S(2)}) collective-permute-start(bf16[2,48,768]{2,1,0:T(8,128)(2,1)S(1)} %get-tuple-element.95), channel_id=1, source_target_pairs={{0,2},{1,3},{2,0},{3,1},{4,6},{5,7},{6,4},{7,5},{8,10},{9,11},{10,... | collective-permute-start | bytes 442376 | tf_op jit(solution)/shard_map/ppermute | solution.py:452
  75.1 2.6 %route.3 = (bf16[2,48,768]{2,1,0:T(8,128)(2,1)S(1)}, bf16[2,48,768]{2,1,0:T(8,128)(2,1)S(1)}, bf16[2,48,768]{2,1,0:T(8,128)(2,1)S(1)}, bf16[2,48,768]{2,1,0:T(8,128)(2,1)S(1)}) custom-call(s32[2]{0:T(128)S(1)} %pad_add_fusion.me_ref, s32[4]{0:T(128)S(1)} %fusion.7.line_ref, s32[16]{0:T(128)S(1)} %get-tuple-element.103.side_ref, ...), custom_call_target="tpu_custom_call" | custom-call | bytes 1179648 | tf_op jit(solution)/shard_map/route/pallas_call | solution.py:311
  78.1 1.5 %collective-permute-start.11 = (bf16[2,48,768]{2,1,0:T(8,128)(2,1)S(1)}, bf16[2,48,768]{2,1,0:T(8,128)(2,1)S(1)}, u32[]{:S(2)}, u32[]{:S(2)}) collective-permute-start(bf16[2,48,768]{2,1,0:T(8,128)(2,1)S(1)} %get-tuple-element.86), channel_id=1, source_target_pairs={{0,2},{1,3},{2,0},{3,1},{4,6},{5,7},{6,4},{7,5},{8,10},{9,11},{10,... | collective-permute-start | bytes 442376 | tf_op jit(solution)/shard_map/ppermute | solution.py:452
  79.7 3.5 %route.5 = (bf16[2,96,768]{2,1,0:T(8,128)(2,1)S(1)}, bf16[2,96,768]{2,1,0:T(8,128)(2,1)S(1)}, bf16[2,96,768]{2,1,0:T(8,128)(2,1)S(1)}, bf16[2,96,768]{2,1,0:T(8,128)(2,1)S(1)}) custom-call(s32[2]{0:T(128)S(1)} %pad_add_fusion.me_ref, s32[4]{0:T(128)S(1)} %fusion.7.line_ref, s32[16]{0:T(128)S(1)} %and_select_fusion.side_ref, ...), custom_call_target="tpu_custom_call" | custom-call | bytes 2359296 | tf_op jit(solution)/shard_map/route/pallas_call | solution.py:311
  83.9 1.5 %collective-permute-start.22 = (bf16[2,96,768]{2,1,0:T(8,128)(2,1)S(1)}, bf16[2,96,768]{2,1,0:T(8,128)(2,1)S(1)}, u32[]{:S(2)}, u32[]{:S(2)}) collective-permute-start(bf16[2,96,768]{2,1,0:T(8,128)(2,1)S(1)} %get-tuple-element.99), channel_id=1, source_target_pairs={{0,2},{1,3},{2,0},{3,1},{4,6},{5,7},{6,4},{7,5},{8,10},{9,11},{10,... | collective-permute-start | bytes 884744 | tf_op jit(solution)/shard_map/ppermute | solution.py:452
  86.3 2.2 %collective-permute-done.12.refs_3_ = bf16[2,48,768]{2,1,0:T(8,128)(2,1)S(1)} collective-permute-done((bf16[2,48,768]{2,1,0:T(8,128)(2,1)S(1)}, bf16[2,48,768]{2,1,0:T(8,128)(2,1)S(1)}, u32[]{:S(2)}, u32[]{:S(2)}) %collective-permute-start.12) | collective-permute-done | bytes 147488 | tf_op jit(solution)/shard_map/ppermute | solution.py:452
  88.5 1.7 %copy-done.3 = bf16[2,768,768]{2,1,0:T(8,128)(2,1)S(1)} copy-done((bf16[2,768,768]{2,1,0:T(8,128)(2,1)S(1)}, bf16[2,768,768]{2,1,0:T(8,128)(2,1)}, u32[]{:S(2)}) %copy-start.3) | copy-done | bytes 2359320
  90.2 11.2 %decode.2 = f32[2,4,384]{2,1,0:T(4,128)S(1)} custom-call(s32[2]{0:T(128)S(1)} %pad_add_fusion.me_ref, f32[2,3,768]{2,1,0:T(4,128)S(1)} %copy.24.gains_ref, bf16[2,4,768]{2,1,0:T(4,128)(2,1)S(1)} %copy-done.4, bf16[2,768,1536]{2,1,0:T(8,128)(2,1)S(1)} %copy-done.1, bf16[2,768,768]{2,1,0:T(8,128)(2,1)S(1)} %copy-done.2, bf16[2,768,768]{2,1,0:T(8,128)(2,1)S(1)} %copy-done.3, ...), custom_call_target="tpu_custom_call" | custom-call | flops 5435817984 | bytes 11796480 | tf_op jit(solution)/shard_map/decode/pallas_call | solution.py:333
  101.4 10.8 %decode.3 = f32[2,4,384]{2,1,0:T(4,128)S(1)} custom-call(s32[2]{0:T(128)S(1)} %pad_add_fusion.me_ref, f32[2,3,768]{2,1,0:T(4,128)S(1)} %copy.24.gains_ref, bf16[2,4,768]{2,1,0:T(4,128)(2,1)S(1)} %copy-done.4, bf16[2,768,1536]{2,1,0:T(8,128)(2,1)S(1)} %copy-done.1, bf16[2,768,768]{2,1,0:T(8,128)(2,1)S(1)} %copy-done.2, bf16[2,768,768]{2,1,0:T(8,128)(2,1)S(1)} %copy-done.3, ...), custom_call_target="tpu_custom_call" | custom-call | flops 5435817984 | bytes 11796480 | tf_op jit(solution)/shard_map/decode/pallas_call | solution.py:333
  112.2 5.6 %all_gather.3 = f32[8,2,4,384]{3,2,1,0:T(4,128)S(1)} all-gather(f32[2,2,4,384]{3,2,1,0:T(4,128)S(1)} %pad_maximum_fusion.1), channel_id=1, replica_groups=mesh['view'=8,'mp'=4] {'mp'}, dimensions={0}, use_global_device_ids=true | all-gather | bytes 122880 | tf_op jit(solution)/shard_map/all_gather | solution.py:469
  118.1 11.6 %all_to_all.5 = f32[8,2,1664]{2,1,0:T(2,128)S(1)} all-to-all(f32[8,2,1664]{2,1,0:T(2,128)S(1)} %reshape.110), channel_id=1, replica_groups=mesh['view'=8,'mp'=4] {'view'}, dimensions={0} | all-to-all | bytes 212992 | tf_op jit(solution)/shard_map/all_to_all | solution.py:473
  (69 shorter events, 11.4 us)
Async XLA Ops:
  0.0 5.2 %copy-start = (bf16[1024,768]{1,0:T(8,128)(2,1)S(1)}, bf16[1024,768]{1,0:T(8,128)(2,1)}, u32[]{:S(2)}) copy-start(bf16[1024,768]{1,0:T(8,128)(2,1)} %refs_0_.1) | copy-start | bytes 4718596
  2.2 10.7 %collective-permute-start = (bf16[4,96,256]{2,1,0:T(8,128)(2,1)}, bf16[4,96,256]{2,1,0:T(8,128)(2,1)S(1)}, u32[]{:S(2)}, u32[]{:S(2)}) collective-permute-start(bf16[4,96,256]{2,1,0:T(8,128)(2,1)} %get-tuple-element.111), channel_id=1, source_target_pairs={{0,1},{1,0},{2,3},{3,2},{4,5},{5,4},{6,7},{7,6},{8,9},{9,8},{10,11... | collective-permute-start | bytes 589832 | tf_op jit(solution)/shard_map/ppermute | solution.py:375
  2.7 10.2 %collective-permute-start.1 = (bf16[4,96,256]{2,1,0:T(8,128)(2,1)}, bf16[4,96,256]{2,1,0:T(8,128)(2,1)}, u32[]{:S(2)}, u32[]{:S(2)}) collective-permute-start(bf16[4,96,256]{2,1,0:T(8,128)(2,1)} %get-tuple-element.112), channel_id=1, source_target_pairs={{0,2},{1,3},{2,0},{3,1},{4,6},{5,7},{6,4},{7,5},{8,10},{9,11},{10,... | collective-permute-start | bytes 589832 | tf_op jit(solution)/shard_map/ppermute | solution.py:375
  5.1 9.9 %collective-permute-start.2 = (bf16[4,96,256]{2,1,0:T(8,128)(2,1)}, bf16[4,96,256]{2,1,0:T(8,128)(2,1)}, u32[]{:S(2)}, u32[]{:S(2)}) collective-permute-start(bf16[4,96,256]{2,1,0:T(8,128)(2,1)} %get-tuple-element.109), channel_id=1, source_target_pairs={{0,3},{1,2},{2,1},{3,0},{4,7},{5,6},{6,5},{7,4},{8,11},{9,10},{10,... | collective-permute-start | bytes 589832 | tf_op jit(solution)/shard_map/ppermute | solution.py:375
  5.2 9.8 %copy-start.6 = (s32[8,2]{0,1:T(2,128)S(1)}, s32[8,2]{0,1:T(2,128)}, u32[]{:S(2)}) copy-start(s32[8,2]{0,1:T(2,128)} %param.10) | copy-start | bytes 196
  15.7 4.6 %collective-permute-start.3 = (s32[16]{0:T(128)S(1)}, s32[16]{0:T(128)S(1)}, u32[]{:S(2)}, u32[]{:S(2)}) collective-permute-start(s32[16]{0:T(128)S(1)} %get-tuple-element.114), channel_id=1, source_target_pairs={{0,4},{4,0},{8,12},{12,8},{16,20},{20,16},{24,28},{28,24},{1,5},{5... | collective-permute-start | bytes 200 | tf_op jit(solution)/shard_map/ppermute | solution.py:394
  20.3 52.9 %copy-start.5 = (f32[2,3,768]{2,0,1:T(2,128)S(1)}, f32[2,3,768]{2,0,1:T(2,128)}, u32[]{:S(2)}) copy-start(f32[2,3,768]{2,0,1:T(2,128)} %param.16) | copy-start | bytes 55300
  20.4 10.8 %collective-permute-start.13 = (bf16[4,48,768]{2,1,0:T(8,128)(2,1)S(1)}, bf16[4,48,768]{2,1,0:T(8,128)(2,1)S(1)}, u32[]{:S(2)}, u32[]{:S(2)}) collective-permute-start(bf16[4,48,768]{2,1,0:T(8,128)(2,1)S(1)} %get-tuple-element.88), channel_id=1, source_target_pairs={{0,8},{4,12},{8,24},{12,28},{24,16},{28,20},{16,0},{20,4},{1,9},{5... | collective-permute-start | bytes 884744 | tf_op jit(solution)/shard_map/ppermute | solution.py:422
  21.9 15.5 %collective-permute-start.4 = (bf16[4,48,768]{2,1,0:T(8,128)(2,1)S(1)}, bf16[4,48,768]{2,1,0:T(8,128)(2,1)S(1)}, u32[]{:S(2)}, u32[]{:S(2)}) collective-permute-start(bf16[4,48,768]{2,1,0:T(8,128)(2,1)S(1)} %get-tuple-element.69), channel_id=1, source_target_pairs={{0,8},{4,12},{8,24},{12,28},{24,16},{28,20},{16,0},{20,4},{1,9},{5... | collective-permute-start | bytes 884744 | tf_op jit(solution)/shard_map/ppermute | solution.py:422
  31.1 12.6 %collective-permute-start.14 = (bf16[4,48,768]{2,1,0:T(8,128)(2,1)S(1)}, bf16[4,48,768]{2,1,0:T(8,128)(2,1)S(1)}, u32[]{:S(2)}, u32[]{:S(2)}) collective-permute-start(bf16[4,48,768]{2,1,0:T(8,128)(2,1)S(1)} %collective-permute-done.13.refs_0_), channel_id=1, source_target_pairs={{0,8},{4,12},{8,24},{12,28},{24,16},{28,20},{16,0},{20,4},{1,9},{5... | collective-permute-start | bytes 884744 | tf_op jit(solution)/shard_map/ppermute | solution.py:422
  37.5 12.6 %collective-permute-start.5 = (bf16[4,48,768]{2,1,0:T(8,128)(2,1)S(1)}, bf16[4,48,768]{2,1,0:T(8,128)(2,1)S(1)}, u32[]{:S(2)}, u32[]{:S(2)}) collective-permute-start(bf16[4,48,768]{2,1,0:T(8,128)(2,1)S(1)} %collective-permute-done.4.refs_0_), channel_id=1, source_target_pairs={{0,8},{4,12},{8,24},{12,28},{24,16},{28,20},{16,0},{20,4},{1,9},{5... | collective-permute-start | bytes 884744 | tf_op jit(solution)/shard_map/ppermute | solution.py:422
  38.2 11.9 %collective-permute-start.6 = (bf16[1,2,96,768]{3,2,1,0:T(8,128)(2,1)S(1)}, bf16[1,2,96,768]{3,2,1,0:T(8,128)(2,1)S(1)}, u32[]{:S(2)}, u32[]{:S(2)}) collective-permute-start(bf16[1,2,96,768]{3,2,1,0:T(8,128)(2,1)S(1)} %get-tuple-element.76), channel_id=1, source_target_pairs={{0,4},{4,0},{8,12},{12,8},{16,20},{20,16},{24,28},{28,24},{1,5},{5... | collective-permute-start | bytes 884744 | tf_op jit(solution)/shard_map/ppermute | solution.py:414
  43.8 12.6 %collective-permute-start.16 = (bf16[4,48,768]{2,1,0:T(8,128)(2,1)S(1)}, bf16[4,48,768]{2,1,0:T(8,128)(2,1)S(1)}, u32[]{:S(2)}, u32[]{:S(2)}) collective-permute-start(bf16[4,48,768]{2,1,0:T(8,128)(2,1)S(1)} %collective-permute-done.14.refs_1_), channel_id=1, source_target_pairs={{0,8},{4,12},{8,24},{12,28},{24,16},{28,20},{16,0},{20,4},{1,9},{5... | collective-permute-start | bytes 884744 | tf_op jit(solution)/shard_map/ppermute | solution.py:422
  50.1 11.7 %collective-permute-start.8 = (bf16[4,48,768]{2,1,0:T(8,128)(2,1)S(1)}, bf16[4,48,768]{2,1,0:T(8,128)(2,1)S(1)}, u32[]{:S(2)}, u32[]{:S(2)}) collective-permute-start(bf16[4,48,768]{2,1,0:T(8,128)(2,1)S(1)} %collective-permute-done.5.refs_1_), channel_id=1, source_target_pairs={{0,8},{4,12},{8,24},{12,28},{24,16},{28,20},{16,0},{20,4},{1,9},{5... | collective-permute-start | bytes 884744 | tf_op jit(solution)/shard_map/ppermute | solution.py:422
  52.5 10.9 %collective-permute-start.15 = (bf16[2,2,48,768]{3,2,1,0:T(8,128)(2,1)S(1)}, bf16[2,2,48,768]{3,2,1,0:T(8,128)(2,1)S(1)}, u32[]{:S(2)}, u32[]{:S(2)}) collective-permute-start(bf16[2,2,48,768]{3,2,1,0:T(8,128)(2,1)S(1)} %get-tuple-element.90), channel_id=1, source_target_pairs={{0,4},{4,0},{8,12},{12,8},{16,20},{20,16},{24,28},{28,24},{1,5},{5... | collective-permute-start | bytes 884744 | tf_op jit(solution)/shard_map/ppermute | solution.py:414
  53.1 35.4 %copy-start.2 = (bf16[2,768,768]{2,1,0:T(8,128)(2,1)S(1)}, bf16[2,768,768]{2,1,0:T(8,128)(2,1)}, u32[]{:S(2)}) copy-start(bf16[2,768,768]{2,1,0:T(8,128)(2,1)} %get-tuple-element.60.wq) | copy-start | bytes 7077892
  54.8 20.3 %collective-permute-start.7 = (bf16[2,2,48,768]{3,2,1,0:T(8,128)(2,1)S(1)}, bf16[2,2,48,768]{3,2,1,0:T(8,128)(2,1)S(1)}, u32[]{:S(2)}, u32[]{:S(2)}) collective-permute-start(bf16[2,2,48,768]{3,2,1,0:T(8,128)(2,1)S(1)} %get-tuple-element.81), channel_id=1, source_target_pairs={{0,4},{4,0},{8,12},{12,8},{16,20},{20,16},{24,28},{28,24},{1,5},{5... | collective-permute-start | bytes 884744 | tf_op jit(solution)/shard_map/ppermute | solution.py:414
  57.5 13.0 %collective-permute-start.17 = (bf16[1,2,48,768]{3,2,1,0:T(8,128)(2,1)S(1)}, bf16[1,2,48,768]{3,2,1,0:T(8,128)(2,1)S(1)}, u32[]{:S(2)}, u32[]{:S(2)}) collective-permute-start(bf16[1,2,48,768]{3,2,1,0:T(8,128)(2,1)S(1)} %get-tuple-element.92), channel_id=1, source_target_pairs={{0,4},{4,0},{8,12},{12,8},{16,20},{20,16},{24,28},{28,24},{1,5},{5... | collective-permute-start | bytes 442376 | tf_op jit(solution)/shard_map/ppermute | solution.py:414
  62.9 12.2 %collective-permute-start.9 = (bf16[1,2,48,768]{3,2,1,0:T(8,128)(2,1)S(1)}, bf16[1,2,48,768]{3,2,1,0:T(8,128)(2,1)S(1)}, u32[]{:S(2)}, u32[]{:S(2)}) collective-permute-start(bf16[1,2,48,768]{3,2,1,0:T(8,128)(2,1)S(1)} %get-tuple-element.83), channel_id=1, source_target_pairs={{0,4},{4,0},{8,12},{12,8},{16,20},{20,16},{24,28},{28,24},{1,5},{5... | collective-permute-start | bytes 442376 | tf_op jit(solution)/shard_map/ppermute | solution.py:414
  70.5 18.0 %copy-start.1 = (bf16[2,768,1536]{2,1,0:T(8,128)(2,1)S(1)}, bf16[2,768,1536]{2,1,0:T(8,128)(2,1)}, u32[]{:S(2)}) copy-start(bf16[2,768,1536]{2,1,0:T(8,128)(2,1)} %get-tuple-element.59.wkv) | copy-start | bytes 14155780
  73.1 15.4 %copy-start.4 = (bf16[2,4,768]{2,1,0:T(4,128)(2,1)S(1)}, bf16[2,4,768]{2,1,0:T(4,128)(2,1)}, u32[]{:S(2)}) copy-start(bf16[2,4,768]{2,1,0:T(4,128)(2,1)} %whead_ref.3) | copy-start | bytes 36868
  73.1 6.5 %collective-permute-start.18 = (bf16[2,48,768]{2,1,0:T(8,128)(2,1)S(1)}, bf16[2,48,768]{2,1,0:T(8,128)(2,1)S(1)}, u32[]{:S(2)}, u32[]{:S(2)}) collective-permute-start(bf16[2,48,768]{2,1,0:T(8,128)(2,1)S(1)} %get-tuple-element.94), channel_id=1, source_target_pairs={{0,1},{1,0},{2,3},{3,2},{4,5},{5,4},{6,7},{7,6},{8,9},{9,8},{10,11... | collective-permute-start | bytes 442376 | tf_op jit(solution)/shard_map/ppermute | solution.py:452
  73.2 10.0 %collective-permute-start.19 = (bf16[2,48,768]{2,1,0:T(8,128)(2,1)S(1)}, bf16[2,48,768]{2,1,0:T(8,128)(2,1)S(1)}, u32[]{:S(2)}, u32[]{:S(2)}) collective-permute-start(bf16[2,48,768]{2,1,0:T(8,128)(2,1)S(1)} %get-tuple-element.95), channel_id=1, source_target_pairs={{0,2},{1,3},{2,0},{3,1},{4,6},{5,7},{6,4},{7,5},{8,10},{9,11},{10,... | collective-permute-start | bytes 442376 | tf_op jit(solution)/shard_map/ppermute | solution.py:452
  74.8 9.1 %collective-permute-start.20 = (bf16[2,48,768]{2,1,0:T(8,128)(2,1)S(1)}, bf16[2,48,768]{2,1,0:T(8,128)(2,1)S(1)}, u32[]{:S(2)}, u32[]{:S(2)}) collective-permute-start(bf16[2,48,768]{2,1,0:T(8,128)(2,1)S(1)} %get-tuple-element.96), channel_id=1, source_target_pairs={{0,3},{1,2},{2,1},{3,0},{4,7},{5,6},{6,5},{7,4},{8,11},{9,10},{10,... | collective-permute-start | bytes 442376 | tf_op jit(solution)/shard_map/ppermute | solution.py:452
  77.7 7.7 %collective-permute-start.10 = (bf16[2,48,768]{2,1,0:T(8,128)(2,1)S(1)}, bf16[2,48,768]{2,1,0:T(8,128)(2,1)S(1)}, u32[]{:S(2)}, u32[]{:S(2)}) collective-permute-start(bf16[2,48,768]{2,1,0:T(8,128)(2,1)S(1)} %get-tuple-element.85), channel_id=1, source_target_pairs={{0,1},{1,0},{2,3},{3,2},{4,5},{5,4},{6,7},{7,6},{8,9},{9,8},{10,11... | collective-permute-start | bytes 442376 | tf_op jit(solution)/shard_map/ppermute | solution.py:452
  78.1 8.2 %collective-permute-start.11 = (bf16[2,48,768]{2,1,0:T(8,128)(2,1)S(1)}, bf16[2,48,768]{2,1,0:T(8,128)(2,1)S(1)}, u32[]{:S(2)}, u32[]{:S(2)}) collective-permute-start(bf16[2,48,768]{2,1,0:T(8,128)(2,1)S(1)} %get-tuple-element.86), channel_id=1, source_target_pairs={{0,2},{1,3},{2,0},{3,1},{4,6},{5,7},{6,4},{7,5},{8,10},{9,11},{10,... | collective-permute-start | bytes 442376 | tf_op jit(solution)/shard_map/ppermute | solution.py:452
  79.6 8.9 %collective-permute-start.12 = (bf16[2,48,768]{2,1,0:T(8,128)(2,1)S(1)}, bf16[2,48,768]{2,1,0:T(8,128)(2,1)S(1)}, u32[]{:S(2)}, u32[]{:S(2)}) collective-permute-start(bf16[2,48,768]{2,1,0:T(8,128)(2,1)S(1)} %get-tuple-element.87), channel_id=1, source_target_pairs={{0,3},{1,2},{2,1},{3,0},{4,7},{5,6},{6,5},{7,4},{8,11},{9,10},{10,... | collective-permute-start | bytes 442376 | tf_op jit(solution)/shard_map/ppermute | solution.py:452
  83.2 18.2 %collective-permute-start.21 = (bf16[2,96,768]{2,1,0:T(8,128)(2,1)S(1)}, bf16[2,96,768]{2,1,0:T(8,128)(2,1)S(1)}, u32[]{:S(2)}, u32[]{:S(2)}) collective-permute-start(bf16[2,96,768]{2,1,0:T(8,128)(2,1)S(1)} %get-tuple-element.98), channel_id=1, source_target_pairs={{0,1},{1,0},{2,3},{3,2},{4,5},{5,4},{6,7},{7,6},{8,9},{9,8},{10,11... | collective-permute-start | bytes 884744 | tf_op jit(solution)/shard_map/ppermute | solution.py:452
  83.9 17.5 %collective-permute-start.22 = (bf16[2,96,768]{2,1,0:T(8,128)(2,1)S(1)}, bf16[2,96,768]{2,1,0:T(8,128)(2,1)S(1)}, u32[]{:S(2)}, u32[]{:S(2)}) collective-permute-start(bf16[2,96,768]{2,1,0:T(8,128)(2,1)S(1)} %get-tuple-element.99), channel_id=1, source_target_pairs={{0,2},{1,3},{2,0},{3,1},{4,6},{5,7},{6,4},{7,5},{8,10},{9,11},{10,... | collective-permute-start | bytes 884744 | tf_op jit(solution)/shard_map/ppermute | solution.py:452
  85.4 16.0 %collective-permute-start.23 = (bf16[2,96,768]{2,1,0:T(8,128)(2,1)S(1)}, bf16[2,96,768]{2,1,0:T(8,128)(2,1)S(1)}, u32[]{:S(2)}, u32[]{:S(2)}) collective-permute-start(bf16[2,96,768]{2,1,0:T(8,128)(2,1)S(1)} %get-tuple-element.100), channel_id=1, source_target_pairs={{0,3},{1,2},{2,1},{3,0},{4,7},{5,6},{6,5},{7,4},{8,11},{9,10},{10,... | collective-permute-start | bytes 884744 | tf_op jit(solution)/shard_map/ppermute | solution.py:452
  88.5 1.7 %copy-start.3 = (bf16[2,768,768]{2,1,0:T(8,128)(2,1)S(1)}, bf16[2,768,768]{2,1,0:T(8,128)(2,1)}, u32[]{:S(2)}) copy-start(bf16[2,768,768]{2,1,0:T(8,128)(2,1)} %get-tuple-element.61.wo) | copy-start | bytes 7077892

commit v3 on v2

--- a/solution.py
+++ b/solution.py
@@ -402,9 +402,9 @@
     ]
     line = jnp.asarray(nearest, jnp.int32)[row // lanes]
 
-    weights = load(w_embed, w_query, w_keyval, w_out)
+    weights = load(w_embed, w_query, w_keyval)
     pieces, weights = lax.optimization_barrier((pieces, weights))
-    w_embed, w_query, w_keyval, w_out = weights
+    w_embed, w_query, w_keyval = weights
     *embedded, whole = embed(parts, cuts, me, w_embed, pieces)
     embedded, wants = lax.optimization_barrier((embedded, wants))
     groups = ((0,), tuple(range(1, length - 1)), (length - 1,))
@@ -436,6 +436,7 @@
             fetched[-1] += swap(group)
     slot_pair = slot_side // 2
     results = []
+    (w_out,) = load(w_out)
     for c in range(pair_dev):
         mine = jnp.logical_and(slot_side >= 0, slot_pair % pair_dev == c)
         place = jnp.where(mine, 2 * (slot_pair // pair_dev) + slot_side % 2, -1).astype(jnp.int32)
@@ -443,9 +444,8 @@
         parcels = []
         for q, step in enumerate(steps):
             wave = fetched[q : q + 1] if c == 0 else fetched
-            parcels += route(
-                lanes, parts, cap, step, groups, me, line, place, [each for g in wave for each in g]
-            )
+            sources = [each for group in wave for each in group]
+            parcels += route(lanes, parts, cap, step, groups, me, line, place, sources)
         arrived = []
         for i, parcel in enumerate(parcels):
             arrived.append(

time: 131 us -> 132 us (level)
  waiting for transfers between devices: 36.6 us -> 39.2 us
  local copies, waits for them, and re-layouts: 5.58 us -> 3.94 us
    unnamed x16, local copies, waits for them, and re-layouts: 1.7 us -> 0.05 us
    ppermute x3, waiting for transfers between devices: 2.18 us -> 3.68 us  [on_device(): lax.ppermute(piece, 'mp', xor_pairs(parts, j))]
    pallas_call x1 -> x2, Pallas kernels: 7.52 us -> 7.85 us  [load(): pl.pallas_call(load_kernel, out_shape=[jax.ShapeDtypeStruct(w.shape, w.dt...]
  transfers between devices with their start and end apart: 24 -> 24, of which waited for: 10 -> 11; matrix products, arithmetic and copies ran while one was open for 1% -> 1% of each run, Pallas kernels for 29% -> 29%
where the time goes in v3:
time: 132 us
  Pallas kernels  48.6 us (37%)
  waiting for transfers between devices  39.2 us (30%)
  starting transfers between devices  21.8 us (17%)
  blocking collectives  17 us (13%)
  local copies, waits for them, and re-layouts  3.94 us (3%)
    ppermute x6, waiting for transfers between devices, on_device(): passed[q].append(lax.ppermute(passed[q][-1], 'view', hop))  24.2 us
    pallas_call x2, Pallas kernels, decode(): pl.pallas_call(functools.partial(decode_kernel, parts, cuts), out_shape=j...  22 us
    all_to_all x1, blocking collectives, on_device(): lax.all_to_all(slotted, 'view', split_axis=0, concat_axis=0, tiled=True)  11.6 us
    pallas_call x3, Pallas kernels, route(): pl.pallas_call(functools.partial(route_kernel, lanes, parts, cap, base, c...  8.75 us
    pallas_call x2, Pallas kernels, load(): pl.pallas_call(load_kernel, out_shape=[jax.ShapeDtypeStruct(w.shape, w.dt...  7.85 us
    ppermute x6, starting transfers between devices, on_device(): passed[q].append(lax.ppermute(passed[q][-1], 'view', hop))  7.31 us
    ppermute x5, waiting for transfers between devices, swap(): lax.ppermute(picked[j], 'view', xor_pairs(count, j))  7.08 us
    pallas_call x5, Pallas kernels, pick(): pl.pallas_call(functools.partial(pick_kernel, lanes, slots, cap), out_sha...  6.97 us
  transfers between devices with their start and end apart: 24, of which 11 were waited for; matrix products, arithmetic and copies ran while one was open for 1% of the time, Pallas kernels for 29%

profile of v3, /device:TPU:0, one launch (start us, length us, event | category | flops | bytes accessed | tf_op | source)
XLA Modules:
  0.0 131.8 jit_solution(4758308429289838397)
XLA Ops:
  0.0 2.2 %constant_dynamic-slice_fusion.1 = (bf16[4,96,256]{2,1,0:T(8,128)(2,1)}, bf16[4,96,256]{2,1,0:T(8,128)(2,1)S(1)}, bf16[4,96,256]{2,1,0:T(8,128)(2,1)}, bf16[4,96,256]{2,1,0:T(8,128)(2,1)}) fusion(bf16[4,384,256]{2,1,0:T(8,128)(2,1)} %param.9, s32[]{:T(128)S(6)} %select_n.93, s32[]{:T(128)S(6)} %select_n.91, s32[]{:T(128)S(6)} %select_n.89, s32[]{:T(128)S(6)} %select_n.92), kind=kLoop, calls=%fused_computation.24 | loop fusion | bytes 1572880 | tf_op jit(solution)/shard_map/dynamic_slice | solution.py:374
  2.7 2.5 %collective-permute-start.1 = (bf16[4,96,256]{2,1,0:T(8,128)(2,1)}, bf16[4,96,256]{2,1,0:T(8,128)(2,1)}, u32[]{:S(2)}, u32[]{:S(2)}) collective-permute-start(bf16[4,96,256]{2,1,0:T(8,128)(2,1)} %get-tuple-element.108), channel_id=1, source_target_pairs={{0,2},{1,3},{2,0},{3,1},{4,6},{5,7},{6,4},{7,5},{8,10},{9,11},{10,... | collective-permute-start | bytes 589832 | tf_op jit(solution)/shard_map/ppermute | solution.py:375
  5.3 6.0 %load.2 = (bf16[1024,768]{1,0:T(8,128)(2,1)S(1)}, bf16[2,768,768]{2,1,0:T(8,128)(2,1)}, bf16[2,768,1536]{2,1,0:T(8,128)(2,1)}) custom-call(bf16[1024,768]{1,0:T(8,128)(2,1)S(1)} %copy-done, bf16[2,768,768]{2,1,0:T(8,128)(2,1)} %refs_1_.1, bf16[2,768,1536]{2,1,0:T(8,128)(2,1)} %refs_2_.1), custom_call_target="tpu_custom_call" | custom-call | tf_op jit(solution)/shard_map/load/pallas_call | solution.py:245
  11.4 3.7 %collective-permute-done.2.refs_3_ = bf16[4,96,256]{2,1,0:T(8,128)(2,1)} collective-permute-done((bf16[4,96,256]{2,1,0:T(8,128)(2,1)}, bf16[4,96,256]{2,1,0:T(8,128)(2,1)}, u32[]{:S(2)}, u32[]{:S(2)}) %collective-permute-start.2) | collective-permute-done | bytes 196640 | tf_op jit(solution)/shard_map/ppermute | solution.py:375
  15.7 1.6 %collective-permute-start.3 = (s32[16]{0:T(128)S(1)}, s32[16]{0:T(128)S(1)}, u32[]{:S(2)}, u32[]{:S(2)}) collective-permute-start(s32[16]{0:T(128)S(1)} %get-tuple-element.110), channel_id=1, source_target_pairs={{0,4},{4,0},{8,12},{12,8},{16,20},{20,16},{24,28},{28,24},{1,5},{5... | collective-permute-start | bytes 200 | tf_op jit(solution)/shard_map/ppermute | solution.py:394
  17.3 3.0 %embed.1 = (bf16[4,48,768]{2,1,0:T(8,128)(2,1)S(1)}, bf16[4,48,768]{2,1,0:T(8,128)(2,1)S(1)}, bf16[4,96,768]{2,1,0:T(8,128)(2,1)S(1)}) custom-call(s32[2]{0:T(128)S(1)} %pad_add_fusion.me_ref, bf16[1024,768]{1,0:T(8,128)(2,1)S(1)} %get-tuple-element.58.w_vmem, bf16[4,96,256]{2,1,0:T(8,128)(2,1)S(1)} %get-tuple-element.59.refs_0_, ...), custom_call_target="tpu_custom_call" | custom-call | flops 603979776 | bytes 3145728 | tf_op jit(solution)/shard_map/embed/pallas_call | solution.py:259
  20.4 1.6 %collective-permute-start.13 = (bf16[4,48,768]{2,1,0:T(8,128)(2,1)S(1)}, bf16[4,48,768]{2,1,0:T(8,128)(2,1)S(1)}, u32[]{:S(2)}, u32[]{:S(2)}) collective-permute-start(bf16[4,48,768]{2,1,0:T(8,128)(2,1)S(1)} %get-tuple-element.84), channel_id=1, source_target_pairs={{0,8},{4,12},{8,24},{12,28},{24,16},{28,20},{16,0},{20,4},{1,9},{5... | collective-permute-start | bytes 884744 | tf_op jit(solution)/shard_map/ppermute | solution.py:422
  21.9 2.6 %collective-permute-start.4 = (bf16[4,48,768]{2,1,0:T(8,128)(2,1)S(1)}, bf16[4,48,768]{2,1,0:T(8,128)(2,1)S(1)}, u32[]{:S(2)}, u32[]{:S(2)}) collective-permute-start(bf16[4,48,768]{2,1,0:T(8,128)(2,1)S(1)} %get-tuple-element.65), channel_id=1, source_target_pairs={{0,8},{4,12},{8,24},{12,28},{24,16},{28,20},{16,0},{20,4},{1,9},{5... | collective-permute-start | bytes 884744 | tf_op jit(solution)/shard_map/ppermute | solution.py:422
  24.5 6.6 %collective-permute-done.13.refs_0_ = bf16[4,48,768]{2,1,0:T(8,128)(2,1)S(1)} collective-permute-done((bf16[4,48,768]{2,1,0:T(8,128)(2,1)S(1)}, bf16[4,48,768]{2,1,0:T(8,128)(2,1)S(1)}, u32[]{:S(2)}, u32[]{:S(2)}) %collective-permute-start.13) | collective-permute-done | bytes 294944 | tf_op jit(solution)/shard_map/ppermute | solution.py:422
  32.6 1.5 %pick.5 = (bf16[1,2,96,768]{3,2,1,0:T(8,128)(2,1)S(1)}, bf16[1,2,96,768]{3,2,1,0:T(8,128)(2,1)S(1)}) custom-call(s32[2]{0:T(128)S(1)} %pad_add_fusion.me_ref, s32[4]{0:T(128)S(1)} %fusion.7.line_ref, s32[32]{0:T(128)S(1)} %pad_add_fusion.1.want_ref, bf16[4,96,768]{2,1,0:T(8,128)(2,1)S(1)} %get-tuple-element.67.refs_0_), custom_call_target="tpu_custom_call" | custom-call | bytes 1179648 | tf_op jit(solution)/shard_map/pick/pallas_call | solution.py:285
  34.1 3.3 %collective-permute-done.4.refs_0_ = bf16[4,48,768]{2,1,0:T(8,128)(2,1)S(1)} collective-permute-done((bf16[4,48,768]{2,1,0:T(8,128)(2,1)S(1)}, bf16[4,48,768]{2,1,0:T(8,128)(2,1)S(1)}, u32[]{:S(2)}, u32[]{:S(2)}) %collective-permute-start.4) | collective-permute-done | bytes 294944 | tf_op jit(solution)/shard_map/ppermute | solution.py:422
  38.8 5.0 %collective-permute-done.14.refs_1_ = bf16[4,48,768]{2,1,0:T(8,128)(2,1)S(1)} collective-permute-done((bf16[4,48,768]{2,1,0:T(8,128)(2,1)S(1)}, bf16[4,48,768]{2,1,0:T(8,128)(2,1)S(1)}, u32[]{:S(2)}, u32[]{:S(2)}) %collective-permute-start.14) | collective-permute-done | bytes 294944 | tf_op jit(solution)/shard_map/ppermute | solution.py:422
  44.6 5.5 %collective-permute-done.5.refs_1_ = bf16[4,48,768]{2,1,0:T(8,128)(2,1)S(1)} collective-permute-done((bf16[4,48,768]{2,1,0:T(8,128)(2,1)S(1)}, bf16[4,48,768]{2,1,0:T(8,128)(2,1)S(1)}, u32[]{:S(2)}, u32[]{:S(2)}) %collective-permute-start.5) | collective-permute-done | bytes 294944 | tf_op jit(solution)/shard_map/ppermute | solution.py:422
  50.9 1.6 %pick.8 = (bf16[2,2,48,768]{3,2,1,0:T(8,128)(2,1)S(1)}, bf16[2,2,48,768]{3,2,1,0:T(8,128)(2,1)S(1)}) custom-call(s32[2]{0:T(128)S(1)} %pad_add_fusion.me_ref, s32[4]{0:T(128)S(1)} %fusion.7.line_ref, s32[32]{0:T(128)S(1)} %pad_add_fusion.1.want_ref, bf16[4,48,768]{2,1,0:T(8,128)(2,1)S(1)} %collective-permute-done.13.refs_0_, ...), custom_call_target="tpu_custom_call" | custom-call | bytes 1179648 | tf_op jit(solution)/shard_map/pick/pallas_call | solution.py:285
  53.1 1.6 %pick.6 = (bf16[2,2,48,768]{3,2,1,0:T(8,128)(2,1)S(1)}, bf16[2,2,48,768]{3,2,1,0:T(8,128)(2,1)S(1)}) custom-call(s32[2]{0:T(128)S(1)} %pad_add_fusion.me_ref, s32[4]{0:T(128)S(1)} %fusion.7.line_ref, s32[32]{0:T(128)S(1)} %pad_add_fusion.1.want_ref, bf16[4,48,768]{2,1,0:T(8,128)(2,1)S(1)} %collective-permute-done.4.refs_0_, ...), custom_call_target="tpu_custom_call" | custom-call | bytes 1179648 | tf_op jit(solution)/shard_map/pick/pallas_call | solution.py:285
  54.8 1.5 %collective-permute-start.7 = (bf16[2,2,48,768]{3,2,1,0:T(8,128)(2,1)S(1)}, bf16[2,2,48,768]{3,2,1,0:T(8,128)(2,1)S(1)}, u32[]{:S(2)}, u32[]{:S(2)}) collective-permute-start(bf16[2,2,48,768]{3,2,1,0:T(8,128)(2,1)S(1)} %get-tuple-element.77), channel_id=1, source_target_pairs={{0,4},{4,0},{8,12},{12,8},{16,20},{20,16},{24,28},{28,24},{1,5},{5... | collective-permute-start | bytes 884744 | tf_op jit(solution)/shard_map/ppermute | solution.py:414
  56.4 1.1 pick.9
  58.1 3.6 %collective-permute-done.8.refs_0_ = bf16[4,48,768]{2,1,0:T(8,128)(2,1)S(1)} collective-permute-done((bf16[4,48,768]{2,1,0:T(8,128)(2,1)S(1)}, bf16[4,48,768]{2,1,0:T(8,128)(2,1)S(1)}, u32[]{:S(2)}, u32[]{:S(2)}) %collective-permute-start.8) | collective-permute-done | bytes 294944 | tf_op jit(solution)/shard_map/ppermute | solution.py:422
  63.4 7.1 %collective-permute-done.17.refs_5_.refs_11_ = bf16[1,2,48,768]{3,2,1,0:T(8,128)(2,1)S(1)} collective-permute-done((bf16[1,2,48,768]{3,2,1,0:T(8,128)(2,1)S(1)}, bf16[1,2,48,768]{3,2,1,0:T(8,128)(2,1)S(1)}, u32[]{:S(2)}, u32[]{:S(2)}) %collective-permute-start.17) | collective-permute-done | bytes 147488 | tf_op jit(solution)/shard_map/ppermute | solution.py:414
  70.5 2.6 %route.4 = (bf16[2,48,768]{2,1,0:T(8,128)(2,1)S(1)}, bf16[2,48,768]{2,1,0:T(8,128)(2,1)S(1)}, bf16[2,48,768]{2,1,0:T(8,128)(2,1)S(1)}, bf16[2,48,768]{2,1,0:T(8,128)(2,1)S(1)}) custom-call(s32[2]{0:T(128)S(1)} %pad_add_fusion.me_ref, s32[4]{0:T(128)S(1)} %fusion.7.line_ref, s32[16]{0:T(128)S(1)} %get-tuple-element.99.side_ref, ...), custom_call_target="tpu_custom_call" | custom-call | bytes 1179648 | tf_op jit(solution)/shard_map/route/pallas_call | solution.py:311
  73.2 1.8 %load.3.wo = bf16[2,768,768]{2,1,0:T(8,128)(2,1)S(1)} custom-call(bf16[2,768,768]{2,1,0:T(8,128)(2,1)} %refs_0_.3), custom_call_target="tpu_custom_call" | custom-call | tf_op jit(solution)/shard_map/load/pallas_call | solution.py:245
  75.1 1.6 %collective-permute-start.19 = (bf16[2,48,768]{2,1,0:T(8,128)(2,1)S(1)}, bf16[2,48,768]{2,1,0:T(8,128)(2,1)S(1)}, u32[]{:S(2)}, u32[]{:S(2)}) collective-permute-start(bf16[2,48,768]{2,1,0:T(8,128)(2,1)S(1)} %get-tuple-element.91), channel_id=1, source_target_pairs={{0,2},{1,3},{2,0},{3,1},{4,6},{5,7},{6,4},{7,5},{8,10},{9,11},{10,... | collective-permute-start | bytes 442376 | tf_op jit(solution)/shard_map/ppermute | solution.py:452
  76.8 2.6 %route.3 = (bf16[2,48,768]{2,1,0:T(8,128)(2,1)S(1)}, bf16[2,48,768]{2,1,0:T(8,128)(2,1)S(1)}, bf16[2,48,768]{2,1,0:T(8,128)(2,1)S(1)}, bf16[2,48,768]{2,1,0:T(8,128)(2,1)S(1)}) custom-call(s32[2]{0:T(128)S(1)} %pad_add_fusion.me_ref, s32[4]{0:T(128)S(1)} %fusion.7.line_ref, s32[16]{0:T(128)S(1)} %get-tuple-element.99.side_ref, ...), custom_call_target="tpu_custom_call" | custom-call | bytes 1179648 | tf_op jit(solution)/shard_map/route/pallas_call | solution.py:311
  80.0 1.5 %collective-permute-start.11 = (bf16[2,48,768]{2,1,0:T(8,128)(2,1)S(1)}, bf16[2,48,768]{2,1,0:T(8,128)(2,1)S(1)}, u32[]{:S(2)}, u32[]{:S(2)}) collective-permute-start(bf16[2,48,768]{2,1,0:T(8,128)(2,1)S(1)} %get-tuple-element.82), channel_id=1, source_target_pairs={{0,2},{1,3},{2,0},{3,1},{4,6},{5,7},{6,4},{7,5},{8,10},{9,11},{10,... | collective-permute-start | bytes 442376 | tf_op jit(solution)/shard_map/ppermute | solution.py:452
  81.5 3.5 %route.5 = (bf16[2,96,768]{2,1,0:T(8,128)(2,1)S(1)}, bf16[2,96,768]{2,1,0:T(8,128)(2,1)S(1)}, bf16[2,96,768]{2,1,0:T(8,128)(2,1)S(1)}, bf16[2,96,768]{2,1,0:T(8,128)(2,1)S(1)}) custom-call(s32[2]{0:T(128)S(1)} %pad_add_fusion.me_ref, s32[4]{0:T(128)S(1)} %fusion.7.line_ref, s32[16]{0:T(128)S(1)} %and_select_fusion.side_ref, ...), custom_call_target="tpu_custom_call" | custom-call | bytes 2359296 | tf_op jit(solution)/shard_map/route/pallas_call | solution.py:311
  85.8 1.5 %collective-permute-start.22 = (bf16[2,96,768]{2,1,0:T(8,128)(2,1)S(1)}, bf16[2,96,768]{2,1,0:T(8,128)(2,1)S(1)}, u32[]{:S(2)}, u32[]{:S(2)}) collective-permute-start(bf16[2,96,768]{2,1,0:T(8,128)(2,1)S(1)} %get-tuple-element.95), channel_id=1, source_target_pairs={{0,2},{1,3},{2,0},{3,1},{4,6},{5,7},{6,4},{7,5},{8,10},{9,11},{10,... | collective-permute-start | bytes 884744 | tf_op jit(solution)/shard_map/ppermute | solution.py:452
  88.2 2.2 %collective-permute-done.12.refs_3_ = bf16[2,48,768]{2,1,0:T(8,128)(2,1)S(1)} collective-permute-done((bf16[2,48,768]{2,1,0:T(8,128)(2,1)S(1)}, bf16[2,48,768]{2,1,0:T(8,128)(2,1)S(1)}, u32[]{:S(2)}, u32[]{:S(2)}) %collective-permute-start.12) | collective-permute-done | bytes 147488 | tf_op jit(solution)/shard_map/ppermute | solution.py:452
  90.4 11.2 %decode.2 = f32[2,4,384]{2,1,0:T(4,128)S(1)} custom-call(s32[2]{0:T(128)S(1)} %pad_add_fusion.me_ref, f32[2,3,768]{2,1,0:T(4,128)S(1)} %copy.24.gains_ref, bf16[2,4,768]{2,1,0:T(4,128)(2,1)S(1)} %copy-done.2, bf16[2,768,1536]{2,1,0:T(8,128)(2,1)S(1)} %bitcast.16, bf16[2,768,768]{2,1,0:T(8,128)(2,1)S(1)} %copy-done.1, bf16[2,768,768]{2,1,0:T(8,128)(2,1)S(1)} %load.3.wo, ...), custom_call_target="tpu_custom_call" | custom-call | flops 5435817984 | bytes 11796480 | tf_op jit(solution)/shard_map/decode/pallas_call | solution.py:333
  101.6 1.1 collective-permute-done.23.refs_3_
  102.7 10.8 %decode.3 = f32[2,4,384]{2,1,0:T(4,128)S(1)} custom-call(s32[2]{0:T(128)S(1)} %pad_add_fusion.me_ref, f32[2,3,768]{2,1,0:T(4,128)S(1)} %copy.24.gains_ref, bf16[2,4,768]{2,1,0:T(4,128)(2,1)S(1)} %copy-done.2, bf16[2,768,1536]{2,1,0:T(8,128)(2,1)S(1)} %bitcast.16, bf16[2,768,768]{2,1,0:T(8,128)(2,1)S(1)} %copy-done.1, bf16[2,768,768]{2,1,0:T(8,128)(2,1)S(1)} %load.3.wo, ...), custom_call_target="tpu_custom_call" | custom-call | flops 5435817984 | bytes 11796480 | tf_op jit(solution)/shard_map/decode/pallas_call | solution.py:333
  113.5 5.3 %all_gather.3 = f32[8,2,4,384]{3,2,1,0:T(4,128)S(1)} all-gather(f32[2,2,4,384]{3,2,1,0:T(4,128)S(1)} %pad_maximum_fusion.1), channel_id=1, replica_groups=mesh['view'=8,'mp'=4] {'mp'}, dimensions={0}, use_global_device_ids=true | all-gather | bytes 122880 | tf_op jit(solution)/shard_map/all_gather | solution.py:469
  119.2 11.6 %all_to_all.5 = f32[8,2,1664]{2,1,0:T(2,128)S(1)} all-to-all(f32[8,2,1664]{2,1,0:T(2,128)S(1)} %reshape.110), channel_id=1, replica_groups=mesh['view'=8,'mp'=4] {'view'}, dimensions={0} | all-to-all | bytes 212992 | tf_op jit(solution)/shard_map/all_to_all | solution.py:473
  (71 shorter events, 12.5 us)
Async XLA Ops:
  0.0 5.3 %copy-start = (bf16[1024,768]{1,0:T(8,128)(2,1)S(1)}, bf16[1024,768]{1,0:T(8,128)(2,1)}, u32[]{:S(2)}) copy-start(bf16[1024,768]{1,0:T(8,128)(2,1)} %refs_0_.2) | copy-start | bytes 4718596
  2.2 9.2 %collective-permute-start = (bf16[4,96,256]{2,1,0:T(8,128)(2,1)}, bf16[4,96,256]{2,1,0:T(8,128)(2,1)S(1)}, u32[]{:S(2)}, u32[]{:S(2)}) collective-permute-start(bf16[4,96,256]{2,1,0:T(8,128)(2,1)} %get-tuple-element.107), channel_id=1, source_target_pairs={{0,1},{1,0},{2,3},{3,2},{4,5},{5,4},{6,7},{7,6},{8,9},{9,8},{10,11... | collective-permute-start | bytes 589832 | tf_op jit(solution)/shard_map/ppermute | solution.py:375
  2.7 8.7 %collective-permute-start.1 = (bf16[4,96,256]{2,1,0:T(8,128)(2,1)}, bf16[4,96,256]{2,1,0:T(8,128)(2,1)}, u32[]{:S(2)}, u32[]{:S(2)}) collective-permute-start(bf16[4,96,256]{2,1,0:T(8,128)(2,1)} %get-tuple-element.108), channel_id=1, source_target_pairs={{0,2},{1,3},{2,0},{3,1},{4,6},{5,7},{6,4},{7,5},{8,10},{9,11},{10,... | collective-permute-start | bytes 589832 | tf_op jit(solution)/shard_map/ppermute | solution.py:375
  5.1 9.9 %collective-permute-start.2 = (bf16[4,96,256]{2,1,0:T(8,128)(2,1)}, bf16[4,96,256]{2,1,0:T(8,128)(2,1)}, u32[]{:S(2)}, u32[]{:S(2)}) collective-permute-start(bf16[4,96,256]{2,1,0:T(8,128)(2,1)} %get-tuple-element.105), channel_id=1, source_target_pairs={{0,3},{1,2},{2,1},{3,0},{4,7},{5,6},{6,5},{7,4},{8,11},{9,10},{10,... | collective-permute-start | bytes 589832 | tf_op jit(solution)/shard_map/ppermute | solution.py:375
  5.3 9.8 %copy-start.4 = (s32[8,2]{0,1:T(2,128)S(1)}, s32[8,2]{0,1:T(2,128)}, u32[]{:S(2)}) copy-start(s32[8,2]{0,1:T(2,128)} %param.10) | copy-start | bytes 196
  15.7 4.6 %collective-permute-start.3 = (s32[16]{0:T(128)S(1)}, s32[16]{0:T(128)S(1)}, u32[]{:S(2)}, u32[]{:S(2)}) collective-permute-start(s32[16]{0:T(128)S(1)} %get-tuple-element.110), channel_id=1, source_target_pairs={{0,4},{4,0},{8,12},{12,8},{16,20},{20,16},{24,28},{28,24},{1,5},{5... | collective-permute-start | bytes 200 | tf_op jit(solution)/shard_map/ppermute | solution.py:394
  20.4 10.8 %collective-permute-start.13 = (bf16[4,48,768]{2,1,0:T(8,128)(2,1)S(1)}, bf16[4,48,768]{2,1,0:T(8,128)(2,1)S(1)}, u32[]{:S(2)}, u32[]{:S(2)}) collective-permute-start(bf16[4,48,768]{2,1,0:T(8,128)(2,1)S(1)} %get-tuple-element.84), channel_id=1, source_target_pairs={{0,8},{4,12},{8,24},{12,28},{24,16},{28,20},{16,0},{20,4},{1,9},{5... | collective-permute-start | bytes 884744 | tf_op jit(solution)/shard_map/ppermute | solution.py:422
  21.9 15.5 %collective-permute-start.4 = (bf16[4,48,768]{2,1,0:T(8,128)(2,1)S(1)}, bf16[4,48,768]{2,1,0:T(8,128)(2,1)S(1)}, u32[]{:S(2)}, u32[]{:S(2)}) collective-permute-start(bf16[4,48,768]{2,1,0:T(8,128)(2,1)S(1)} %get-tuple-element.65), channel_id=1, source_target_pairs={{0,8},{4,12},{8,24},{12,28},{24,16},{28,20},{16,0},{20,4},{1,9},{5... | collective-permute-start | bytes 884744 | tf_op jit(solution)/shard_map/ppermute | solution.py:422
  31.1 12.6 %collective-permute-start.14 = (bf16[4,48,768]{2,1,0:T(8,128)(2,1)S(1)}, bf16[4,48,768]{2,1,0:T(8,128)(2,1)S(1)}, u32[]{:S(2)}, u32[]{:S(2)}) collective-permute-start(bf16[4,48,768]{2,1,0:T(8,128)(2,1)S(1)} %collective-permute-done.13.refs_0_), channel_id=1, source_target_pairs={{0,8},{4,12},{8,24},{12,28},{24,16},{28,20},{16,0},{20,4},{1,9},{5... | collective-permute-start | bytes 884744 | tf_op jit(solution)/shard_map/ppermute | solution.py:422
  37.5 12.6 %collective-permute-start.5 = (bf16[4,48,768]{2,1,0:T(8,128)(2,1)S(1)}, bf16[4,48,768]{2,1,0:T(8,128)(2,1)S(1)}, u32[]{:S(2)}, u32[]{:S(2)}) collective-permute-start(bf16[4,48,768]{2,1,0:T(8,128)(2,1)S(1)} %collective-permute-done.4.refs_0_), channel_id=1, source_target_pairs={{0,8},{4,12},{8,24},{12,28},{24,16},{28,20},{16,0},{20,4},{1,9},{5... | collective-permute-start | bytes 884744 | tf_op jit(solution)/shard_map/ppermute | solution.py:422
  38.2 11.9 %collective-permute-start.6 = (bf16[1,2,96,768]{3,2,1,0:T(8,128)(2,1)S(1)}, bf16[1,2,96,768]{3,2,1,0:T(8,128)(2,1)S(1)}, u32[]{:S(2)}, u32[]{:S(2)}) collective-permute-start(bf16[1,2,96,768]{3,2,1,0:T(8,128)(2,1)S(1)} %get-tuple-element.72), channel_id=1, source_target_pairs={{0,4},{4,0},{8,12},{12,8},{16,20},{20,16},{24,28},{28,24},{1,5},{5... | collective-permute-start | bytes 884744 | tf_op jit(solution)/shard_map/ppermute | solution.py:414
  43.8 12.6 %collective-permute-start.16 = (bf16[4,48,768]{2,1,0:T(8,128)(2,1)S(1)}, bf16[4,48,768]{2,1,0:T(8,128)(2,1)S(1)}, u32[]{:S(2)}, u32[]{:S(2)}) collective-permute-start(bf16[4,48,768]{2,1,0:T(8,128)(2,1)S(1)} %collective-permute-done.14.refs_1_), channel_id=1, source_target_pairs={{0,8},{4,12},{8,24},{12,28},{24,16},{28,20},{16,0},{20,4},{1,9},{5... | collective-permute-start | bytes 884744 | tf_op jit(solution)/shard_map/ppermute | solution.py:422
  50.1 11.7 %collective-permute-start.8 = (bf16[4,48,768]{2,1,0:T(8,128)(2,1)S(1)}, bf16[4,48,768]{2,1,0:T(8,128)(2,1)S(1)}, u32[]{:S(2)}, u32[]{:S(2)}) collective-permute-start(bf16[4,48,768]{2,1,0:T(8,128)(2,1)S(1)} %collective-permute-done.5.refs_1_), channel_id=1, source_target_pairs={{0,8},{4,12},{8,24},{12,28},{24,16},{28,20},{16,0},{20,4},{1,9},{5... | collective-permute-start | bytes 884744 | tf_op jit(solution)/shard_map/ppermute | solution.py:422
  52.5 10.9 %collective-permute-start.15 = (bf16[2,2,48,768]{3,2,1,0:T(8,128)(2,1)S(1)}, bf16[2,2,48,768]{3,2,1,0:T(8,128)(2,1)S(1)}, u32[]{:S(2)}, u32[]{:S(2)}) collective-permute-start(bf16[2,2,48,768]{3,2,1,0:T(8,128)(2,1)S(1)} %get-tuple-element.86), channel_id=1, source_target_pairs={{0,4},{4,0},{8,12},{12,8},{16,20},{20,16},{24,28},{28,24},{1,5},{5... | collective-permute-start | bytes 884744 | tf_op jit(solution)/shard_map/ppermute | solution.py:414
  54.8 22.1 %collective-permute-start.7 = (bf16[2,2,48,768]{3,2,1,0:T(8,128)(2,1)S(1)}, bf16[2,2,48,768]{3,2,1,0:T(8,128)(2,1)S(1)}, u32[]{:S(2)}, u32[]{:S(2)}) collective-permute-start(bf16[2,2,48,768]{3,2,1,0:T(8,128)(2,1)S(1)} %get-tuple-element.77), channel_id=1, source_target_pairs={{0,4},{4,0},{8,12},{12,8},{16,20},{20,16},{24,28},{28,24},{1,5},{5... | collective-permute-start | bytes 884744 | tf_op jit(solution)/shard_map/ppermute | solution.py:414
  57.5 13.0 %collective-permute-start.17 = (bf16[1,2,48,768]{3,2,1,0:T(8,128)(2,1)S(1)}, bf16[1,2,48,768]{3,2,1,0:T(8,128)(2,1)S(1)}, u32[]{:S(2)}, u32[]{:S(2)}) collective-permute-start(bf16[1,2,48,768]{3,2,1,0:T(8,128)(2,1)S(1)} %get-tuple-element.88), channel_id=1, source_target_pairs={{0,4},{4,0},{8,12},{12,8},{16,20},{20,16},{24,28},{28,24},{1,5},{5... | collective-permute-start | bytes 442376 | tf_op jit(solution)/shard_map/ppermute | solution.py:414
  62.9 14.0 %collective-permute-start.9 = (bf16[1,2,48,768]{3,2,1,0:T(8,128)(2,1)S(1)}, bf16[1,2,48,768]{3,2,1,0:T(8,128)(2,1)S(1)}, u32[]{:S(2)}, u32[]{:S(2)}) collective-permute-start(bf16[1,2,48,768]{3,2,1,0:T(8,128)(2,1)S(1)} %get-tuple-element.79), channel_id=1, source_target_pairs={{0,4},{4,0},{8,12},{12,8},{16,20},{20,16},{24,28},{28,24},{1,5},{5... | collective-permute-start | bytes 442376 | tf_op jit(solution)/shard_map/ppermute | solution.py:414
  73.1 1.9 %copy-start.3 = (f32[2,3,768]{2,0,1:T(2,128)S(1)}, f32[2,3,768]{2,0,1:T(2,128)}, u32[]{:S(2)}) copy-start(f32[2,3,768]{2,0,1:T(2,128)} %param.16) | copy-start | bytes 55300
  73.1 17.3 %slice-start = ((s8[4718592]{0:T(1024)(128)(4,1)}), s8[4194304]{0:T(1024)(128)(4,1)S(1)}, s32[]{:S(2)}) async-start(s8[4718592]{0:T(1024)(128)(4,1)} %bitcast.15), calls=%async_computation.1 | async-start | bytes 8388608
  73.1 17.3 %slice-start.1 = ((s8[4718592]{0:T(1024)(128)(4,1)}), s8[524288]{0:T(1024)(128)(4,1)S(1)}, s32[]{:S(2)}) async-start(s8[4718592]{0:T(1024)(128)(4,1)} %bitcast.15), calls=%async_computation.2 | async-start | bytes 1048576
  73.1 8.3 %collective-permute-start.18 = (bf16[2,48,768]{2,1,0:T(8,128)(2,1)S(1)}, bf16[2,48,768]{2,1,0:T(8,128)(2,1)S(1)}, u32[]{:S(2)}, u32[]{:S(2)}) collective-permute-start(bf16[2,48,768]{2,1,0:T(8,128)(2,1)S(1)} %get-tuple-element.90), channel_id=1, source_target_pairs={{0,1},{1,0},{2,3},{3,2},{4,5},{5,4},{6,7},{7,6},{8,9},{9,8},{10,11... | collective-permute-start | bytes 442376 | tf_op jit(solution)/shard_map/ppermute | solution.py:452
  75.0 15.3 %copy-start.1 = (bf16[2,768,768]{2,1,0:T(8,128)(2,1)S(1)}, bf16[2,768,768]{2,1,0:T(8,128)(2,1)}, u32[]{:S(2)}) copy-start(bf16[2,768,768]{2,1,0:T(8,128)(2,1)} %get-tuple-element.57.wq) | copy-start | bytes 7077892
  75.0 15.3 %copy-start.2 = (bf16[2,4,768]{2,1,0:T(4,128)(2,1)S(1)}, bf16[2,4,768]{2,1,0:T(4,128)(2,1)}, u32[]{:S(2)}) copy-start(bf16[2,4,768]{2,1,0:T(4,128)(2,1)} %whead_ref.3) | copy-start | bytes 36868
  75.1 10.0 %collective-permute-start.19 = (bf16[2,48,768]{2,1,0:T(8,128)(2,1)S(1)}, bf16[2,48,768]{2,1,0:T(8,128)(2,1)S(1)}, u32[]{:S(2)}, u32[]{:S(2)}) collective-permute-start(bf16[2,48,768]{2,1,0:T(8,128)(2,1)S(1)} %get-tuple-element.91), channel_id=1, source_target_pairs={{0,2},{1,3},{2,0},{3,1},{4,6},{5,7},{6,4},{7,5},{8,10},{9,11},{10,... | collective-permute-start | bytes 442376 | tf_op jit(solution)/shard_map/ppermute | solution.py:452
  76.6 9.1 %collective-permute-start.20 = (bf16[2,48,768]{2,1,0:T(8,128)(2,1)S(1)}, bf16[2,48,768]{2,1,0:T(8,128)(2,1)S(1)}, u32[]{:S(2)}, u32[]{:S(2)}) collective-permute-start(bf16[2,48,768]{2,1,0:T(8,128)(2,1)S(1)} %get-tuple-element.92), channel_id=1, source_target_pairs={{0,3},{1,2},{2,1},{3,0},{4,7},{5,6},{6,5},{7,4},{8,11},{9,10},{10,... | collective-permute-start | bytes 442376 | tf_op jit(solution)/shard_map/ppermute | solution.py:452
  79.5 7.8 %collective-permute-start.10 = (bf16[2,48,768]{2,1,0:T(8,128)(2,1)S(1)}, bf16[2,48,768]{2,1,0:T(8,128)(2,1)S(1)}, u32[]{:S(2)}, u32[]{:S(2)}) collective-permute-start(bf16[2,48,768]{2,1,0:T(8,128)(2,1)S(1)} %get-tuple-element.81), channel_id=1, source_target_pairs={{0,1},{1,0},{2,3},{3,2},{4,5},{5,4},{6,7},{7,6},{8,9},{9,8},{10,11... | collective-permute-start | bytes 442376 | tf_op jit(solution)/shard_map/ppermute | solution.py:452
  80.0 8.2 %collective-permute-start.11 = (bf16[2,48,768]{2,1,0:T(8,128)(2,1)S(1)}, bf16[2,48,768]{2,1,0:T(8,128)(2,1)S(1)}, u32[]{:S(2)}, u32[]{:S(2)}) collective-permute-start(bf16[2,48,768]{2,1,0:T(8,128)(2,1)S(1)} %get-tuple-element.82), channel_id=1, source_target_pairs={{0,2},{1,3},{2,0},{3,1},{4,6},{5,7},{6,4},{7,5},{8,10},{9,11},{10,... | collective-permute-start | bytes 442376 | tf_op jit(solution)/shard_map/ppermute | solution.py:452
  81.5 8.9 %collective-permute-start.12 = (bf16[2,48,768]{2,1,0:T(8,128)(2,1)S(1)}, bf16[2,48,768]{2,1,0:T(8,128)(2,1)S(1)}, u32[]{:S(2)}, u32[]{:S(2)}) collective-permute-start(bf16[2,48,768]{2,1,0:T(8,128)(2,1)S(1)} %get-tuple-element.83), channel_id=1, source_target_pairs={{0,3},{1,2},{2,1},{3,0},{4,7},{5,6},{6,5},{7,4},{8,11},{9,10},{10,... | collective-permute-start | bytes 442376 | tf_op jit(solution)/shard_map/ppermute | solution.py:452
  85.0 16.5 %collective-permute-start.21 = (bf16[2,96,768]{2,1,0:T(8,128)(2,1)S(1)}, bf16[2,96,768]{2,1,0:T(8,128)(2,1)S(1)}, u32[]{:S(2)}, u32[]{:S(2)}) collective-permute-start(bf16[2,96,768]{2,1,0:T(8,128)(2,1)S(1)} %get-tuple-element.94), channel_id=1, source_target_pairs={{0,1},{1,0},{2,3},{3,2},{4,5},{5,4},{6,7},{7,6},{8,9},{9,8},{10,11... | collective-permute-start | bytes 884744 | tf_op jit(solution)/shard_map/ppermute | solution.py:452
  85.8 15.8 %collective-permute-start.22 = (bf16[2,96,768]{2,1,0:T(8,128)(2,1)S(1)}, bf16[2,96,768]{2,1,0:T(8,128)(2,1)S(1)}, u32[]{:S(2)}, u32[]{:S(2)}) collective-permute-start(bf16[2,96,768]{2,1,0:T(8,128)(2,1)S(1)} %get-tuple-element.95), channel_id=1, source_target_pairs={{0,2},{1,3},{2,0},{3,1},{4,6},{5,7},{6,4},{7,5},{8,10},{9,11},{10,... | collective-permute-start | bytes 884744 | tf_op jit(solution)/shard_map/ppermute | solution.py:452
  87.2 15.5 %collective-permute-start.23 = (bf16[2,96,768]{2,1,0:T(8,128)(2,1)S(1)}, bf16[2,96,768]{2,1,0:T(8,128)(2,1)S(1)}, u32[]{:S(2)}, u32[]{:S(2)}) collective-permute-start(bf16[2,96,768]{2,1,0:T(8,128)(2,1)S(1)} %get-tuple-element.96), channel_id=1, source_target_pairs={{0,3},{1,2},{2,1},{3,0},{4,7},{5,6},{6,5},{7,4},{8,11},{9,10},{10,... | collective-permute-start | bytes 884744 | tf_op jit(solution)/shard_map/ppermute | solution.py:452

commit v4 on v3

--- a/solution.py
+++ b/solution.py
@@ -402,11 +402,9 @@
     ]
     line = jnp.asarray(nearest, jnp.int32)[row // lanes]
 
-    weights = load(w_embed, w_query, w_keyval)
-    pieces, weights = lax.optimization_barrier((pieces, weights))
-    w_embed, w_query, w_keyval = weights
+    (w_embed,) = load(w_embed)
+    pieces, w_embed, wants, line = lax.optimization_barrier((pieces, w_embed, wants, line))
     *embedded, whole = embed(parts, cuts, me, w_embed, pieces)
-    embedded, wants = lax.optimization_barrier((embedded, wants))
     groups = ((0,), tuple(range(1, length - 1)), (length - 1,))
 
     def swap(picked):

time: 132 us -> 130 us (0.985)
  Pallas kernels: 48.6 us -> 42 us
  starting transfers between devices: 21.8 us -> 27.6 us
  waiting for transfers between devices: 39.2 us -> 36.7 us
    pallas_call x2, Pallas kernels: 7.85 us -> 1.94 us  [load(): pl.pallas_call(load_kernel, out_shape=[jax.ShapeDtypeStruct(w.shape, w.dt...]
    ppermute x5, starting transfers between devices: 3.83 us -> 7.32 us  [swap(): lax.ppermute(picked[j], 'view', xor_pairs(count, j))]
    ppermute x6, waiting for transfers between devices: 24.2 us -> 21.2 us  [on_device(): passed[q].append(lax.ppermute(passed[q][-1], 'view', hop))]
    ppermute x6, starting transfers between devices: 7.31 us -> 9.17 us  [on_device(): passed[q].append(lax.ppermute(passed[q][-1], 'view', hop))]
    ppermute x1, waiting for transfers between devices: 0.01 us -> 1.69 us  [on_device(): lax.ppermute(wanted, 'view', xor_pairs(count, j))]
  transfers between devices with their start and end apart: 24 -> 24, of which waited for: 11 -> 13; matrix products, arithmetic and copies ran while one was open for 1% -> 2% of each run, Pallas kernels for 29% -> 22%
where the time goes in v4:
time: 130 us; the launch traced here: 129 us
  Pallas kernels  42 us (32%)
  waiting for transfers between devices  36.7 us (28%)
  starting transfers between devices  27.6 us (21%)
  blocking collectives  17.9 us (14%)
  local copies, waits for them, and re-layouts  3.83 us (3%)
    pallas_call x2, Pallas kernels, decode(): pl.pallas_call(functools.partial(decode_kernel, parts, cuts), out_shape=j...  22.3 us
    ppermute x6, waiting for transfers between devices, on_device(): passed[q].append(lax.ppermute(passed[q][-1], 'view', hop))  21.2 us
    all_to_all x1, blocking collectives, on_device(): lax.all_to_all(slotted, 'view', split_axis=0, concat_axis=0, tiled=True)  12.6 us
    ppermute x6, starting transfers between devices, on_device(): passed[q].append(lax.ppermute(passed[q][-1], 'view', hop))  9.17 us
    pallas_call x3, Pallas kernels, route(): pl.pallas_call(functools.partial(route_kernel, lanes, parts, cap, base, c...  8.75 us
    ppermute x5, starting transfers between devices, swap(): lax.ppermute(picked[j], 'view', xor_pairs(count, j))  7.32 us
    pallas_call x5, Pallas kernels, pick(): pl.pallas_call(functools.partial(pick_kernel, lanes, slots, cap), out_sha...  6.97 us
    ppermute x5, waiting for transfers between devices, swap(): lax.ppermute(picked[j], 'view', xor_pairs(count, j))  6.41 us
  transfers between devices with their start and end apart: 24, of which 13 were waited for; matrix products, arithmetic and copies ran while one was open for 2% of the time, Pallas kernels for 22%

profile of v4, /device:TPU:0, one launch (start us, length us, event | category | flops | bytes accessed | tf_op | source)
XLA Modules:
  0.0 129.4 jit_solution(8790560512749222747)
XLA Ops:
  1.4 2.5 %collective-permute-start.2 = (bf16[4,96,256]{2,1,0:T(8,128)(2,1)S(1)}, bf16[4,96,256]{2,1,0:T(8,128)(2,1)S(1)}, u32[]{:S(2)}, u32[]{:S(2)}) collective-permute-start(bf16[4,96,256]{2,1,0:T(8,128)(2,1)S(1)} %get-tuple-element.93), channel_id=1, source_target_pairs={{0,3},{1,2},{2,1},{3,0},{4,7},{5,6},{6,5},{7,4},{8,11},{9,10},{10,... | collective-permute-start | bytes 589832 | tf_op jit(solution)/shard_map/ppermute | solution.py:375
  6.9 1.8 %collective-permute-start.3 = (s32[16]{0:T(128)S(1)}, s32[16]{0:T(128)S(1)}, u32[]{:S(2)}, u32[]{:S(2)}) collective-permute-start(s32[16]{0:T(128)S(1)} %get-tuple-element.98), channel_id=1, source_target_pairs={{0,4},{4,0},{8,12},{12,8},{16,20},{20,16},{24,28},{28,24},{1,5},{5... | collective-permute-start | bytes 200 | tf_op jit(solution)/shard_map/ppermute | solution.py:394
  8.9 1.7 %collective-permute-done.3 = s32[16]{0:T(128)S(1)} collective-permute-done((s32[16]{0:T(128)S(1)}, s32[16]{0:T(128)S(1)}, u32[]{:S(2)}, u32[]{:S(2)}) %collective-permute-start.3) | collective-permute-done | bytes 96 | tf_op jit(solution)/shard_map/ppermute | solution.py:394
  10.6 2.9 %collective-permute-done.1.refs_2_ = bf16[4,96,256]{2,1,0:T(8,128)(2,1)S(1)} collective-permute-done((bf16[4,96,256]{2,1,0:T(8,128)(2,1)S(1)}, bf16[4,96,256]{2,1,0:T(8,128)(2,1)S(1)}, u32[]{:S(2)}, u32[]{:S(2)}) %collective-permute-start.1) | collective-permute-done | bytes 196640 | tf_op jit(solution)/shard_map/ppermute | solution.py:375
  13.5 2.0 %embed.1 = (bf16[4,48,768]{2,1,0:T(8,128)(2,1)S(1)}, bf16[4,48,768]{2,1,0:T(8,128)(2,1)S(1)}, bf16[4,96,768]{2,1,0:T(8,128)(2,1)S(1)}) custom-call(s32[2]{0:T(128)S(1)} %pad_add_fusion.me_ref, bf16[1024,768]{1,0:T(8,128)(2,1)S(1)} %load.3.w_vmem, bf16[4,96,256]{2,1,0:T(8,128)(2,1)S(1)} %get-tuple-element.49.refs_0_, ...), custom_call_target="tpu_custom_call" | custom-call | flops 603979776 | bytes 3145728 | tf_op jit(solution)/shard_map/embed/pallas_call | solution.py:259
  15.6 2.4 %collective-permute-start.4 = (bf16[4,48,768]{2,1,0:T(8,128)(2,1)S(1)}, bf16[4,48,768]{2,1,0:T(8,128)(2,1)S(1)}, u32[]{:S(2)}, u32[]{:S(2)}) collective-permute-start(bf16[4,48,768]{2,1,0:T(8,128)(2,1)S(1)} %get-tuple-element.53), channel_id=1, source_target_pairs={{0,8},{4,12},{8,24},{12,28},{24,16},{28,20},{16,0},{20,4},{1,9},{5... | collective-permute-start | bytes 884744 | tf_op jit(solution)/shard_map/ppermute | solution.py:420
  18.0 2.6 %collective-permute-start.13 = (bf16[4,48,768]{2,1,0:T(8,128)(2,1)S(1)}, bf16[4,48,768]{2,1,0:T(8,128)(2,1)S(1)}, u32[]{:S(2)}, u32[]{:S(2)}) collective-permute-start(bf16[4,48,768]{2,1,0:T(8,128)(2,1)S(1)} %get-tuple-element.72), channel_id=1, source_target_pairs={{0,8},{4,12},{8,24},{12,28},{24,16},{28,20},{16,0},{20,4},{1,9},{5... | collective-permute-start | bytes 884744 | tf_op jit(solution)/shard_map/ppermute | solution.py:420
  20.6 1.5 %pick.5 = (bf16[1,2,96,768]{3,2,1,0:T(8,128)(2,1)S(1)}, bf16[1,2,96,768]{3,2,1,0:T(8,128)(2,1)S(1)}) custom-call(s32[2]{0:T(128)S(1)} %pad_add_fusion.me_ref, s32[4]{0:T(128)S(1)} %fusion.7.line_ref, s32[32]{0:T(128)S(1)} %pad_add_fusion.1.want_ref, bf16[4,96,768]{2,1,0:T(8,128)(2,1)S(1)} %get-tuple-element.55.refs_0_), custom_call_target="tpu_custom_call" | custom-call | bytes 1179648 | tf_op jit(solution)/shard_map/pick/pallas_call | solution.py:285
  22.2 4.7 %collective-permute-done.4.refs_0_ = bf16[4,48,768]{2,1,0:T(8,128)(2,1)S(1)} collective-permute-done((bf16[4,48,768]{2,1,0:T(8,128)(2,1)S(1)}, bf16[4,48,768]{2,1,0:T(8,128)(2,1)S(1)}, u32[]{:S(2)}, u32[]{:S(2)}) %collective-permute-start.4) | collective-permute-done | bytes 294944 | tf_op jit(solution)/shard_map/ppermute | solution.py:420
  26.9 1.9 %collective-permute-start.6 = (bf16[1,2,96,768]{3,2,1,0:T(8,128)(2,1)S(1)}, bf16[1,2,96,768]{3,2,1,0:T(8,128)(2,1)S(1)}, u32[]{:S(2)}, u32[]{:S(2)}) collective-permute-start(bf16[1,2,96,768]{3,2,1,0:T(8,128)(2,1)S(1)} %get-tuple-element.60), channel_id=1, source_target_pairs={{0,4},{4,0},{8,12},{12,8},{16,20},{20,16},{24,28},{28,24},{1,5},{5... | collective-permute-start | bytes 884744 | tf_op jit(solution)/shard_map/ppermute | solution.py:412
  29.5 3.7 %collective-permute-done.13.refs_0_ = bf16[4,48,768]{2,1,0:T(8,128)(2,1)S(1)} collective-permute-done((bf16[4,48,768]{2,1,0:T(8,128)(2,1)S(1)}, bf16[4,48,768]{2,1,0:T(8,128)(2,1)S(1)}, u32[]{:S(2)}, u32[]{:S(2)}) %collective-permute-start.13) | collective-permute-done | bytes 294944 | tf_op jit(solution)/shard_map/ppermute | solution.py:420
  34.7 4.9 %collective-permute-done.5.refs_1_ = bf16[4,48,768]{2,1,0:T(8,128)(2,1)S(1)} collective-permute-done((bf16[4,48,768]{2,1,0:T(8,128)(2,1)S(1)}, bf16[4,48,768]{2,1,0:T(8,128)(2,1)S(1)}, u32[]{:S(2)}, u32[]{:S(2)}) %collective-permute-start.5) | collective-permute-done | bytes 294944 | tf_op jit(solution)/shard_map/ppermute | solution.py:420
  40.7 5.2 %collective-permute-done.14.refs_1_ = bf16[4,48,768]{2,1,0:T(8,128)(2,1)S(1)} collective-permute-done((bf16[4,48,768]{2,1,0:T(8,128)(2,1)S(1)}, bf16[4,48,768]{2,1,0:T(8,128)(2,1)S(1)}, u32[]{:S(2)}, u32[]{:S(2)}) %collective-permute-start.14) | collective-permute-done | bytes 294944 | tf_op jit(solution)/shard_map/ppermute | solution.py:420
  47.0 1.6 %pick.6 = (bf16[2,2,48,768]{3,2,1,0:T(8,128)(2,1)S(1)}, bf16[2,2,48,768]{3,2,1,0:T(8,128)(2,1)S(1)}) custom-call(s32[2]{0:T(128)S(1)} %pad_add_fusion.me_ref, s32[4]{0:T(128)S(1)} %fusion.7.line_ref, s32[32]{0:T(128)S(1)} %pad_add_fusion.1.want_ref, bf16[4,48,768]{2,1,0:T(8,128)(2,1)S(1)} %collective-permute-done.4.refs_0_, ...), custom_call_target="tpu_custom_call" | custom-call | bytes 1179648 | tf_op jit(solution)/shard_map/pick/pallas_call | solution.py:285
  48.6 1.6 %collective-permute-start.7 = (bf16[2,2,48,768]{3,2,1,0:T(8,128)(2,1)S(1)}, bf16[2,2,48,768]{3,2,1,0:T(8,128)(2,1)S(1)}, u32[]{:S(2)}, u32[]{:S(2)}) collective-permute-start(bf16[2,2,48,768]{3,2,1,0:T(8,128)(2,1)S(1)} %get-tuple-element.65), channel_id=1, source_target_pairs={{0,4},{4,0},{8,12},{12,8},{16,20},{20,16},{24,28},{28,24},{1,5},{5... | collective-permute-start | bytes 884744 | tf_op jit(solution)/shard_map/ppermute | solution.py:412
  50.2 1.6 %pick.8 = (bf16[2,2,48,768]{3,2,1,0:T(8,128)(2,1)S(1)}, bf16[2,2,48,768]{3,2,1,0:T(8,128)(2,1)S(1)}) custom-call(s32[2]{0:T(128)S(1)} %pad_add_fusion.me_ref, s32[4]{0:T(128)S(1)} %fusion.7.line_ref, s32[32]{0:T(128)S(1)} %pad_add_fusion.1.want_ref, bf16[4,48,768]{2,1,0:T(8,128)(2,1)S(1)} %collective-permute-done.13.refs_0_, ...), custom_call_target="tpu_custom_call" | custom-call | bytes 1179648 | tf_op jit(solution)/shard_map/pick/pallas_call | solution.py:285
  53.5 1.7 %collective-permute-start.9 = (bf16[1,2,48,768]{3,2,1,0:T(8,128)(2,1)S(1)}, bf16[1,2,48,768]{3,2,1,0:T(8,128)(2,1)S(1)}, u32[]{:S(2)}, u32[]{:S(2)}) collective-permute-start(bf16[1,2,48,768]{3,2,1,0:T(8,128)(2,1)S(1)} %get-tuple-element.67), channel_id=1, source_target_pairs={{0,4},{4,0},{8,12},{12,8},{16,20},{20,16},{24,28},{28,24},{1,5},{5... | collective-permute-start | bytes 442376 | tf_op jit(solution)/shard_map/ppermute | solution.py:412
  55.2 2.7 %collective-permute-done.16.refs_0_ = bf16[4,48,768]{2,1,0:T(8,128)(2,1)S(1)} collective-permute-done((bf16[4,48,768]{2,1,0:T(8,128)(2,1)S(1)}, bf16[4,48,768]{2,1,0:T(8,128)(2,1)S(1)}, u32[]{:S(2)}, u32[]{:S(2)}) %collective-permute-start.16) | collective-permute-done | bytes 294944 | tf_op jit(solution)/shard_map/ppermute | solution.py:420
  59.0 1.6 %collective-permute-start.17 = (bf16[1,2,48,768]{3,2,1,0:T(8,128)(2,1)S(1)}, bf16[1,2,48,768]{3,2,1,0:T(8,128)(2,1)S(1)}, u32[]{:S(2)}, u32[]{:S(2)}) collective-permute-start(bf16[1,2,48,768]{3,2,1,0:T(8,128)(2,1)S(1)} %get-tuple-element.76), channel_id=1, source_target_pairs={{0,4},{4,0},{8,12},{12,8},{16,20},{20,16},{24,28},{28,24},{1,5},{5... | collective-permute-start | bytes 442376 | tf_op jit(solution)/shard_map/ppermute | solution.py:412
  60.6 6.1 %collective-permute-done.9.refs_5_ = bf16[1,2,48,768]{3,2,1,0:T(8,128)(2,1)S(1)} collective-permute-done((bf16[1,2,48,768]{3,2,1,0:T(8,128)(2,1)S(1)}, bf16[1,2,48,768]{3,2,1,0:T(8,128)(2,1)S(1)}, u32[]{:S(2)}, u32[]{:S(2)}) %collective-permute-start.9) | collective-permute-done | bytes 147488 | tf_op jit(solution)/shard_map/ppermute | solution.py:412
  66.7 2.6 %route.3 = (bf16[2,48,768]{2,1,0:T(8,128)(2,1)S(1)}, bf16[2,48,768]{2,1,0:T(8,128)(2,1)S(1)}, bf16[2,48,768]{2,1,0:T(8,128)(2,1)S(1)}, bf16[2,48,768]{2,1,0:T(8,128)(2,1)S(1)}) custom-call(s32[2]{0:T(128)S(1)} %pad_add_fusion.me_ref, s32[4]{0:T(128)S(1)} %fusion.7.line_ref, s32[16]{0:T(128)S(1)} %get-tuple-element.87.side_ref, ...), custom_call_target="tpu_custom_call" | custom-call | bytes 1179648 | tf_op jit(solution)/shard_map/route/pallas_call | solution.py:311
  69.4 1.8 %load.2.wo = bf16[2,768,768]{2,1,0:T(8,128)(2,1)S(1)} custom-call(bf16[2,768,768]{2,1,0:T(8,128)(2,1)} %refs_0_.2), custom_call_target="tpu_custom_call" | custom-call | tf_op jit(solution)/shard_map/load/pallas_call | solution.py:245
  71.3 1.6 %collective-permute-start.11 = (bf16[2,48,768]{2,1,0:T(8,128)(2,1)S(1)}, bf16[2,48,768]{2,1,0:T(8,128)(2,1)S(1)}, u32[]{:S(2)}, u32[]{:S(2)}) collective-permute-start(bf16[2,48,768]{2,1,0:T(8,128)(2,1)S(1)} %get-tuple-element.70), channel_id=1, source_target_pairs={{0,2},{1,3},{2,0},{3,1},{4,6},{5,7},{6,4},{7,5},{8,10},{9,11},{10,... | collective-permute-start | bytes 442376 | tf_op jit(solution)/shard_map/ppermute | solution.py:450
  73.2 2.6 %route.4 = (bf16[2,48,768]{2,1,0:T(8,128)(2,1)S(1)}, bf16[2,48,768]{2,1,0:T(8,128)(2,1)S(1)}, bf16[2,48,768]{2,1,0:T(8,128)(2,1)S(1)}, bf16[2,48,768]{2,1,0:T(8,128)(2,1)S(1)}) custom-call(s32[2]{0:T(128)S(1)} %pad_add_fusion.me_ref, s32[4]{0:T(128)S(1)} %fusion.7.line_ref, s32[16]{0:T(128)S(1)} %get-tuple-element.87.side_ref, ...), custom_call_target="tpu_custom_call" | custom-call | bytes 1179648 | tf_op jit(solution)/shard_map/route/pallas_call | solution.py:311
  76.2 1.6 %collective-permute-start.19 = (bf16[2,48,768]{2,1,0:T(8,128)(2,1)S(1)}, bf16[2,48,768]{2,1,0:T(8,128)(2,1)S(1)}, u32[]{:S(2)}, u32[]{:S(2)}) collective-permute-start(bf16[2,48,768]{2,1,0:T(8,128)(2,1)S(1)} %get-tuple-element.79), channel_id=1, source_target_pairs={{0,2},{1,3},{2,0},{3,1},{4,6},{5,7},{6,4},{7,5},{8,10},{9,11},{10,... | collective-permute-start | bytes 442376 | tf_op jit(solution)/shard_map/ppermute | solution.py:450
  77.8 3.5 %route.5 = (bf16[2,96,768]{2,1,0:T(8,128)(2,1)S(1)}, bf16[2,96,768]{2,1,0:T(8,128)(2,1)S(1)}, bf16[2,96,768]{2,1,0:T(8,128)(2,1)S(1)}, bf16[2,96,768]{2,1,0:T(8,128)(2,1)S(1)}) custom-call(s32[2]{0:T(128)S(1)} %pad_add_fusion.me_ref, s32[4]{0:T(128)S(1)} %fusion.7.line_ref, s32[16]{0:T(128)S(1)} %and_select_fusion.side_ref, ...), custom_call_target="tpu_custom_call" | custom-call | bytes 2359296 | tf_op jit(solution)/shard_map/route/pallas_call | solution.py:311
  82.0 1.6 %collective-permute-start.22 = (bf16[2,96,768]{2,1,0:T(8,128)(2,1)S(1)}, bf16[2,96,768]{2,1,0:T(8,128)(2,1)S(1)}, u32[]{:S(2)}, u32[]{:S(2)}) collective-permute-start(bf16[2,96,768]{2,1,0:T(8,128)(2,1)S(1)} %get-tuple-element.83), channel_id=1, source_target_pairs={{0,2},{1,3},{2,0},{3,1},{4,6},{5,7},{6,4},{7,5},{8,10},{9,11},{10,... | collective-permute-start | bytes 884744 | tf_op jit(solution)/shard_map/ppermute | solution.py:450
  84.4 2.2 %collective-permute-done.20.refs_7_ = bf16[2,48,768]{2,1,0:T(8,128)(2,1)S(1)} collective-permute-done((bf16[2,48,768]{2,1,0:T(8,128)(2,1)S(1)}, bf16[2,48,768]{2,1,0:T(8,128)(2,1)S(1)}, u32[]{:S(2)}, u32[]{:S(2)}) %collective-permute-start.20) | collective-permute-done | bytes 147488 | tf_op jit(solution)/shard_map/ppermute | solution.py:450
  86.7 11.4 %decode.2 = f32[2,4,384]{2,1,0:T(4,128)S(1)} custom-call(s32[2]{0:T(128)S(1)} %pad_add_fusion.me_ref, f32[2,3,768]{2,1,0:T(4,128)S(1)} %copy.24.gains_ref, bf16[2,4,768]{2,1,0:T(4,128)(2,1)S(1)} %copy-done.2, bf16[2,768,1536]{2,1,0:T(8,128)(2,1)S(1)} %bitcast.16, bf16[2,768,768]{2,1,0:T(8,128)(2,1)S(1)} %copy-done.1, bf16[2,768,768]{2,1,0:T(8,128)(2,1)S(1)} %load.2.wo, ...), custom_call_target="tpu_custom_call" | custom-call | flops 5435817984 | bytes 11796480 | tf_op jit(solution)/shard_map/decode/pallas_call | solution.py:333
  99.2 10.9 %decode.3 = f32[2,4,384]{2,1,0:T(4,128)S(1)} custom-call(s32[2]{0:T(128)S(1)} %pad_add_fusion.me_ref, f32[2,3,768]{2,1,0:T(4,128)S(1)} %copy.24.gains_ref, bf16[2,4,768]{2,1,0:T(4,128)(2,1)S(1)} %copy-done.2, bf16[2,768,1536]{2,1,0:T(8,128)(2,1)S(1)} %bitcast.16, bf16[2,768,768]{2,1,0:T(8,128)(2,1)S(1)} %copy-done.1, bf16[2,768,768]{2,1,0:T(8,128)(2,1)S(1)} %load.2.wo, ...), custom_call_target="tpu_custom_call" | custom-call | flops 5435817984 | bytes 11796480 | tf_op jit(solution)/shard_map/decode/pallas_call | solution.py:333
  110.2 5.3 %all_gather.3 = f32[8,2,4,384]{3,2,1,0:T(4,128)S(1)} all-gather(f32[2,2,4,384]{3,2,1,0:T(4,128)S(1)} %pad_maximum_fusion.1), channel_id=1, replica_groups=mesh['view'=8,'mp'=4] {'mp'}, dimensions={0}, use_global_device_ids=true | all-gather | bytes 122880 | tf_op jit(solution)/shard_map/all_gather | solution.py:467
  115.8 12.6 %all_to_all.5 = f32[8,2,1664]{2,1,0:T(2,128)S(1)} all-to-all(f32[8,2,1664]{2,1,0:T(2,128)S(1)} %reshape.110), channel_id=1, replica_groups=mesh['view'=8,'mp'=4] {'view'}, dimensions={0} | all-to-all | bytes 212992 | tf_op jit(solution)/shard_map/all_to_all | solution.py:471
  (69 shorter events, 16.6 us)
Async XLA Ops:
  0.0 8.7 %copy-start = (bf16[1024,768]{1,0:T(8,128)(2,1)S(1)}, bf16[1024,768]{1,0:T(8,128)(2,1)}, u32[]{:S(2)}) copy-start(bf16[1024,768]{1,0:T(8,128)(2,1)} %refs_0_.3) | copy-start | bytes 4718596
  1.4 9.2 %collective-permute-start.2 = (bf16[4,96,256]{2,1,0:T(8,128)(2,1)S(1)}, bf16[4,96,256]{2,1,0:T(8,128)(2,1)S(1)}, u32[]{:S(2)}, u32[]{:S(2)}) collective-permute-start(bf16[4,96,256]{2,1,0:T(8,128)(2,1)S(1)} %get-tuple-element.93), channel_id=1, source_target_pairs={{0,3},{1,2},{2,1},{3,0},{4,7},{5,6},{6,5},{7,4},{8,11},{9,10},{10,... | collective-permute-start | bytes 589832 | tf_op jit(solution)/shard_map/ppermute | solution.py:375
  3.9 1.7 %collective-permute-start = (bf16[4,96,256]{2,1,0:T(8,128)(2,1)S(1)}, bf16[4,96,256]{2,1,0:T(8,128)(2,1)S(1)}, u32[]{:S(2)}, u32[]{:S(2)}) collective-permute-start(bf16[4,96,256]{2,1,0:T(8,128)(2,1)S(1)} %get-tuple-element.95), channel_id=1, source_target_pairs={{0,1},{1,0},{2,3},{3,2},{4,5},{5,4},{6,7},{7,6},{8,9},{9,8},{10,11... | collective-permute-start | bytes 589832 | tf_op jit(solution)/shard_map/ppermute | solution.py:375
  4.5 9.0 %collective-permute-start.1 = (bf16[4,96,256]{2,1,0:T(8,128)(2,1)S(1)}, bf16[4,96,256]{2,1,0:T(8,128)(2,1)S(1)}, u32[]{:S(2)}, u32[]{:S(2)}) collective-permute-start(bf16[4,96,256]{2,1,0:T(8,128)(2,1)S(1)} %get-tuple-element.96), channel_id=1, source_target_pairs={{0,2},{1,3},{2,0},{3,1},{4,6},{5,7},{6,4},{7,5},{8,10},{9,11},{10,... | collective-permute-start | bytes 589832 | tf_op jit(solution)/shard_map/ppermute | solution.py:375
  6.9 3.6 %collective-permute-start.3 = (s32[16]{0:T(128)S(1)}, s32[16]{0:T(128)S(1)}, u32[]{:S(2)}, u32[]{:S(2)}) collective-permute-start(s32[16]{0:T(128)S(1)} %get-tuple-element.98), channel_id=1, source_target_pairs={{0,4},{4,0},{8,12},{12,8},{16,20},{20,16},{24,28},{28,24},{1,5},{5... | collective-permute-start | bytes 200 | tf_op jit(solution)/shard_map/ppermute | solution.py:394
  15.6 53.8 %copy-start.3 = (f32[2,3,768]{2,0,1:T(2,128)S(1)}, f32[2,3,768]{2,0,1:T(2,128)}, u32[]{:S(2)}) copy-start(f32[2,3,768]{2,0,1:T(2,128)} %param.16) | copy-start | bytes 55300
  15.6 11.3 %collective-permute-start.4 = (bf16[4,48,768]{2,1,0:T(8,128)(2,1)S(1)}, bf16[4,48,768]{2,1,0:T(8,128)(2,1)S(1)}, u32[]{:S(2)}, u32[]{:S(2)}) collective-permute-start(bf16[4,48,768]{2,1,0:T(8,128)(2,1)S(1)} %get-tuple-element.53), channel_id=1, source_target_pairs={{0,8},{4,12},{8,24},{12,28},{24,16},{28,20},{16,0},{20,4},{1,9},{5... | collective-permute-start | bytes 884744 | tf_op jit(solution)/shard_map/ppermute | solution.py:420
  18.0 15.2 %collective-permute-start.13 = (bf16[4,48,768]{2,1,0:T(8,128)(2,1)S(1)}, bf16[4,48,768]{2,1,0:T(8,128)(2,1)S(1)}, u32[]{:S(2)}, u32[]{:S(2)}) collective-permute-start(bf16[4,48,768]{2,1,0:T(8,128)(2,1)S(1)} %get-tuple-element.72), channel_id=1, source_target_pairs={{0,8},{4,12},{8,24},{12,28},{24,16},{28,20},{16,0},{20,4},{1,9},{5... | collective-permute-start | bytes 884744 | tf_op jit(solution)/shard_map/ppermute | solution.py:420
  26.9 7.8 %collective-permute-start.6 = (bf16[1,2,96,768]{3,2,1,0:T(8,128)(2,1)S(1)}, bf16[1,2,96,768]{3,2,1,0:T(8,128)(2,1)S(1)}, u32[]{:S(2)}, u32[]{:S(2)}) collective-permute-start(bf16[1,2,96,768]{3,2,1,0:T(8,128)(2,1)S(1)} %get-tuple-element.60), channel_id=1, source_target_pairs={{0,4},{4,0},{8,12},{12,8},{16,20},{20,16},{24,28},{28,24},{1,5},{5... | collective-permute-start | bytes 884744 | tf_op jit(solution)/shard_map/ppermute | solution.py:412
  28.8 10.8 %collective-permute-start.5 = (bf16[4,48,768]{2,1,0:T(8,128)(2,1)S(1)}, bf16[4,48,768]{2,1,0:T(8,128)(2,1)S(1)}, u32[]{:S(2)}, u32[]{:S(2)}) collective-permute-start(bf16[4,48,768]{2,1,0:T(8,128)(2,1)S(1)} %collective-permute-done.4.refs_0_), channel_id=1, source_target_pairs={{0,8},{4,12},{8,24},{12,28},{24,16},{28,20},{16,0},{20,4},{1,9},{5... | collective-permute-start | bytes 884744 | tf_op jit(solution)/shard_map/ppermute | solution.py:420
  33.2 12.6 %collective-permute-start.14 = (bf16[4,48,768]{2,1,0:T(8,128)(2,1)S(1)}, bf16[4,48,768]{2,1,0:T(8,128)(2,1)S(1)}, u32[]{:S(2)}, u32[]{:S(2)}) collective-permute-start(bf16[4,48,768]{2,1,0:T(8,128)(2,1)S(1)} %collective-permute-done.13.refs_0_), channel_id=1, source_target_pairs={{0,8},{4,12},{8,24},{12,28},{24,16},{28,20},{16,0},{20,4},{1,9},{5... | collective-permute-start | bytes 884744 | tf_op jit(solution)/shard_map/ppermute | solution.py:420
  39.6 12.9 %collective-permute-start.8 = (bf16[4,48,768]{2,1,0:T(8,128)(2,1)S(1)}, bf16[4,48,768]{2,1,0:T(8,128)(2,1)S(1)}, u32[]{:S(2)}, u32[]{:S(2)}) collective-permute-start(bf16[4,48,768]{2,1,0:T(8,128)(2,1)S(1)} %collective-permute-done.5.refs_1_), channel_id=1, source_target_pairs={{0,8},{4,12},{8,24},{12,28},{24,16},{28,20},{16,0},{20,4},{1,9},{5... | collective-permute-start | bytes 884744 | tf_op jit(solution)/shard_map/ppermute | solution.py:420
  45.9 12.0 %collective-permute-start.16 = (bf16[4,48,768]{2,1,0:T(8,128)(2,1)S(1)}, bf16[4,48,768]{2,1,0:T(8,128)(2,1)S(1)}, u32[]{:S(2)}, u32[]{:S(2)}) collective-permute-start(bf16[4,48,768]{2,1,0:T(8,128)(2,1)S(1)} %collective-permute-done.14.refs_1_), channel_id=1, source_target_pairs={{0,8},{4,12},{8,24},{12,28},{24,16},{28,20},{16,0},{20,4},{1,9},{5... | collective-permute-start | bytes 884744 | tf_op jit(solution)/shard_map/ppermute | solution.py:420
  48.6 12.0 %collective-permute-start.7 = (bf16[2,2,48,768]{3,2,1,0:T(8,128)(2,1)S(1)}, bf16[2,2,48,768]{3,2,1,0:T(8,128)(2,1)S(1)}, u32[]{:S(2)}, u32[]{:S(2)}) collective-permute-start(bf16[2,2,48,768]{3,2,1,0:T(8,128)(2,1)S(1)} %get-tuple-element.65), channel_id=1, source_target_pairs={{0,4},{4,0},{8,12},{12,8},{16,20},{20,16},{24,28},{28,24},{1,5},{5... | collective-permute-start | bytes 884744 | tf_op jit(solution)/shard_map/ppermute | solution.py:412
  51.8 21.3 %collective-permute-start.15 = (bf16[2,2,48,768]{3,2,1,0:T(8,128)(2,1)S(1)}, bf16[2,2,48,768]{3,2,1,0:T(8,128)(2,1)S(1)}, u32[]{:S(2)}, u32[]{:S(2)}) collective-permute-start(bf16[2,2,48,768]{3,2,1,0:T(8,128)(2,1)S(1)} %get-tuple-element.74), channel_id=1, source_target_pairs={{0,4},{4,0},{8,12},{12,8},{16,20},{20,16},{24,28},{28,24},{1,5},{5... | collective-permute-start | bytes 884744 | tf_op jit(solution)/shard_map/ppermute | solution.py:412
  53.5 13.2 %collective-permute-start.9 = (bf16[1,2,48,768]{3,2,1,0:T(8,128)(2,1)S(1)}, bf16[1,2,48,768]{3,2,1,0:T(8,128)(2,1)S(1)}, u32[]{:S(2)}, u32[]{:S(2)}) collective-permute-start(bf16[1,2,48,768]{3,2,1,0:T(8,128)(2,1)S(1)} %get-tuple-element.67), channel_id=1, source_target_pairs={{0,4},{4,0},{8,12},{12,8},{16,20},{20,16},{24,28},{28,24},{1,5},{5... | collective-permute-start | bytes 442376 | tf_op jit(solution)/shard_map/ppermute | solution.py:412
  59.0 14.2 %collective-permute-start.17 = (bf16[1,2,48,768]{3,2,1,0:T(8,128)(2,1)S(1)}, bf16[1,2,48,768]{3,2,1,0:T(8,128)(2,1)S(1)}, u32[]{:S(2)}, u32[]{:S(2)}) collective-permute-start(bf16[1,2,48,768]{3,2,1,0:T(8,128)(2,1)S(1)} %get-tuple-element.76), channel_id=1, source_target_pairs={{0,4},{4,0},{8,12},{12,8},{16,20},{20,16},{24,28},{28,24},{1,5},{5... | collective-permute-start | bytes 442376 | tf_op jit(solution)/shard_map/ppermute | solution.py:412
  69.3 8.4 %collective-permute-start.10 = (bf16[2,48,768]{2,1,0:T(8,128)(2,1)S(1)}, bf16[2,48,768]{2,1,0:T(8,128)(2,1)S(1)}, u32[]{:S(2)}, u32[]{:S(2)}) collective-permute-start(bf16[2,48,768]{2,1,0:T(8,128)(2,1)S(1)} %get-tuple-element.69), channel_id=1, source_target_pairs={{0,1},{1,0},{2,3},{3,2},{4,5},{5,4},{6,7},{7,6},{8,9},{9,8},{10,11... | collective-permute-start | bytes 442376 | tf_op jit(solution)/shard_map/ppermute | solution.py:450
  69.4 17.3 %slice-start = ((s8[4718592]{0:T(1024)(128)(4,1)}), s8[4194304]{0:T(1024)(128)(4,1)S(1)}, s32[]{:S(2)}) async-start(s8[4718592]{0:T(1024)(128)(4,1)} %bitcast.15), calls=%async_computation.1 | async-start | bytes 8388608
  69.4 17.2 %slice-start.1 = ((s8[4718592]{0:T(1024)(128)(4,1)}), s8[524288]{0:T(1024)(128)(4,1)S(1)}, s32[]{:S(2)}) async-start(s8[4718592]{0:T(1024)(128)(4,1)} %bitcast.15), calls=%async_computation.2 | async-start | bytes 1048576
  71.3 15.4 %copy-start.1 = (bf16[2,768,768]{2,1,0:T(8,128)(2,1)S(1)}, bf16[2,768,768]{2,1,0:T(8,128)(2,1)}, u32[]{:S(2)}) copy-start(bf16[2,768,768]{2,1,0:T(8,128)(2,1)} %wq.3) | copy-start | bytes 7077892
  71.3 15.4 %copy-start.2 = (bf16[2,4,768]{2,1,0:T(4,128)(2,1)S(1)}, bf16[2,4,768]{2,1,0:T(4,128)(2,1)}, u32[]{:S(2)}) copy-start(bf16[2,4,768]{2,1,0:T(4,128)(2,1)} %whead_ref.3) | copy-start | bytes 36868
  71.3 10.0 %collective-permute-start.11 = (bf16[2,48,768]{2,1,0:T(8,128)(2,1)S(1)}, bf16[2,48,768]{2,1,0:T(8,128)(2,1)S(1)}, u32[]{:S(2)}, u32[]{:S(2)}) collective-permute-start(bf16[2,48,768]{2,1,0:T(8,128)(2,1)S(1)} %get-tuple-element.70), channel_id=1, source_target_pairs={{0,2},{1,3},{2,0},{3,1},{4,6},{5,7},{6,4},{7,5},{8,10},{9,11},{10,... | collective-permute-start | bytes 442376 | tf_op jit(solution)/shard_map/ppermute | solution.py:450
  72.9 9.1 %collective-permute-start.12 = (bf16[2,48,768]{2,1,0:T(8,128)(2,1)S(1)}, bf16[2,48,768]{2,1,0:T(8,128)(2,1)S(1)}, u32[]{:S(2)}, u32[]{:S(2)}) collective-permute-start(bf16[2,48,768]{2,1,0:T(8,128)(2,1)S(1)} %get-tuple-element.71), channel_id=1, source_target_pairs={{0,3},{1,2},{2,1},{3,0},{4,7},{5,6},{6,5},{7,4},{8,11},{9,10},{10,... | collective-permute-start | bytes 442376 | tf_op jit(solution)/shard_map/ppermute | solution.py:450
  75.8 7.7 %collective-permute-start.18 = (bf16[2,48,768]{2,1,0:T(8,128)(2,1)S(1)}, bf16[2,48,768]{2,1,0:T(8,128)(2,1)S(1)}, u32[]{:S(2)}, u32[]{:S(2)}) collective-permute-start(bf16[2,48,768]{2,1,0:T(8,128)(2,1)S(1)} %get-tuple-element.78), channel_id=1, source_target_pairs={{0,1},{1,0},{2,3},{3,2},{4,5},{5,4},{6,7},{7,6},{8,9},{9,8},{10,11... | collective-permute-start | bytes 442376 | tf_op jit(solution)/shard_map/ppermute | solution.py:450
  76.2 8.2 %collective-permute-start.19 = (bf16[2,48,768]{2,1,0:T(8,128)(2,1)S(1)}, bf16[2,48,768]{2,1,0:T(8,128)(2,1)S(1)}, u32[]{:S(2)}, u32[]{:S(2)}) collective-permute-start(bf16[2,48,768]{2,1,0:T(8,128)(2,1)S(1)} %get-tuple-element.79), channel_id=1, source_target_pairs={{0,2},{1,3},{2,0},{3,1},{4,6},{5,7},{6,4},{7,5},{8,10},{9,11},{10,... | collective-permute-start | bytes 442376 | tf_op jit(solution)/shard_map/ppermute | solution.py:450
  77.7 8.9 %collective-permute-start.20 = (bf16[2,48,768]{2,1,0:T(8,128)(2,1)S(1)}, bf16[2,48,768]{2,1,0:T(8,128)(2,1)S(1)}, u32[]{:S(2)}, u32[]{:S(2)}) collective-permute-start(bf16[2,48,768]{2,1,0:T(8,128)(2,1)S(1)} %get-tuple-element.80), channel_id=1, source_target_pairs={{0,3},{1,2},{2,1},{3,0},{4,7},{5,6},{6,5},{7,4},{8,11},{9,10},{10,... | collective-permute-start | bytes 442376 | tf_op jit(solution)/shard_map/ppermute | solution.py:450
  81.3 16.7 %collective-permute-start.21 = (bf16[2,96,768]{2,1,0:T(8,128)(2,1)S(1)}, bf16[2,96,768]{2,1,0:T(8,128)(2,1)S(1)}, u32[]{:S(2)}, u32[]{:S(2)}) collective-permute-start(bf16[2,96,768]{2,1,0:T(8,128)(2,1)S(1)} %get-tuple-element.82), channel_id=1, source_target_pairs={{0,1},{1,0},{2,3},{3,2},{4,5},{5,4},{6,7},{7,6},{8,9},{9,8},{10,11... | collective-permute-start | bytes 884744 | tf_op jit(solution)/shard_map/ppermute | solution.py:450
  82.0 16.1 %collective-permute-start.22 = (bf16[2,96,768]{2,1,0:T(8,128)(2,1)S(1)}, bf16[2,96,768]{2,1,0:T(8,128)(2,1)S(1)}, u32[]{:S(2)}, u32[]{:S(2)}) collective-permute-start(bf16[2,96,768]{2,1,0:T(8,128)(2,1)S(1)} %get-tuple-element.83), channel_id=1, source_target_pairs={{0,2},{1,3},{2,0},{3,1},{4,6},{5,7},{6,4},{7,5},{8,10},{9,11},{10,... | collective-permute-start | bytes 884744 | tf_op jit(solution)/shard_map/ppermute | solution.py:450
  83.5 15.7 %collective-permute-start.23 = (bf16[2,96,768]{2,1,0:T(8,128)(2,1)S(1)}, bf16[2,96,768]{2,1,0:T(8,128)(2,1)S(1)}, u32[]{:S(2)}, u32[]{:S(2)}) collective-permute-start(bf16[2,96,768]{2,1,0:T(8,128)(2,1)S(1)} %get-tuple-element.84), channel_id=1, source_target_pairs={{0,3},{1,2},{2,1},{3,0},{4,7},{5,6},{6,5},{7,4},{8,11},{9,10},{10,... | collective-permute-start | bytes 884744 | tf_op jit(solution)/shard_map/ppermute | solution.py:450

commit v5 on v4

--- a/solution.py
+++ b/solution.py
@@ -28,9 +28,9 @@
         copy.wait()
 
 
-def embed_kernel(parts, cuts, me_ref, w_vmem, *refs):
-    pieces, outs, whole = refs[:parts], refs[parts : parts + len(cuts)], refs[parts + len(cuts)]
-    x_ref, emb_ref, in_sem, out_sem = refs[parts + len(cuts) + 1 :]
+def embed_kernel(parts, cuts, keep, me_ref, w_vmem, *refs):
+    pieces, outs = refs[:parts], refs[parts : parts + len(cuts) + keep]
+    x_ref, emb_ref, in_sem, out_sem = refs[parts + len(cuts) + keep :]
     views, _, feat = pieces[0].shape
     width = w_vmem.shape[1]
     column = me_ref[1]
@@ -57,8 +57,9 @@
             )
         )
         copies[-1].start()
-    copies.append(pltpu.make_async_copy(emb_ref, whole, out_sem.at[len(cuts)]))
-    copies[-1].start()
+    if keep:
+        copies.append(pltpu.make_async_copy(emb_ref, outs[-1], out_sem.at[len(cuts)]))
+        copies[-1].start()
     for copy in copies:
         copy.wait()
 
@@ -253,17 +254,17 @@
     )(*weights)
 
 
-def embed(parts, cuts, me, w_embed, pieces):
+def embed(parts, cuts, keep, me, w_embed, pieces):
     views, rows, _ = pieces[0].shape
     full, width = w_embed.shape
     return pl.pallas_call(
-        functools.partial(embed_kernel, parts, cuts),
+        functools.partial(embed_kernel, parts, cuts, keep),
         out_shape=[
             jax.ShapeDtypeStruct((views, size, width), jnp.bfloat16)
-            for size in [size for _, size in cuts] + [rows]
+            for size in [size for _, size in cuts] + [rows] * keep
         ],
         in_specs=[SMEM, VMEM] + [HBM] * parts,
-        out_specs=[HBM] * (len(cuts) + 1),
+        out_specs=[HBM] * (len(cuts) + keep),
         scratch_shapes=[
             pltpu.VMEM((views, rows, full), jnp.bfloat16),
             pltpu.VMEM((views, rows, width), jnp.bfloat16),
@@ -404,7 +405,9 @@
 
     (w_embed,) = load(w_embed)
     pieces, w_embed, wants, line = lax.optimization_barrier((pieces, w_embed, wants, line))
-    *embedded, whole = embed(parts, cuts, me, w_embed, pieces)
+    (first_cut,) = embed(parts, cuts[:1], 0, me, w_embed, pieces)
+    *embedded, whole = embed(parts, cuts, 1, me, w_embed, pieces)
+    embedded[0] = first_cut
     groups = ((0,), tuple(range(1, length - 1)), (length - 1,))
 
     def swap(picked):

time: 130 us -> 129 us (level)
  waiting for transfers between devices: 36.7 us -> 34.6 us
    ppermute x6, waiting for transfers between devices: 21.2 us -> 19.1 us  [on_device(): passed[q].append(lax.ppermute(passed[q][-1], 'view', hop))]
    pallas_call x1 -> x2, Pallas kernels: 2.05 us -> 3.23 us  [embed(): pl.pallas_call(functools.partial(embed_kernel, parts, cuts, keep), out_sh...]
  transfers between devices with their start and end apart: 24 -> 24, of which waited for: 13 -> 13; matrix products, arithmetic and copies ran while one was open for 2% -> 2% of each run, Pallas kernels for 22% -> 24%
where the time goes in v5:
time: 129 us
  Pallas kernels  43.2 us (33%)
  waiting for transfers between devices  34.6 us (27%)
  starting transfers between devices  27.6 us (21%)
  blocking collectives  17.9 us (14%)
  local copies, waits for them, and re-layouts  3.83 us (3%)
    pallas_call x2, Pallas kernels, decode(): pl.pallas_call(functools.partial(decode_kernel, parts, cuts), out_shape=j...  22.3 us
    ppermute x6, waiting for transfers between devices, on_device(): passed[q].append(lax.ppermute(passed[q][-1], 'view', hop))  19.1 us
    all_to_all x1, blocking collectives, on_device(): lax.all_to_all(slotted, 'view', split_axis=0, concat_axis=0, tiled=True)  12.6 us
    ppermute x6, starting transfers between devices, on_device(): passed[q].append(lax.ppermute(passed[q][-1], 'view', hop))  9.2 us
    pallas_call x3, Pallas kernels, route(): pl.pallas_call(functools.partial(route_kernel, lanes, parts, cap, base, c...  8.75 us
    ppermute x5, starting transfers between devices, swap(): lax.ppermute(picked[j], 'view', xor_pairs(count, j))  7.33 us
    pallas_call x5, Pallas kernels, pick(): pl.pallas_call(functools.partial(pick_kernel, lanes, slots, cap), out_sha...  6.97 us
    ppermute x5, waiting for transfers between devices, swap(): lax.ppermute(picked[j], 'view', xor_pairs(count, j))  6.42 us
  transfers between devices with their start and end apart: 24, of which 13 were waited for; matrix products, arithmetic and copies ran while one was open for 2% of the time, Pallas kernels for 24%

profile of v5, /device:TPU:0, one launch (start us, length us, event | category | flops | bytes accessed | tf_op | source)
XLA Modules:
  0.0 128.6 jit_solution(15389926937349180667)
XLA Ops:
  1.4 2.5 %collective-permute-start.2 = (bf16[4,96,256]{2,1,0:T(8,128)(2,1)S(1)}, bf16[4,96,256]{2,1,0:T(8,128)(2,1)S(1)}, u32[]{:S(2)}, u32[]{:S(2)}) collective-permute-start(bf16[4,96,256]{2,1,0:T(8,128)(2,1)S(1)} %get-tuple-element.91), channel_id=1, source_target_pairs={{0,3},{1,2},{2,1},{3,0},{4,7},{5,6},{6,5},{7,4},{8,11},{9,10},{10,... | collective-permute-start | bytes 589832 | tf_op jit(solution)/shard_map/ppermute | solution.py:376
  6.9 1.8 %collective-permute-start.3 = (s32[16]{0:T(128)S(1)}, s32[16]{0:T(128)S(1)}, u32[]{:S(2)}, u32[]{:S(2)}) collective-permute-start(s32[16]{0:T(128)S(1)} %get-tuple-element.96), channel_id=1, source_target_pairs={{0,4},{4,0},{8,12},{12,8},{16,20},{20,16},{24,28},{28,24},{1,5},{5... | collective-permute-start | bytes 200 | tf_op jit(solution)/shard_map/ppermute | solution.py:395
  8.9 1.7 %collective-permute-done.3 = s32[16]{0:T(128)S(1)} collective-permute-done((s32[16]{0:T(128)S(1)}, s32[16]{0:T(128)S(1)}, u32[]{:S(2)}, u32[]{:S(2)}) %collective-permute-start.3) | collective-permute-done | bytes 96 | tf_op jit(solution)/shard_map/ppermute | solution.py:395
  10.6 2.9 %collective-permute-done.1.refs_2_ = bf16[4,96,256]{2,1,0:T(8,128)(2,1)S(1)} collective-permute-done((bf16[4,96,256]{2,1,0:T(8,128)(2,1)S(1)}, bf16[4,96,256]{2,1,0:T(8,128)(2,1)S(1)}, u32[]{:S(2)}, u32[]{:S(2)}) %collective-permute-start.1) | collective-permute-done | bytes 196640 | tf_op jit(solution)/shard_map/ppermute | solution.py:376
  14.8 2.4 %collective-permute-start.4 = (bf16[4,48,768]{2,1,0:T(8,128)(2,1)S(1)}, bf16[4,48,768]{2,1,0:T(8,128)(2,1)S(1)}, u32[]{:S(2)}, u32[]{:S(2)}) collective-permute-start(bf16[4,48,768]{2,1,0:T(8,128)(2,1)S(1)} %embed.2), channel_id=1, source_target_pairs={{0,8},{4,12},{8,24},{12,28},{24,16},{28,20},{16,0},{20,4},{1,9},{5... | collective-permute-start | bytes 884744 | tf_op jit(solution)/shard_map/ppermute | solution.py:423
  17.2 2.0 %embed.3 = (bf16[4,48,768]{2,1,0:T(8,128)(2,1)}, bf16[4,48,768]{2,1,0:T(8,128)(2,1)S(1)}, bf16[4,96,768]{2,1,0:T(8,128)(2,1)S(1)}) custom-call(s32[2]{0:T(128)S(1)} %pad_add_fusion.me_ref, bf16[1024,768]{1,0:T(8,128)(2,1)S(1)} %load.3.w_vmem, bf16[4,96,256]{2,1,0:T(8,128)(2,1)S(1)} %get-tuple-element.48.refs_0_, ...), custom_call_target="tpu_custom_call" | custom-call | flops 603979776 | bytes 3145728 | tf_op jit(solution)/shard_map/embed/pallas_call | solution.py:260
  19.2 2.6 %collective-permute-start.13 = (bf16[4,48,768]{2,1,0:T(8,128)(2,1)S(1)}, bf16[4,48,768]{2,1,0:T(8,128)(2,1)S(1)}, u32[]{:S(2)}, u32[]{:S(2)}) collective-permute-start(bf16[4,48,768]{2,1,0:T(8,128)(2,1)S(1)} %get-tuple-element.70), channel_id=1, source_target_pairs={{0,8},{4,12},{8,24},{12,28},{24,16},{28,20},{16,0},{20,4},{1,9},{5... | collective-permute-start | bytes 884744 | tf_op jit(solution)/shard_map/ppermute | solution.py:423
  21.9 1.5 %pick.5 = (bf16[1,2,96,768]{3,2,1,0:T(8,128)(2,1)S(1)}, bf16[1,2,96,768]{3,2,1,0:T(8,128)(2,1)S(1)}) custom-call(s32[2]{0:T(128)S(1)} %pad_add_fusion.me_ref, s32[4]{0:T(128)S(1)} %fusion.7.line_ref, s32[32]{0:T(128)S(1)} %pad_add_fusion.1.want_ref, bf16[4,96,768]{2,1,0:T(8,128)(2,1)S(1)} %get-tuple-element.53.refs_0_), custom_call_target="tpu_custom_call" | custom-call | bytes 1179648 | tf_op jit(solution)/shard_map/pick/pallas_call | solution.py:286
  23.4 2.7 %collective-permute-done.4.refs_0_ = bf16[4,48,768]{2,1,0:T(8,128)(2,1)S(1)} collective-permute-done((bf16[4,48,768]{2,1,0:T(8,128)(2,1)S(1)}, bf16[4,48,768]{2,1,0:T(8,128)(2,1)S(1)}, u32[]{:S(2)}, u32[]{:S(2)}) %collective-permute-start.4) | collective-permute-done | bytes 294944 | tf_op jit(solution)/shard_map/ppermute | solution.py:423
  26.1 1.9 %collective-permute-start.6 = (bf16[1,2,96,768]{3,2,1,0:T(8,128)(2,1)S(1)}, bf16[1,2,96,768]{3,2,1,0:T(8,128)(2,1)S(1)}, u32[]{:S(2)}, u32[]{:S(2)}) collective-permute-start(bf16[1,2,96,768]{3,2,1,0:T(8,128)(2,1)S(1)} %get-tuple-element.58), channel_id=1, source_target_pairs={{0,4},{4,0},{8,12},{12,8},{16,20},{20,16},{24,28},{28,24},{1,5},{5... | collective-permute-start | bytes 884744 | tf_op jit(solution)/shard_map/ppermute | solution.py:415
  28.7 3.7 %collective-permute-done.13.refs_0_ = bf16[4,48,768]{2,1,0:T(8,128)(2,1)S(1)} collective-permute-done((bf16[4,48,768]{2,1,0:T(8,128)(2,1)S(1)}, bf16[4,48,768]{2,1,0:T(8,128)(2,1)S(1)}, u32[]{:S(2)}, u32[]{:S(2)}) %collective-permute-start.13) | collective-permute-done | bytes 294944 | tf_op jit(solution)/shard_map/ppermute | solution.py:423
  33.9 4.9 %collective-permute-done.5.refs_1_ = bf16[4,48,768]{2,1,0:T(8,128)(2,1)S(1)} collective-permute-done((bf16[4,48,768]{2,1,0:T(8,128)(2,1)S(1)}, bf16[4,48,768]{2,1,0:T(8,128)(2,1)S(1)}, u32[]{:S(2)}, u32[]{:S(2)}) %collective-permute-start.5) | collective-permute-done | bytes 294944 | tf_op jit(solution)/shard_map/ppermute | solution.py:423
  39.8 5.2 %collective-permute-done.14.refs_1_ = bf16[4,48,768]{2,1,0:T(8,128)(2,1)S(1)} collective-permute-done((bf16[4,48,768]{2,1,0:T(8,128)(2,1)S(1)}, bf16[4,48,768]{2,1,0:T(8,128)(2,1)S(1)}, u32[]{:S(2)}, u32[]{:S(2)}) %collective-permute-start.14) | collective-permute-done | bytes 294944 | tf_op jit(solution)/shard_map/ppermute | solution.py:423
  46.1 1.6 %pick.6 = (bf16[2,2,48,768]{3,2,1,0:T(8,128)(2,1)S(1)}, bf16[2,2,48,768]{3,2,1,0:T(8,128)(2,1)S(1)}) custom-call(s32[2]{0:T(128)S(1)} %pad_add_fusion.me_ref, s32[4]{0:T(128)S(1)} %fusion.7.line_ref, s32[32]{0:T(128)S(1)} %pad_add_fusion.1.want_ref, bf16[4,48,768]{2,1,0:T(8,128)(2,1)S(1)} %collective-permute-done.4.refs_0_, ...), custom_call_target="tpu_custom_call" | custom-call | bytes 1179648 | tf_op jit(solution)/shard_map/pick/pallas_call | solution.py:286
  47.8 1.6 %collective-permute-start.7 = (bf16[2,2,48,768]{3,2,1,0:T(8,128)(2,1)S(1)}, bf16[2,2,48,768]{3,2,1,0:T(8,128)(2,1)S(1)}, u32[]{:S(2)}, u32[]{:S(2)}) collective-permute-start(bf16[2,2,48,768]{3,2,1,0:T(8,128)(2,1)S(1)} %get-tuple-element.63), channel_id=1, source_target_pairs={{0,4},{4,0},{8,12},{12,8},{16,20},{20,16},{24,28},{28,24},{1,5},{5... | collective-permute-start | bytes 884744 | tf_op jit(solution)/shard_map/ppermute | solution.py:415
  49.4 1.6 %pick.8 = (bf16[2,2,48,768]{3,2,1,0:T(8,128)(2,1)S(1)}, bf16[2,2,48,768]{3,2,1,0:T(8,128)(2,1)S(1)}) custom-call(s32[2]{0:T(128)S(1)} %pad_add_fusion.me_ref, s32[4]{0:T(128)S(1)} %fusion.7.line_ref, s32[32]{0:T(128)S(1)} %pad_add_fusion.1.want_ref, bf16[4,48,768]{2,1,0:T(8,128)(2,1)S(1)} %collective-permute-done.13.refs_0_, ...), custom_call_target="tpu_custom_call" | custom-call | bytes 1179648 | tf_op jit(solution)/shard_map/pick/pallas_call | solution.py:286
  52.7 1.7 %collective-permute-start.9 = (bf16[1,2,48,768]{3,2,1,0:T(8,128)(2,1)S(1)}, bf16[1,2,48,768]{3,2,1,0:T(8,128)(2,1)S(1)}, u32[]{:S(2)}, u32[]{:S(2)}) collective-permute-start(bf16[1,2,48,768]{3,2,1,0:T(8,128)(2,1)S(1)} %get-tuple-element.65), channel_id=1, source_target_pairs={{0,4},{4,0},{8,12},{12,8},{16,20},{20,16},{24,28},{28,24},{1,5},{5... | collective-permute-start | bytes 442376 | tf_op jit(solution)/shard_map/ppermute | solution.py:415
  54.4 2.7 %collective-permute-done.16.refs_0_ = bf16[4,48,768]{2,1,0:T(8,128)(2,1)S(1)} collective-permute-done((bf16[4,48,768]{2,1,0:T(8,128)(2,1)S(1)}, bf16[4,48,768]{2,1,0:T(8,128)(2,1)S(1)}, u32[]{:S(2)}, u32[]{:S(2)}) %collective-permute-start.16) | collective-permute-done | bytes 294944 | tf_op jit(solution)/shard_map/ppermute | solution.py:423
  58.2 1.6 %collective-permute-start.17 = (bf16[1,2,48,768]{3,2,1,0:T(8,128)(2,1)S(1)}, bf16[1,2,48,768]{3,2,1,0:T(8,128)(2,1)S(1)}, u32[]{:S(2)}, u32[]{:S(2)}) collective-permute-start(bf16[1,2,48,768]{3,2,1,0:T(8,128)(2,1)S(1)} %get-tuple-element.74), channel_id=1, source_target_pairs={{0,4},{4,0},{8,12},{12,8},{16,20},{20,16},{24,28},{28,24},{1,5},{5... | collective-permute-start | bytes 442376 | tf_op jit(solution)/shard_map/ppermute | solution.py:415
  59.8 6.1 %collective-permute-done.9.refs_5_ = bf16[1,2,48,768]{3,2,1,0:T(8,128)(2,1)S(1)} collective-permute-done((bf16[1,2,48,768]{3,2,1,0:T(8,128)(2,1)S(1)}, bf16[1,2,48,768]{3,2,1,0:T(8,128)(2,1)S(1)}, u32[]{:S(2)}, u32[]{:S(2)}) %collective-permute-start.9) | collective-permute-done | bytes 147488 | tf_op jit(solution)/shard_map/ppermute | solution.py:415
  65.9 2.6 %route.3 = (bf16[2,48,768]{2,1,0:T(8,128)(2,1)S(1)}, bf16[2,48,768]{2,1,0:T(8,128)(2,1)S(1)}, bf16[2,48,768]{2,1,0:T(8,128)(2,1)S(1)}, bf16[2,48,768]{2,1,0:T(8,128)(2,1)S(1)}) custom-call(s32[2]{0:T(128)S(1)} %pad_add_fusion.me_ref, s32[4]{0:T(128)S(1)} %fusion.7.line_ref, s32[16]{0:T(128)S(1)} %get-tuple-element.85.side_ref, ...), custom_call_target="tpu_custom_call" | custom-call | bytes 1179648 | tf_op jit(solution)/shard_map/route/pallas_call | solution.py:312
  68.6 1.8 %load.2.wo = bf16[2,768,768]{2,1,0:T(8,128)(2,1)S(1)} custom-call(bf16[2,768,768]{2,1,0:T(8,128)(2,1)} %refs_0_.2), custom_call_target="tpu_custom_call" | custom-call | tf_op jit(solution)/shard_map/load/pallas_call | solution.py:246
  70.5 1.6 %collective-permute-start.11 = (bf16[2,48,768]{2,1,0:T(8,128)(2,1)S(1)}, bf16[2,48,768]{2,1,0:T(8,128)(2,1)S(1)}, u32[]{:S(2)}, u32[]{:S(2)}) collective-permute-start(bf16[2,48,768]{2,1,0:T(8,128)(2,1)S(1)} %get-tuple-element.68), channel_id=1, source_target_pairs={{0,2},{1,3},{2,0},{3,1},{4,6},{5,7},{6,4},{7,5},{8,10},{9,11},{10,... | collective-permute-start | bytes 442376 | tf_op jit(solution)/shard_map/ppermute | solution.py:453
  72.4 2.6 %route.4 = (bf16[2,48,768]{2,1,0:T(8,128)(2,1)S(1)}, bf16[2,48,768]{2,1,0:T(8,128)(2,1)S(1)}, bf16[2,48,768]{2,1,0:T(8,128)(2,1)S(1)}, bf16[2,48,768]{2,1,0:T(8,128)(2,1)S(1)}) custom-call(s32[2]{0:T(128)S(1)} %pad_add_fusion.me_ref, s32[4]{0:T(128)S(1)} %fusion.7.line_ref, s32[16]{0:T(128)S(1)} %get-tuple-element.85.side_ref, ...), custom_call_target="tpu_custom_call" | custom-call | bytes 1179648 | tf_op jit(solution)/shard_map/route/pallas_call | solution.py:312
  75.4 1.6 %collective-permute-start.19 = (bf16[2,48,768]{2,1,0:T(8,128)(2,1)S(1)}, bf16[2,48,768]{2,1,0:T(8,128)(2,1)S(1)}, u32[]{:S(2)}, u32[]{:S(2)}) collective-permute-start(bf16[2,48,768]{2,1,0:T(8,128)(2,1)S(1)} %get-tuple-element.77), channel_id=1, source_target_pairs={{0,2},{1,3},{2,0},{3,1},{4,6},{5,7},{6,4},{7,5},{8,10},{9,11},{10,... | collective-permute-start | bytes 442376 | tf_op jit(solution)/shard_map/ppermute | solution.py:453
  76.9 3.5 %route.5 = (bf16[2,96,768]{2,1,0:T(8,128)(2,1)S(1)}, bf16[2,96,768]{2,1,0:T(8,128)(2,1)S(1)}, bf16[2,96,768]{2,1,0:T(8,128)(2,1)S(1)}, bf16[2,96,768]{2,1,0:T(8,128)(2,1)S(1)}) custom-call(s32[2]{0:T(128)S(1)} %pad_add_fusion.me_ref, s32[4]{0:T(128)S(1)} %fusion.7.line_ref, s32[16]{0:T(128)S(1)} %and_select_fusion.side_ref, ...), custom_call_target="tpu_custom_call" | custom-call | bytes 2359296 | tf_op jit(solution)/shard_map/route/pallas_call | solution.py:312
  81.1 1.6 %collective-permute-start.22 = (bf16[2,96,768]{2,1,0:T(8,128)(2,1)S(1)}, bf16[2,96,768]{2,1,0:T(8,128)(2,1)S(1)}, u32[]{:S(2)}, u32[]{:S(2)}) collective-permute-start(bf16[2,96,768]{2,1,0:T(8,128)(2,1)S(1)} %get-tuple-element.81), channel_id=1, source_target_pairs={{0,2},{1,3},{2,0},{3,1},{4,6},{5,7},{6,4},{7,5},{8,10},{9,11},{10,... | collective-permute-start | bytes 884744 | tf_op jit(solution)/shard_map/ppermute | solution.py:453
  83.6 2.2 %collective-permute-done.20.refs_7_ = bf16[2,48,768]{2,1,0:T(8,128)(2,1)S(1)} collective-permute-done((bf16[2,48,768]{2,1,0:T(8,128)(2,1)S(1)}, bf16[2,48,768]{2,1,0:T(8,128)(2,1)S(1)}, u32[]{:S(2)}, u32[]{:S(2)}) %collective-permute-start.20) | collective-permute-done | bytes 147488 | tf_op jit(solution)/shard_map/ppermute | solution.py:453
  85.8 11.4 %decode.2 = f32[2,4,384]{2,1,0:T(4,128)S(1)} custom-call(s32[2]{0:T(128)S(1)} %pad_add_fusion.me_ref, f32[2,3,768]{2,1,0:T(4,128)S(1)} %copy.24.gains_ref, bf16[2,4,768]{2,1,0:T(4,128)(2,1)S(1)} %copy-done.2, bf16[2,768,1536]{2,1,0:T(8,128)(2,1)S(1)} %bitcast.16, bf16[2,768,768]{2,1,0:T(8,128)(2,1)S(1)} %copy-done.1, bf16[2,768,768]{2,1,0:T(8,128)(2,1)S(1)} %load.2.wo, ...), custom_call_target="tpu_custom_call" | custom-call | flops 5435817984 | bytes 11796480 | tf_op jit(solution)/shard_map/decode/pallas_call | solution.py:334
  98.4 10.9 %decode.3 = f32[2,4,384]{2,1,0:T(4,128)S(1)} custom-call(s32[2]{0:T(128)S(1)} %pad_add_fusion.me_ref, f32[2,3,768]{2,1,0:T(4,128)S(1)} %copy.24.gains_ref, bf16[2,4,768]{2,1,0:T(4,128)(2,1)S(1)} %copy-done.2, bf16[2,768,1536]{2,1,0:T(8,128)(2,1)S(1)} %bitcast.16, bf16[2,768,768]{2,1,0:T(8,128)(2,1)S(1)} %copy-done.1, bf16[2,768,768]{2,1,0:T(8,128)(2,1)S(1)} %load.2.wo, ...), custom_call_target="tpu_custom_call" | custom-call | flops 5435817984 | bytes 11796480 | tf_op jit(solution)/shard_map/decode/pallas_call | solution.py:334
  109.3 5.3 %all_gather.3 = f32[8,2,4,384]{3,2,1,0:T(4,128)S(1)} all-gather(f32[2,2,4,384]{3,2,1,0:T(4,128)S(1)} %pad_maximum_fusion.1), channel_id=1, replica_groups=mesh['view'=8,'mp'=4] {'mp'}, dimensions={0}, use_global_device_ids=true | all-gather | bytes 122880 | tf_op jit(solution)/shard_map/all_gather | solution.py:470
  115.0 12.6 %all_to_all.5 = f32[8,2,1664]{2,1,0:T(2,128)S(1)} all-to-all(f32[8,2,1664]{2,1,0:T(2,128)S(1)} %reshape.110), channel_id=1, replica_groups=mesh['view'=8,'mp'=4] {'view'}, dimensions={0} | all-to-all | bytes 212992 | tf_op jit(solution)/shard_map/all_to_all | solution.py:474
  (70 shorter events, 17.8 us)
Async XLA Ops:
  0.0 8.7 %copy-start = (bf16[1024,768]{1,0:T(8,128)(2,1)S(1)}, bf16[1024,768]{1,0:T(8,128)(2,1)}, u32[]{:S(2)}) copy-start(bf16[1024,768]{1,0:T(8,128)(2,1)} %refs_0_.3) | copy-start | bytes 4718596
  1.4 9.2 %collective-permute-start.2 = (bf16[4,96,256]{2,1,0:T(8,128)(2,1)S(1)}, bf16[4,96,256]{2,1,0:T(8,128)(2,1)S(1)}, u32[]{:S(2)}, u32[]{:S(2)}) collective-permute-start(bf16[4,96,256]{2,1,0:T(8,128)(2,1)S(1)} %get-tuple-element.91), channel_id=1, source_target_pairs={{0,3},{1,2},{2,1},{3,0},{4,7},{5,6},{6,5},{7,4},{8,11},{9,10},{10,... | collective-permute-start | bytes 589832 | tf_op jit(solution)/shard_map/ppermute | solution.py:376
  3.9 1.7 %collective-permute-start = (bf16[4,96,256]{2,1,0:T(8,128)(2,1)S(1)}, bf16[4,96,256]{2,1,0:T(8,128)(2,1)S(1)}, u32[]{:S(2)}, u32[]{:S(2)}) collective-permute-start(bf16[4,96,256]{2,1,0:T(8,128)(2,1)S(1)} %get-tuple-element.93), channel_id=1, source_target_pairs={{0,1},{1,0},{2,3},{3,2},{4,5},{5,4},{6,7},{7,6},{8,9},{9,8},{10,11... | collective-permute-start | bytes 589832 | tf_op jit(solution)/shard_map/ppermute | solution.py:376
  4.5 9.0 %collective-permute-start.1 = (bf16[4,96,256]{2,1,0:T(8,128)(2,1)S(1)}, bf16[4,96,256]{2,1,0:T(8,128)(2,1)S(1)}, u32[]{:S(2)}, u32[]{:S(2)}) collective-permute-start(bf16[4,96,256]{2,1,0:T(8,128)(2,1)S(1)} %get-tuple-element.94), channel_id=1, source_target_pairs={{0,2},{1,3},{2,0},{3,1},{4,6},{5,7},{6,4},{7,5},{8,10},{9,11},{10,... | collective-permute-start | bytes 589832 | tf_op jit(solution)/shard_map/ppermute | solution.py:376
  6.9 3.6 %collective-permute-start.3 = (s32[16]{0:T(128)S(1)}, s32[16]{0:T(128)S(1)}, u32[]{:S(2)}, u32[]{:S(2)}) collective-permute-start(s32[16]{0:T(128)S(1)} %get-tuple-element.96), channel_id=1, source_target_pairs={{0,4},{4,0},{8,12},{12,8},{16,20},{20,16},{24,28},{28,24},{1,5},{5... | collective-permute-start | bytes 200 | tf_op jit(solution)/shard_map/ppermute | solution.py:395
  14.8 11.3 %collective-permute-start.4 = (bf16[4,48,768]{2,1,0:T(8,128)(2,1)S(1)}, bf16[4,48,768]{2,1,0:T(8,128)(2,1)S(1)}, u32[]{:S(2)}, u32[]{:S(2)}) collective-permute-start(bf16[4,48,768]{2,1,0:T(8,128)(2,1)S(1)} %embed.2), channel_id=1, source_target_pairs={{0,8},{4,12},{8,24},{12,28},{24,16},{28,20},{16,0},{20,4},{1,9},{5... | collective-permute-start | bytes 884744 | tf_op jit(solution)/shard_map/ppermute | solution.py:423
  19.2 49.3 %copy-start.3 = (f32[2,3,768]{2,0,1:T(2,128)S(1)}, f32[2,3,768]{2,0,1:T(2,128)}, u32[]{:S(2)}) copy-start(f32[2,3,768]{2,0,1:T(2,128)} %param.16) | copy-start | bytes 55300
  19.2 13.2 %collective-permute-start.13 = (bf16[4,48,768]{2,1,0:T(8,128)(2,1)S(1)}, bf16[4,48,768]{2,1,0:T(8,128)(2,1)S(1)}, u32[]{:S(2)}, u32[]{:S(2)}) collective-permute-start(bf16[4,48,768]{2,1,0:T(8,128)(2,1)S(1)} %get-tuple-element.70), channel_id=1, source_target_pairs={{0,8},{4,12},{8,24},{12,28},{24,16},{28,20},{16,0},{20,4},{1,9},{5... | collective-permute-start | bytes 884744 | tf_op jit(solution)/shard_map/ppermute | solution.py:423
  26.1 7.8 %collective-permute-start.6 = (bf16[1,2,96,768]{3,2,1,0:T(8,128)(2,1)S(1)}, bf16[1,2,96,768]{3,2,1,0:T(8,128)(2,1)S(1)}, u32[]{:S(2)}, u32[]{:S(2)}) collective-permute-start(bf16[1,2,96,768]{3,2,1,0:T(8,128)(2,1)S(1)} %get-tuple-element.58), channel_id=1, source_target_pairs={{0,4},{4,0},{8,12},{12,8},{16,20},{20,16},{24,28},{28,24},{1,5},{5... | collective-permute-start | bytes 884744 | tf_op jit(solution)/shard_map/ppermute | solution.py:415
  27.9 10.8 %collective-permute-start.5 = (bf16[4,48,768]{2,1,0:T(8,128)(2,1)S(1)}, bf16[4,48,768]{2,1,0:T(8,128)(2,1)S(1)}, u32[]{:S(2)}, u32[]{:S(2)}) collective-permute-start(bf16[4,48,768]{2,1,0:T(8,128)(2,1)S(1)} %collective-permute-done.4.refs_0_), channel_id=1, source_target_pairs={{0,8},{4,12},{8,24},{12,28},{24,16},{28,20},{16,0},{20,4},{1,9},{5... | collective-permute-start | bytes 884744 | tf_op jit(solution)/shard_map/ppermute | solution.py:423
  32.4 12.6 %collective-permute-start.14 = (bf16[4,48,768]{2,1,0:T(8,128)(2,1)S(1)}, bf16[4,48,768]{2,1,0:T(8,128)(2,1)S(1)}, u32[]{:S(2)}, u32[]{:S(2)}) collective-permute-start(bf16[4,48,768]{2,1,0:T(8,128)(2,1)S(1)} %collective-permute-done.13.refs_0_), channel_id=1, source_target_pairs={{0,8},{4,12},{8,24},{12,28},{24,16},{28,20},{16,0},{20,4},{1,9},{5... | collective-permute-start | bytes 884744 | tf_op jit(solution)/shard_map/ppermute | solution.py:423
  38.7 12.9 %collective-permute-start.8 = (bf16[4,48,768]{2,1,0:T(8,128)(2,1)S(1)}, bf16[4,48,768]{2,1,0:T(8,128)(2,1)S(1)}, u32[]{:S(2)}, u32[]{:S(2)}) collective-permute-start(bf16[4,48,768]{2,1,0:T(8,128)(2,1)S(1)} %collective-permute-done.5.refs_1_), channel_id=1, source_target_pairs={{0,8},{4,12},{8,24},{12,28},{24,16},{28,20},{16,0},{20,4},{1,9},{5... | collective-permute-start | bytes 884744 | tf_op jit(solution)/shard_map/ppermute | solution.py:423
  45.0 12.0 %collective-permute-start.16 = (bf16[4,48,768]{2,1,0:T(8,128)(2,1)S(1)}, bf16[4,48,768]{2,1,0:T(8,128)(2,1)S(1)}, u32[]{:S(2)}, u32[]{:S(2)}) collective-permute-start(bf16[4,48,768]{2,1,0:T(8,128)(2,1)S(1)} %collective-permute-done.14.refs_1_), channel_id=1, source_target_pairs={{0,8},{4,12},{8,24},{12,28},{24,16},{28,20},{16,0},{20,4},{1,9},{5... | collective-permute-start | bytes 884744 | tf_op jit(solution)/shard_map/ppermute | solution.py:423
  47.8 12.0 %collective-permute-start.7 = (bf16[2,2,48,768]{3,2,1,0:T(8,128)(2,1)S(1)}, bf16[2,2,48,768]{3,2,1,0:T(8,128)(2,1)S(1)}, u32[]{:S(2)}, u32[]{:S(2)}) collective-permute-start(bf16[2,2,48,768]{3,2,1,0:T(8,128)(2,1)S(1)} %get-tuple-element.63), channel_id=1, source_target_pairs={{0,4},{4,0},{8,12},{12,8},{16,20},{20,16},{24,28},{28,24},{1,5},{5... | collective-permute-start | bytes 884744 | tf_op jit(solution)/shard_map/ppermute | solution.py:415
  51.0 21.3 %collective-permute-start.15 = (bf16[2,2,48,768]{3,2,1,0:T(8,128)(2,1)S(1)}, bf16[2,2,48,768]{3,2,1,0:T(8,128)(2,1)S(1)}, u32[]{:S(2)}, u32[]{:S(2)}) collective-permute-start(bf16[2,2,48,768]{3,2,1,0:T(8,128)(2,1)S(1)} %get-tuple-element.72), channel_id=1, source_target_pairs={{0,4},{4,0},{8,12},{12,8},{16,20},{20,16},{24,28},{28,24},{1,5},{5... | collective-permute-start | bytes 884744 | tf_op jit(solution)/shard_map/ppermute | solution.py:415
  52.7 13.2 %collective-permute-start.9 = (bf16[1,2,48,768]{3,2,1,0:T(8,128)(2,1)S(1)}, bf16[1,2,48,768]{3,2,1,0:T(8,128)(2,1)S(1)}, u32[]{:S(2)}, u32[]{:S(2)}) collective-permute-start(bf16[1,2,48,768]{3,2,1,0:T(8,128)(2,1)S(1)} %get-tuple-element.65), channel_id=1, source_target_pairs={{0,4},{4,0},{8,12},{12,8},{16,20},{20,16},{24,28},{28,24},{1,5},{5... | collective-permute-start | bytes 442376 | tf_op jit(solution)/shard_map/ppermute | solution.py:415
  58.2 14.2 %collective-permute-start.17 = (bf16[1,2,48,768]{3,2,1,0:T(8,128)(2,1)S(1)}, bf16[1,2,48,768]{3,2,1,0:T(8,128)(2,1)S(1)}, u32[]{:S(2)}, u32[]{:S(2)}) collective-permute-start(bf16[1,2,48,768]{3,2,1,0:T(8,128)(2,1)S(1)} %get-tuple-element.74), channel_id=1, source_target_pairs={{0,4},{4,0},{8,12},{12,8},{16,20},{20,16},{24,28},{28,24},{1,5},{5... | collective-permute-start | bytes 442376 | tf_op jit(solution)/shard_map/ppermute | solution.py:415
  68.5 8.4 %collective-permute-start.10 = (bf16[2,48,768]{2,1,0:T(8,128)(2,1)S(1)}, bf16[2,48,768]{2,1,0:T(8,128)(2,1)S(1)}, u32[]{:S(2)}, u32[]{:S(2)}) collective-permute-start(bf16[2,48,768]{2,1,0:T(8,128)(2,1)S(1)} %get-tuple-element.67), channel_id=1, source_target_pairs={{0,1},{1,0},{2,3},{3,2},{4,5},{5,4},{6,7},{7,6},{8,9},{9,8},{10,11... | collective-permute-start | bytes 442376 | tf_op jit(solution)/shard_map/ppermute | solution.py:453
  68.6 17.2 %slice-start = ((s8[4718592]{0:T(1024)(128)(4,1)}), s8[4194304]{0:T(1024)(128)(4,1)S(1)}, s32[]{:S(2)}) async-start(s8[4718592]{0:T(1024)(128)(4,1)} %bitcast.15), calls=%async_computation.1 | async-start | bytes 8388608
  68.6 17.2 %slice-start.1 = ((s8[4718592]{0:T(1024)(128)(4,1)}), s8[524288]{0:T(1024)(128)(4,1)S(1)}, s32[]{:S(2)}) async-start(s8[4718592]{0:T(1024)(128)(4,1)} %bitcast.15), calls=%async_computation.2 | async-start | bytes 1048576
  70.4 15.4 %copy-start.1 = (bf16[2,768,768]{2,1,0:T(8,128)(2,1)S(1)}, bf16[2,768,768]{2,1,0:T(8,128)(2,1)}, u32[]{:S(2)}) copy-start(bf16[2,768,768]{2,1,0:T(8,128)(2,1)} %wq.3) | copy-start | bytes 7077892
  70.4 15.4 %copy-start.2 = (bf16[2,4,768]{2,1,0:T(4,128)(2,1)S(1)}, bf16[2,4,768]{2,1,0:T(4,128)(2,1)}, u32[]{:S(2)}) copy-start(bf16[2,4,768]{2,1,0:T(4,128)(2,1)} %whead_ref.3) | copy-start | bytes 36868
  70.5 10.0 %collective-permute-start.11 = (bf16[2,48,768]{2,1,0:T(8,128)(2,1)S(1)}, bf16[2,48,768]{2,1,0:T(8,128)(2,1)S(1)}, u32[]{:S(2)}, u32[]{:S(2)}) collective-permute-start(bf16[2,48,768]{2,1,0:T(8,128)(2,1)S(1)} %get-tuple-element.68), channel_id=1, source_target_pairs={{0,2},{1,3},{2,0},{3,1},{4,6},{5,7},{6,4},{7,5},{8,10},{9,11},{10,... | collective-permute-start | bytes 442376 | tf_op jit(solution)/shard_map/ppermute | solution.py:453
  72.1 9.1 %collective-permute-start.12 = (bf16[2,48,768]{2,1,0:T(8,128)(2,1)S(1)}, bf16[2,48,768]{2,1,0:T(8,128)(2,1)S(1)}, u32[]{:S(2)}, u32[]{:S(2)}) collective-permute-start(bf16[2,48,768]{2,1,0:T(8,128)(2,1)S(1)} %get-tuple-element.69), channel_id=1, source_target_pairs={{0,3},{1,2},{2,1},{3,0},{4,7},{5,6},{6,5},{7,4},{8,11},{9,10},{10,... | collective-permute-start | bytes 442376 | tf_op jit(solution)/shard_map/ppermute | solution.py:453
  75.0 7.7 %collective-permute-start.18 = (bf16[2,48,768]{2,1,0:T(8,128)(2,1)S(1)}, bf16[2,48,768]{2,1,0:T(8,128)(2,1)S(1)}, u32[]{:S(2)}, u32[]{:S(2)}) collective-permute-start(bf16[2,48,768]{2,1,0:T(8,128)(2,1)S(1)} %get-tuple-element.76), channel_id=1, source_target_pairs={{0,1},{1,0},{2,3},{3,2},{4,5},{5,4},{6,7},{7,6},{8,9},{9,8},{10,11... | collective-permute-start | bytes 442376 | tf_op jit(solution)/shard_map/ppermute | solution.py:453
  75.4 8.2 %collective-permute-start.19 = (bf16[2,48,768]{2,1,0:T(8,128)(2,1)S(1)}, bf16[2,48,768]{2,1,0:T(8,128)(2,1)S(1)}, u32[]{:S(2)}, u32[]{:S(2)}) collective-permute-start(bf16[2,48,768]{2,1,0:T(8,128)(2,1)S(1)} %get-tuple-element.77), channel_id=1, source_target_pairs={{0,2},{1,3},{2,0},{3,1},{4,6},{5,7},{6,4},{7,5},{8,10},{9,11},{10,... | collective-permute-start | bytes 442376 | tf_op jit(solution)/shard_map/ppermute | solution.py:453
  76.9 8.9 %collective-permute-start.20 = (bf16[2,48,768]{2,1,0:T(8,128)(2,1)S(1)}, bf16[2,48,768]{2,1,0:T(8,128)(2,1)S(1)}, u32[]{:S(2)}, u32[]{:S(2)}) collective-permute-start(bf16[2,48,768]{2,1,0:T(8,128)(2,1)S(1)} %get-tuple-element.78), channel_id=1, source_target_pairs={{0,3},{1,2},{2,1},{3,0},{4,7},{5,6},{6,5},{7,4},{8,11},{9,10},{10,... | collective-permute-start | bytes 442376 | tf_op jit(solution)/shard_map/ppermute | solution.py:453
  80.5 16.7 %collective-permute-start.21 = (bf16[2,96,768]{2,1,0:T(8,128)(2,1)S(1)}, bf16[2,96,768]{2,1,0:T(8,128)(2,1)S(1)}, u32[]{:S(2)}, u32[]{:S(2)}) collective-permute-start(bf16[2,96,768]{2,1,0:T(8,128)(2,1)S(1)} %get-tuple-element.80), channel_id=1, source_target_pairs={{0,1},{1,0},{2,3},{3,2},{4,5},{5,4},{6,7},{7,6},{8,9},{9,8},{10,11... | collective-permute-start | bytes 884744 | tf_op jit(solution)/shard_map/ppermute | solution.py:453
  81.1 16.1 %collective-permute-start.22 = (bf16[2,96,768]{2,1,0:T(8,128)(2,1)S(1)}, bf16[2,96,768]{2,1,0:T(8,128)(2,1)S(1)}, u32[]{:S(2)}, u32[]{:S(2)}) collective-permute-start(bf16[2,96,768]{2,1,0:T(8,128)(2,1)S(1)} %get-tuple-element.81), channel_id=1, source_target_pairs={{0,2},{1,3},{2,0},{3,1},{4,6},{5,7},{6,4},{7,5},{8,10},{9,11},{10,... | collective-permute-start | bytes 884744 | tf_op jit(solution)/shard_map/ppermute | solution.py:453
  82.7 15.7 %collective-permute-start.23 = (bf16[2,96,768]{2,1,0:T(8,128)(2,1)S(1)}, bf16[2,96,768]{2,1,0:T(8,128)(2,1)S(1)}, u32[]{:S(2)}, u32[]{:S(2)}) collective-permute-start(bf16[2,96,768]{2,1,0:T(8,128)(2,1)S(1)} %get-tuple-element.82), channel_id=1, source_target_pairs={{0,3},{1,2},{2,1},{3,0},{4,7},{5,6},{6,5},{7,4},{8,11},{9,10},{10,... | collective-permute-start | bytes 884744 | tf_op jit(solution)/shard_map/ppermute | solution.py:453

commit v6 on v5

--- a/solution.py
+++ b/solution.py
@@ -67,16 +67,9 @@
 def pick_kernel(lanes, slots, cap, me_ref, line_ref, want_ref, *refs):
     count = len(slots)
     sources, outs = refs[:count], refs[count : count + lanes]
-    stage_ref, in_sem, out_sem = refs[count + lanes :]
+    out_sem = refs[count + lanes]
     lane = me_ref[0] % lanes
     rows = line_ref.shape[0] * lanes
-    copies = [
-        pltpu.make_async_copy(sources[n], stage_ref.at[n], in_sem.at[n]) for n in range(count)
-    ]
-    for copy in copies:
-        copy.start()
-    for copy in copies:
-        copy.wait()
     copies = []
     for j in range(lanes):
         for n, i in enumerate(slots):
@@ -84,7 +77,7 @@
                 view = want_ref[(j * rows + line_ref[i] * lanes + lane) * cap + c]
                 copies.append(
                     pltpu.make_async_copy(
-                        stage_ref.at[n, jnp.maximum(view, 0)], outs[j].at[n, c], out_sem.at[len(copies)]
+                        sources[n].at[jnp.maximum(view, 0)], outs[j].at[n, c], out_sem.at[len(copies)]
                     )
                 )
                 copies[-1].start()
@@ -282,15 +275,13 @@
 
 
 def pick(lanes, slots, cap, me, line, wants, sources):
-    views, size, width = sources[0].shape
+    _, size, width = sources[0].shape
     return pl.pallas_call(
         functools.partial(pick_kernel, lanes, slots, cap),
         out_shape=[jax.ShapeDtypeStruct((len(slots), cap, size, width), jnp.bfloat16)] * lanes,
         in_specs=[SMEM, SMEM, SMEM] + [HBM] * len(sources),
         out_specs=[HBM] * lanes,
         scratch_shapes=[
-            pltpu.VMEM((len(slots), views, size, width), jnp.bfloat16),
-            pltpu.SemaphoreType.DMA((len(slots),)),
             pltpu.SemaphoreType.DMA((lanes * len(slots) * cap,)),
         ],
         compiler_params=pltpu.CompilerParams(vmem_limit_bytes=16 * 1024 * 1024),

time: 129 us -> 129 us (level)
  transfers between devices with their start and end apart: 24 -> 24, of which waited for: 13 -> 14; matrix products, arithmetic and copies ran while one was open for 2% -> 2% of each run, Pallas kernels for 24% -> 24%
where the time goes in v6:
time: 129 us; the launch traced here: 128 us
  Pallas kernels  42.6 us (33%)
  waiting for transfers between devices  34.8 us (27%)
  starting transfers between devices  27.9 us (22%)
  blocking collectives  17.9 us (14%)
  local copies, waits for them, and re-layouts  3.83 us (3%)
    pallas_call x2, Pallas kernels, decode(): pl.pallas_call(functools.partial(decode_kernel, parts, cuts), out_shape=j...  22.3 us
    ppermute x6, waiting for transfers between devices, on_device(): passed[q].append(lax.ppermute(passed[q][-1], 'view', hop))  19.4 us
    all_to_all x1, blocking collectives, on_device(): lax.all_to_all(slotted, 'view', split_axis=0, concat_axis=0, tiled=True)  12.6 us
    ppermute x6, starting transfers between devices, on_device(): passed[q].append(lax.ppermute(passed[q][-1], 'view', hop))  9.2 us
    pallas_call x3, Pallas kernels, route(): pl.pallas_call(functools.partial(route_kernel, lanes, parts, cap, base, c...  8.75 us
    ppermute x5, starting transfers between devices, swap(): lax.ppermute(picked[j], 'view', xor_pairs(count, j))  7.56 us
    pallas_call x5, Pallas kernels, pick(): pl.pallas_call(functools.partial(pick_kernel, lanes, slots, cap), out_sha...  6.4 us
    ppermute x5, waiting for transfers between devices, swap(): lax.ppermute(picked[j], 'view', xor_pairs(count, j))  6.35 us
  transfers between devices with their start and end apart: 24, of which 14 were waited for; matrix products, arithmetic and copies ran while one was open for 2% of the time, Pallas kernels for 24%

profile of v6, /device:TPU:0, one launch (start us, length us, event | category | flops | bytes accessed | tf_op | source)
XLA Modules:
  0.0 128.4 jit_solution(13642073115677042428)
XLA Ops:
  1.4 2.5 %collective-permute-start.2 = (bf16[4,96,256]{2,1,0:T(8,128)(2,1)S(1)}, bf16[4,96,256]{2,1,0:T(8,128)(2,1)S(1)}, u32[]{:S(2)}, u32[]{:S(2)}) collective-permute-start(bf16[4,96,256]{2,1,0:T(8,128)(2,1)S(1)} %get-tuple-element.91), channel_id=1, source_target_pairs={{0,3},{1,2},{2,1},{3,0},{4,7},{5,6},{6,5},{7,4},{8,11},{9,10},{10,... | collective-permute-start | bytes 589832 | tf_op jit(solution)/shard_map/ppermute | solution.py:367
  6.9 1.8 %collective-permute-start.3 = (s32[16]{0:T(128)S(1)}, s32[16]{0:T(128)S(1)}, u32[]{:S(2)}, u32[]{:S(2)}) collective-permute-start(s32[16]{0:T(128)S(1)} %get-tuple-element.96), channel_id=1, source_target_pairs={{0,4},{4,0},{8,12},{12,8},{16,20},{20,16},{24,28},{28,24},{1,5},{5... | collective-permute-start | bytes 200 | tf_op jit(solution)/shard_map/ppermute | solution.py:386
  8.9 1.7 %collective-permute-done.3 = s32[16]{0:T(128)S(1)} collective-permute-done((s32[16]{0:T(128)S(1)}, s32[16]{0:T(128)S(1)}, u32[]{:S(2)}, u32[]{:S(2)}) %collective-permute-start.3) | collective-permute-done | bytes 96 | tf_op jit(solution)/shard_map/ppermute | solution.py:386
  10.6 2.9 %collective-permute-done.1.refs_2_ = bf16[4,96,256]{2,1,0:T(8,128)(2,1)S(1)} collective-permute-done((bf16[4,96,256]{2,1,0:T(8,128)(2,1)S(1)}, bf16[4,96,256]{2,1,0:T(8,128)(2,1)S(1)}, u32[]{:S(2)}, u32[]{:S(2)}) %collective-permute-start.1) | collective-permute-done | bytes 196640 | tf_op jit(solution)/shard_map/ppermute | solution.py:367
  14.8 2.4 %collective-permute-start.4 = (bf16[4,48,768]{2,1,0:T(8,128)(2,1)S(1)}, bf16[4,48,768]{2,1,0:T(8,128)(2,1)S(1)}, u32[]{:S(2)}, u32[]{:S(2)}) collective-permute-start(bf16[4,48,768]{2,1,0:T(8,128)(2,1)S(1)} %embed.2), channel_id=1, source_target_pairs={{0,8},{4,12},{8,24},{12,28},{24,16},{28,20},{16,0},{20,4},{1,9},{5... | collective-permute-start | bytes 884744 | tf_op jit(solution)/shard_map/ppermute | solution.py:414
  17.2 2.0 %embed.3 = (bf16[4,48,768]{2,1,0:T(8,128)(2,1)}, bf16[4,48,768]{2,1,0:T(8,128)(2,1)S(1)}, bf16[4,96,768]{2,1,0:T(8,128)(2,1)S(1)}) custom-call(s32[2]{0:T(128)S(1)} %pad_add_fusion.me_ref, bf16[1024,768]{1,0:T(8,128)(2,1)S(1)} %load.3.w_vmem, bf16[4,96,256]{2,1,0:T(8,128)(2,1)S(1)} %get-tuple-element.48.refs_0_, ...), custom_call_target="tpu_custom_call" | custom-call | flops 603979776 | bytes 3145728 | tf_op jit(solution)/shard_map/embed/pallas_call | solution.py:253
  19.2 2.6 %collective-permute-start.13 = (bf16[4,48,768]{2,1,0:T(8,128)(2,1)S(1)}, bf16[4,48,768]{2,1,0:T(8,128)(2,1)S(1)}, u32[]{:S(2)}, u32[]{:S(2)}) collective-permute-start(bf16[4,48,768]{2,1,0:T(8,128)(2,1)S(1)} %get-tuple-element.70), channel_id=1, source_target_pairs={{0,8},{4,12},{8,24},{12,28},{24,16},{28,20},{16,0},{20,4},{1,9},{5... | collective-permute-start | bytes 884744 | tf_op jit(solution)/shard_map/ppermute | solution.py:414
  21.9 1.4 %pick.5 = (bf16[1,2,96,768]{3,2,1,0:T(8,128)(2,1)S(1)}, bf16[1,2,96,768]{3,2,1,0:T(8,128)(2,1)S(1)}) custom-call(s32[2]{0:T(128)S(1)} %pad_add_fusion.me_ref, s32[4]{0:T(128)S(1)} %fusion.7.line_ref, s32[32]{0:T(128)S(1)} %pad_add_fusion.1.want_ref, bf16[4,96,768]{2,1,0:T(8,128)(2,1)S(1)} %get-tuple-element.53.refs_0_), custom_call_target="tpu_custom_call" | custom-call | bytes 1179648 | tf_op jit(solution)/shard_map/pick/pallas_call | solution.py:279
  23.3 2.8 %collective-permute-done.4.refs_0_ = bf16[4,48,768]{2,1,0:T(8,128)(2,1)S(1)} collective-permute-done((bf16[4,48,768]{2,1,0:T(8,128)(2,1)S(1)}, bf16[4,48,768]{2,1,0:T(8,128)(2,1)S(1)}, u32[]{:S(2)}, u32[]{:S(2)}) %collective-permute-start.4) | collective-permute-done | bytes 294944 | tf_op jit(solution)/shard_map/ppermute | solution.py:414
  26.1 1.9 %collective-permute-start.6 = (bf16[1,2,96,768]{3,2,1,0:T(8,128)(2,1)S(1)}, bf16[1,2,96,768]{3,2,1,0:T(8,128)(2,1)S(1)}, u32[]{:S(2)}, u32[]{:S(2)}) collective-permute-start(bf16[1,2,96,768]{3,2,1,0:T(8,128)(2,1)S(1)} %get-tuple-element.58), channel_id=1, source_target_pairs={{0,4},{4,0},{8,12},{12,8},{16,20},{20,16},{24,28},{28,24},{1,5},{5... | collective-permute-start | bytes 884744 | tf_op jit(solution)/shard_map/ppermute | solution.py:406
  28.7 3.7 %collective-permute-done.13.refs_0_ = bf16[4,48,768]{2,1,0:T(8,128)(2,1)S(1)} collective-permute-done((bf16[4,48,768]{2,1,0:T(8,128)(2,1)S(1)}, bf16[4,48,768]{2,1,0:T(8,128)(2,1)S(1)}, u32[]{:S(2)}, u32[]{:S(2)}) %collective-permute-start.13) | collective-permute-done | bytes 294944 | tf_op jit(solution)/shard_map/ppermute | solution.py:414
  33.9 4.9 %collective-permute-done.5.refs_1_ = bf16[4,48,768]{2,1,0:T(8,128)(2,1)S(1)} collective-permute-done((bf16[4,48,768]{2,1,0:T(8,128)(2,1)S(1)}, bf16[4,48,768]{2,1,0:T(8,128)(2,1)S(1)}, u32[]{:S(2)}, u32[]{:S(2)}) %collective-permute-start.5) | collective-permute-done | bytes 294944 | tf_op jit(solution)/shard_map/ppermute | solution.py:414
  39.8 5.2 %collective-permute-done.14.refs_1_ = bf16[4,48,768]{2,1,0:T(8,128)(2,1)S(1)} collective-permute-done((bf16[4,48,768]{2,1,0:T(8,128)(2,1)S(1)}, bf16[4,48,768]{2,1,0:T(8,128)(2,1)S(1)}, u32[]{:S(2)}, u32[]{:S(2)}) %collective-permute-start.14) | collective-permute-done | bytes 294944 | tf_op jit(solution)/shard_map/ppermute | solution.py:414
  46.1 1.5 %pick.6 = (bf16[2,2,48,768]{3,2,1,0:T(8,128)(2,1)S(1)}, bf16[2,2,48,768]{3,2,1,0:T(8,128)(2,1)S(1)}) custom-call(s32[2]{0:T(128)S(1)} %pad_add_fusion.me_ref, s32[4]{0:T(128)S(1)} %fusion.7.line_ref, s32[32]{0:T(128)S(1)} %pad_add_fusion.1.want_ref, bf16[4,48,768]{2,1,0:T(8,128)(2,1)S(1)} %collective-permute-done.4.refs_0_, ...), custom_call_target="tpu_custom_call" | custom-call | bytes 1179648 | tf_op jit(solution)/shard_map/pick/pallas_call | solution.py:279
  47.6 1.6 %collective-permute-start.7 = (bf16[2,2,48,768]{3,2,1,0:T(8,128)(2,1)S(1)}, bf16[2,2,48,768]{3,2,1,0:T(8,128)(2,1)S(1)}, u32[]{:S(2)}, u32[]{:S(2)}) collective-permute-start(bf16[2,2,48,768]{3,2,1,0:T(8,128)(2,1)S(1)} %get-tuple-element.63), channel_id=1, source_target_pairs={{0,4},{4,0},{8,12},{12,8},{16,20},{20,16},{24,28},{28,24},{1,5},{5... | collective-permute-start | bytes 884744 | tf_op jit(solution)/shard_map/ppermute | solution.py:406
  49.2 1.5 %pick.8 = (bf16[2,2,48,768]{3,2,1,0:T(8,128)(2,1)S(1)}, bf16[2,2,48,768]{3,2,1,0:T(8,128)(2,1)S(1)}) custom-call(s32[2]{0:T(128)S(1)} %pad_add_fusion.me_ref, s32[4]{0:T(128)S(1)} %fusion.7.line_ref, s32[32]{0:T(128)S(1)} %pad_add_fusion.1.want_ref, bf16[4,48,768]{2,1,0:T(8,128)(2,1)S(1)} %collective-permute-done.13.refs_0_, ...), custom_call_target="tpu_custom_call" | custom-call | bytes 1179648 | tf_op jit(solution)/shard_map/pick/pallas_call | solution.py:279
  52.4 1.9 %collective-permute-start.9 = (bf16[1,2,48,768]{3,2,1,0:T(8,128)(2,1)S(1)}, bf16[1,2,48,768]{3,2,1,0:T(8,128)(2,1)S(1)}, u32[]{:S(2)}, u32[]{:S(2)}) collective-permute-start(bf16[1,2,48,768]{3,2,1,0:T(8,128)(2,1)S(1)} %get-tuple-element.65), channel_id=1, source_target_pairs={{0,4},{4,0},{8,12},{12,8},{16,20},{20,16},{24,28},{28,24},{1,5},{5... | collective-permute-start | bytes 442376 | tf_op jit(solution)/shard_map/ppermute | solution.py:406
  54.3 2.8 %collective-permute-done.16.refs_0_ = bf16[4,48,768]{2,1,0:T(8,128)(2,1)S(1)} collective-permute-done((bf16[4,48,768]{2,1,0:T(8,128)(2,1)S(1)}, bf16[4,48,768]{2,1,0:T(8,128)(2,1)S(1)}, u32[]{:S(2)}, u32[]{:S(2)}) %collective-permute-start.16) | collective-permute-done | bytes 294944 | tf_op jit(solution)/shard_map/ppermute | solution.py:414
  58.1 1.6 %collective-permute-start.17 = (bf16[1,2,48,768]{3,2,1,0:T(8,128)(2,1)S(1)}, bf16[1,2,48,768]{3,2,1,0:T(8,128)(2,1)S(1)}, u32[]{:S(2)}, u32[]{:S(2)}) collective-permute-start(bf16[1,2,48,768]{3,2,1,0:T(8,128)(2,1)S(1)} %get-tuple-element.74), channel_id=1, source_target_pairs={{0,4},{4,0},{8,12},{12,8},{16,20},{20,16},{24,28},{28,24},{1,5},{5... | collective-permute-start | bytes 442376 | tf_op jit(solution)/shard_map/ppermute | solution.py:406
  59.7 6.0 %collective-permute-done.9.refs_5_ = bf16[1,2,48,768]{3,2,1,0:T(8,128)(2,1)S(1)} collective-permute-done((bf16[1,2,48,768]{3,2,1,0:T(8,128)(2,1)S(1)}, bf16[1,2,48,768]{3,2,1,0:T(8,128)(2,1)S(1)}, u32[]{:S(2)}, u32[]{:S(2)}) %collective-permute-start.9) | collective-permute-done | bytes 147488 | tf_op jit(solution)/shard_map/ppermute | solution.py:406
  65.7 2.6 %route.3 = (bf16[2,48,768]{2,1,0:T(8,128)(2,1)S(1)}, bf16[2,48,768]{2,1,0:T(8,128)(2,1)S(1)}, bf16[2,48,768]{2,1,0:T(8,128)(2,1)S(1)}, bf16[2,48,768]{2,1,0:T(8,128)(2,1)S(1)}) custom-call(s32[2]{0:T(128)S(1)} %pad_add_fusion.me_ref, s32[4]{0:T(128)S(1)} %fusion.7.line_ref, s32[16]{0:T(128)S(1)} %get-tuple-element.85.side_ref, ...), custom_call_target="tpu_custom_call" | custom-call | bytes 1179648 | tf_op jit(solution)/shard_map/route/pallas_call | solution.py:303
  68.5 1.8 %load.2.wo = bf16[2,768,768]{2,1,0:T(8,128)(2,1)S(1)} custom-call(bf16[2,768,768]{2,1,0:T(8,128)(2,1)} %refs_0_.2), custom_call_target="tpu_custom_call" | custom-call | tf_op jit(solution)/shard_map/load/pallas_call | solution.py:239
  70.3 1.6 %collective-permute-start.11 = (bf16[2,48,768]{2,1,0:T(8,128)(2,1)S(1)}, bf16[2,48,768]{2,1,0:T(8,128)(2,1)S(1)}, u32[]{:S(2)}, u32[]{:S(2)}) collective-permute-start(bf16[2,48,768]{2,1,0:T(8,128)(2,1)S(1)} %get-tuple-element.68), channel_id=1, source_target_pairs={{0,2},{1,3},{2,0},{3,1},{4,6},{5,7},{6,4},{7,5},{8,10},{9,11},{10,... | collective-permute-start | bytes 442376 | tf_op jit(solution)/shard_map/ppermute | solution.py:444
  72.2 2.6 %route.4 = (bf16[2,48,768]{2,1,0:T(8,128)(2,1)S(1)}, bf16[2,48,768]{2,1,0:T(8,128)(2,1)S(1)}, bf16[2,48,768]{2,1,0:T(8,128)(2,1)S(1)}, bf16[2,48,768]{2,1,0:T(8,128)(2,1)S(1)}) custom-call(s32[2]{0:T(128)S(1)} %pad_add_fusion.me_ref, s32[4]{0:T(128)S(1)} %fusion.7.line_ref, s32[16]{0:T(128)S(1)} %get-tuple-element.85.side_ref, ...), custom_call_target="tpu_custom_call" | custom-call | bytes 1179648 | tf_op jit(solution)/shard_map/route/pallas_call | solution.py:303
  75.2 1.6 %collective-permute-start.19 = (bf16[2,48,768]{2,1,0:T(8,128)(2,1)S(1)}, bf16[2,48,768]{2,1,0:T(8,128)(2,1)S(1)}, u32[]{:S(2)}, u32[]{:S(2)}) collective-permute-start(bf16[2,48,768]{2,1,0:T(8,128)(2,1)S(1)} %get-tuple-element.77), channel_id=1, source_target_pairs={{0,2},{1,3},{2,0},{3,1},{4,6},{5,7},{6,4},{7,5},{8,10},{9,11},{10,... | collective-permute-start | bytes 442376 | tf_op jit(solution)/shard_map/ppermute | solution.py:444
  76.8 3.5 %route.5 = (bf16[2,96,768]{2,1,0:T(8,128)(2,1)S(1)}, bf16[2,96,768]{2,1,0:T(8,128)(2,1)S(1)}, bf16[2,96,768]{2,1,0:T(8,128)(2,1)S(1)}, bf16[2,96,768]{2,1,0:T(8,128)(2,1)S(1)}) custom-call(s32[2]{0:T(128)S(1)} %pad_add_fusion.me_ref, s32[4]{0:T(128)S(1)} %fusion.7.line_ref, s32[16]{0:T(128)S(1)} %and_select_fusion.side_ref, ...), custom_call_target="tpu_custom_call" | custom-call | bytes 2359296 | tf_op jit(solution)/shard_map/route/pallas_call | solution.py:303
  81.0 1.6 %collective-permute-start.22 = (bf16[2,96,768]{2,1,0:T(8,128)(2,1)S(1)}, bf16[2,96,768]{2,1,0:T(8,128)(2,1)S(1)}, u32[]{:S(2)}, u32[]{:S(2)}) collective-permute-start(bf16[2,96,768]{2,1,0:T(8,128)(2,1)S(1)} %get-tuple-element.81), channel_id=1, source_target_pairs={{0,2},{1,3},{2,0},{3,1},{4,6},{5,7},{6,4},{7,5},{8,10},{9,11},{10,... | collective-permute-start | bytes 884744 | tf_op jit(solution)/shard_map/ppermute | solution.py:444
  83.4 2.2 %collective-permute-done.20.refs_7_ = bf16[2,48,768]{2,1,0:T(8,128)(2,1)S(1)} collective-permute-done((bf16[2,48,768]{2,1,0:T(8,128)(2,1)S(1)}, bf16[2,48,768]{2,1,0:T(8,128)(2,1)S(1)}, u32[]{:S(2)}, u32[]{:S(2)}) %collective-permute-start.20) | collective-permute-done | bytes 147488 | tf_op jit(solution)/shard_map/ppermute | solution.py:444
  85.7 11.4 %decode.2 = f32[2,4,384]{2,1,0:T(4,128)S(1)} custom-call(s32[2]{0:T(128)S(1)} %pad_add_fusion.me_ref, f32[2,3,768]{2,1,0:T(4,128)S(1)} %copy.24.gains_ref, bf16[2,4,768]{2,1,0:T(4,128)(2,1)S(1)} %copy-done.2, bf16[2,768,1536]{2,1,0:T(8,128)(2,1)S(1)} %bitcast.16, bf16[2,768,768]{2,1,0:T(8,128)(2,1)S(1)} %copy-done.1, bf16[2,768,768]{2,1,0:T(8,128)(2,1)S(1)} %load.2.wo, ...), custom_call_target="tpu_custom_call" | custom-call | flops 5435817984 | bytes 11796480 | tf_op jit(solution)/shard_map/decode/pallas_call | solution.py:325
  98.2 10.9 %decode.3 = f32[2,4,384]{2,1,0:T(4,128)S(1)} custom-call(s32[2]{0:T(128)S(1)} %pad_add_fusion.me_ref, f32[2,3,768]{2,1,0:T(4,128)S(1)} %copy.24.gains_ref, bf16[2,4,768]{2,1,0:T(4,128)(2,1)S(1)} %copy-done.2, bf16[2,768,1536]{2,1,0:T(8,128)(2,1)S(1)} %bitcast.16, bf16[2,768,768]{2,1,0:T(8,128)(2,1)S(1)} %copy-done.1, bf16[2,768,768]{2,1,0:T(8,128)(2,1)S(1)} %load.2.wo, ...), custom_call_target="tpu_custom_call" | custom-call | flops 5435817984 | bytes 11796480 | tf_op jit(solution)/shard_map/decode/pallas_call | solution.py:325
  109.2 5.3 %all_gather.3 = f32[8,2,4,384]{3,2,1,0:T(4,128)S(1)} all-gather(f32[2,2,4,384]{3,2,1,0:T(4,128)S(1)} %pad_maximum_fusion.1), channel_id=1, replica_groups=mesh['view'=8,'mp'=4] {'mp'}, dimensions={0}, use_global_device_ids=true | all-gather | bytes 122880 | tf_op jit(solution)/shard_map/all_gather | solution.py:461
  114.9 12.6 %all_to_all.5 = f32[8,2,1664]{2,1,0:T(2,128)S(1)} all-to-all(f32[8,2,1664]{2,1,0:T(2,128)S(1)} %reshape.110), channel_id=1, replica_groups=mesh['view'=8,'mp'=4] {'view'}, dimensions={0} | all-to-all | bytes 212992 | tf_op jit(solution)/shard_map/all_to_all | solution.py:465
  (70 shorter events, 17.7 us)
Async XLA Ops:
  0.0 8.7 %copy-start = (bf16[1024,768]{1,0:T(8,128)(2,1)S(1)}, bf16[1024,768]{1,0:T(8,128)(2,1)}, u32[]{:S(2)}) copy-start(bf16[1024,768]{1,0:T(8,128)(2,1)} %refs_0_.3) | copy-start | bytes 4718596
  1.4 9.2 %collective-permute-start.2 = (bf16[4,96,256]{2,1,0:T(8,128)(2,1)S(1)}, bf16[4,96,256]{2,1,0:T(8,128)(2,1)S(1)}, u32[]{:S(2)}, u32[]{:S(2)}) collective-permute-start(bf16[4,96,256]{2,1,0:T(8,128)(2,1)S(1)} %get-tuple-element.91), channel_id=1, source_target_pairs={{0,3},{1,2},{2,1},{3,0},{4,7},{5,6},{6,5},{7,4},{8,11},{9,10},{10,... | collective-permute-start | bytes 589832 | tf_op jit(solution)/shard_map/ppermute | solution.py:367
  3.9 1.7 %collective-permute-start = (bf16[4,96,256]{2,1,0:T(8,128)(2,1)S(1)}, bf16[4,96,256]{2,1,0:T(8,128)(2,1)S(1)}, u32[]{:S(2)}, u32[]{:S(2)}) collective-permute-start(bf16[4,96,256]{2,1,0:T(8,128)(2,1)S(1)} %get-tuple-element.93), channel_id=1, source_target_pairs={{0,1},{1,0},{2,3},{3,2},{4,5},{5,4},{6,7},{7,6},{8,9},{9,8},{10,11... | collective-permute-start | bytes 589832 | tf_op jit(solution)/shard_map/ppermute | solution.py:367
  4.5 9.0 %collective-permute-start.1 = (bf16[4,96,256]{2,1,0:T(8,128)(2,1)S(1)}, bf16[4,96,256]{2,1,0:T(8,128)(2,1)S(1)}, u32[]{:S(2)}, u32[]{:S(2)}) collective-permute-start(bf16[4,96,256]{2,1,0:T(8,128)(2,1)S(1)} %get-tuple-element.94), channel_id=1, source_target_pairs={{0,2},{1,3},{2,0},{3,1},{4,6},{5,7},{6,4},{7,5},{8,10},{9,11},{10,... | collective-permute-start | bytes 589832 | tf_op jit(solution)/shard_map/ppermute | solution.py:367
  6.9 3.6 %collective-permute-start.3 = (s32[16]{0:T(128)S(1)}, s32[16]{0:T(128)S(1)}, u32[]{:S(2)}, u32[]{:S(2)}) collective-permute-start(s32[16]{0:T(128)S(1)} %get-tuple-element.96), channel_id=1, source_target_pairs={{0,4},{4,0},{8,12},{12,8},{16,20},{20,16},{24,28},{28,24},{1,5},{5... | collective-permute-start | bytes 200 | tf_op jit(solution)/shard_map/ppermute | solution.py:386
  14.8 11.3 %collective-permute-start.4 = (bf16[4,48,768]{2,1,0:T(8,128)(2,1)S(1)}, bf16[4,48,768]{2,1,0:T(8,128)(2,1)S(1)}, u32[]{:S(2)}, u32[]{:S(2)}) collective-permute-start(bf16[4,48,768]{2,1,0:T(8,128)(2,1)S(1)} %embed.2), channel_id=1, source_target_pairs={{0,8},{4,12},{8,24},{12,28},{24,16},{28,20},{16,0},{20,4},{1,9},{5... | collective-permute-start | bytes 884744 | tf_op jit(solution)/shard_map/ppermute | solution.py:414
  19.2 49.2 %copy-start.3 = (f32[2,3,768]{2,0,1:T(2,128)S(1)}, f32[2,3,768]{2,0,1:T(2,128)}, u32[]{:S(2)}) copy-start(f32[2,3,768]{2,0,1:T(2,128)} %param.16) | copy-start | bytes 55300
  19.2 13.2 %collective-permute-start.13 = (bf16[4,48,768]{2,1,0:T(8,128)(2,1)S(1)}, bf16[4,48,768]{2,1,0:T(8,128)(2,1)S(1)}, u32[]{:S(2)}, u32[]{:S(2)}) collective-permute-start(bf16[4,48,768]{2,1,0:T(8,128)(2,1)S(1)} %get-tuple-element.70), channel_id=1, source_target_pairs={{0,8},{4,12},{8,24},{12,28},{24,16},{28,20},{16,0},{20,4},{1,9},{5... | collective-permute-start | bytes 884744 | tf_op jit(solution)/shard_map/ppermute | solution.py:414
  26.1 7.8 %collective-permute-start.6 = (bf16[1,2,96,768]{3,2,1,0:T(8,128)(2,1)S(1)}, bf16[1,2,96,768]{3,2,1,0:T(8,128)(2,1)S(1)}, u32[]{:S(2)}, u32[]{:S(2)}) collective-permute-start(bf16[1,2,96,768]{3,2,1,0:T(8,128)(2,1)S(1)} %get-tuple-element.58), channel_id=1, source_target_pairs={{0,4},{4,0},{8,12},{12,8},{16,20},{20,16},{24,28},{28,24},{1,5},{5... | collective-permute-start | bytes 884744 | tf_op jit(solution)/shard_map/ppermute | solution.py:406
  27.9 10.8 %collective-permute-start.5 = (bf16[4,48,768]{2,1,0:T(8,128)(2,1)S(1)}, bf16[4,48,768]{2,1,0:T(8,128)(2,1)S(1)}, u32[]{:S(2)}, u32[]{:S(2)}) collective-permute-start(bf16[4,48,768]{2,1,0:T(8,128)(2,1)S(1)} %collective-permute-done.4.refs_0_), channel_id=1, source_target_pairs={{0,8},{4,12},{8,24},{12,28},{24,16},{28,20},{16,0},{20,4},{1,9},{5... | collective-permute-start | bytes 884744 | tf_op jit(solution)/shard_map/ppermute | solution.py:414
  32.4 12.6 %collective-permute-start.14 = (bf16[4,48,768]{2,1,0:T(8,128)(2,1)S(1)}, bf16[4,48,768]{2,1,0:T(8,128)(2,1)S(1)}, u32[]{:S(2)}, u32[]{:S(2)}) collective-permute-start(bf16[4,48,768]{2,1,0:T(8,128)(2,1)S(1)} %collective-permute-done.13.refs_0_), channel_id=1, source_target_pairs={{0,8},{4,12},{8,24},{12,28},{24,16},{28,20},{16,0},{20,4},{1,9},{5... | collective-permute-start | bytes 884744 | tf_op jit(solution)/shard_map/ppermute | solution.py:414
  38.7 12.6 %collective-permute-start.8 = (bf16[4,48,768]{2,1,0:T(8,128)(2,1)S(1)}, bf16[4,48,768]{2,1,0:T(8,128)(2,1)S(1)}, u32[]{:S(2)}, u32[]{:S(2)}) collective-permute-start(bf16[4,48,768]{2,1,0:T(8,128)(2,1)S(1)} %collective-permute-done.5.refs_1_), channel_id=1, source_target_pairs={{0,8},{4,12},{8,24},{12,28},{24,16},{28,20},{16,0},{20,4},{1,9},{5... | collective-permute-start | bytes 884744 | tf_op jit(solution)/shard_map/ppermute | solution.py:414
  45.0 12.0 %collective-permute-start.16 = (bf16[4,48,768]{2,1,0:T(8,128)(2,1)S(1)}, bf16[4,48,768]{2,1,0:T(8,128)(2,1)S(1)}, u32[]{:S(2)}, u32[]{:S(2)}) collective-permute-start(bf16[4,48,768]{2,1,0:T(8,128)(2,1)S(1)} %collective-permute-done.14.refs_1_), channel_id=1, source_target_pairs={{0,8},{4,12},{8,24},{12,28},{24,16},{28,20},{16,0},{20,4},{1,9},{5... | collective-permute-start | bytes 884744 | tf_op jit(solution)/shard_map/ppermute | solution.py:414
  47.6 12.1 %collective-permute-start.7 = (bf16[2,2,48,768]{3,2,1,0:T(8,128)(2,1)S(1)}, bf16[2,2,48,768]{3,2,1,0:T(8,128)(2,1)S(1)}, u32[]{:S(2)}, u32[]{:S(2)}) collective-permute-start(bf16[2,2,48,768]{3,2,1,0:T(8,128)(2,1)S(1)} %get-tuple-element.63), channel_id=1, source_target_pairs={{0,4},{4,0},{8,12},{12,8},{16,20},{20,16},{24,28},{28,24},{1,5},{5... | collective-permute-start | bytes 884744 | tf_op jit(solution)/shard_map/ppermute | solution.py:406
  50.7 21.5 %collective-permute-start.15 = (bf16[2,2,48,768]{3,2,1,0:T(8,128)(2,1)S(1)}, bf16[2,2,48,768]{3,2,1,0:T(8,128)(2,1)S(1)}, u32[]{:S(2)}, u32[]{:S(2)}) collective-permute-start(bf16[2,2,48,768]{3,2,1,0:T(8,128)(2,1)S(1)} %get-tuple-element.72), channel_id=1, source_target_pairs={{0,4},{4,0},{8,12},{12,8},{16,20},{20,16},{24,28},{28,24},{1,5},{5... | collective-permute-start | bytes 884744 | tf_op jit(solution)/shard_map/ppermute | solution.py:406
  52.4 13.3 %collective-permute-start.9 = (bf16[1,2,48,768]{3,2,1,0:T(8,128)(2,1)S(1)}, bf16[1,2,48,768]{3,2,1,0:T(8,128)(2,1)S(1)}, u32[]{:S(2)}, u32[]{:S(2)}) collective-permute-start(bf16[1,2,48,768]{3,2,1,0:T(8,128)(2,1)S(1)} %get-tuple-element.65), channel_id=1, source_target_pairs={{0,4},{4,0},{8,12},{12,8},{16,20},{20,16},{24,28},{28,24},{1,5},{5... | collective-permute-start | bytes 442376 | tf_op jit(solution)/shard_map/ppermute | solution.py:406
  58.1 14.1 %collective-permute-start.17 = (bf16[1,2,48,768]{3,2,1,0:T(8,128)(2,1)S(1)}, bf16[1,2,48,768]{3,2,1,0:T(8,128)(2,1)S(1)}, u32[]{:S(2)}, u32[]{:S(2)}) collective-permute-start(bf16[1,2,48,768]{3,2,1,0:T(8,128)(2,1)S(1)} %get-tuple-element.74), channel_id=1, source_target_pairs={{0,4},{4,0},{8,12},{12,8},{16,20},{20,16},{24,28},{28,24},{1,5},{5... | collective-permute-start | bytes 442376 | tf_op jit(solution)/shard_map/ppermute | solution.py:406
  68.3 8.4 %collective-permute-start.10 = (bf16[2,48,768]{2,1,0:T(8,128)(2,1)S(1)}, bf16[2,48,768]{2,1,0:T(8,128)(2,1)S(1)}, u32[]{:S(2)}, u32[]{:S(2)}) collective-permute-start(bf16[2,48,768]{2,1,0:T(8,128)(2,1)S(1)} %get-tuple-element.67), channel_id=1, source_target_pairs={{0,1},{1,0},{2,3},{3,2},{4,5},{5,4},{6,7},{7,6},{8,9},{9,8},{10,11... | collective-permute-start | bytes 442376 | tf_op jit(solution)/shard_map/ppermute | solution.py:444
  68.4 17.2 %slice-start = ((s8[4718592]{0:T(1024)(128)(4,1)}), s8[4194304]{0:T(1024)(128)(4,1)S(1)}, s32[]{:S(2)}) async-start(s8[4718592]{0:T(1024)(128)(4,1)} %bitcast.15), calls=%async_computation.1 | async-start | bytes 8388608
  68.4 17.2 %slice-start.1 = ((s8[4718592]{0:T(1024)(128)(4,1)}), s8[524288]{0:T(1024)(128)(4,1)S(1)}, s32[]{:S(2)}) async-start(s8[4718592]{0:T(1024)(128)(4,1)} %bitcast.15), calls=%async_computation.2 | async-start | bytes 1048576
  70.3 15.4 %copy-start.1 = (bf16[2,768,768]{2,1,0:T(8,128)(2,1)S(1)}, bf16[2,768,768]{2,1,0:T(8,128)(2,1)}, u32[]{:S(2)}) copy-start(bf16[2,768,768]{2,1,0:T(8,128)(2,1)} %wq.3) | copy-start | bytes 7077892
  70.3 15.4 %copy-start.2 = (bf16[2,4,768]{2,1,0:T(4,128)(2,1)S(1)}, bf16[2,4,768]{2,1,0:T(4,128)(2,1)}, u32[]{:S(2)}) copy-start(bf16[2,4,768]{2,1,0:T(4,128)(2,1)} %whead_ref.3) | copy-start | bytes 36868
  70.3 10.0 %collective-permute-start.11 = (bf16[2,48,768]{2,1,0:T(8,128)(2,1)S(1)}, bf16[2,48,768]{2,1,0:T(8,128)(2,1)S(1)}, u32[]{:S(2)}, u32[]{:S(2)}) collective-permute-start(bf16[2,48,768]{2,1,0:T(8,128)(2,1)S(1)} %get-tuple-element.68), channel_id=1, source_target_pairs={{0,2},{1,3},{2,0},{3,1},{4,6},{5,7},{6,4},{7,5},{8,10},{9,11},{10,... | collective-permute-start | bytes 442376 | tf_op jit(solution)/shard_map/ppermute | solution.py:444
  71.9 9.1 %collective-permute-start.12 = (bf16[2,48,768]{2,1,0:T(8,128)(2,1)S(1)}, bf16[2,48,768]{2,1,0:T(8,128)(2,1)S(1)}, u32[]{:S(2)}, u32[]{:S(2)}) collective-permute-start(bf16[2,48,768]{2,1,0:T(8,128)(2,1)S(1)} %get-tuple-element.69), channel_id=1, source_target_pairs={{0,3},{1,2},{2,1},{3,0},{4,7},{5,6},{6,5},{7,4},{8,11},{9,10},{10,... | collective-permute-start | bytes 442376 | tf_op jit(solution)/shard_map/ppermute | solution.py:444
  74.8 7.7 %collective-permute-start.18 = (bf16[2,48,768]{2,1,0:T(8,128)(2,1)S(1)}, bf16[2,48,768]{2,1,0:T(8,128)(2,1)S(1)}, u32[]{:S(2)}, u32[]{:S(2)}) collective-permute-start(bf16[2,48,768]{2,1,0:T(8,128)(2,1)S(1)} %get-tuple-element.76), channel_id=1, source_target_pairs={{0,1},{1,0},{2,3},{3,2},{4,5},{5,4},{6,7},{7,6},{8,9},{9,8},{10,11... | collective-permute-start | bytes 442376 | tf_op jit(solution)/shard_map/ppermute | solution.py:444
  75.2 8.2 %collective-permute-start.19 = (bf16[2,48,768]{2,1,0:T(8,128)(2,1)S(1)}, bf16[2,48,768]{2,1,0:T(8,128)(2,1)S(1)}, u32[]{:S(2)}, u32[]{:S(2)}) collective-permute-start(bf16[2,48,768]{2,1,0:T(8,128)(2,1)S(1)} %get-tuple-element.77), channel_id=1, source_target_pairs={{0,2},{1,3},{2,0},{3,1},{4,6},{5,7},{6,4},{7,5},{8,10},{9,11},{10,... | collective-permute-start | bytes 442376 | tf_op jit(solution)/shard_map/ppermute | solution.py:444
  76.8 8.9 %collective-permute-start.20 = (bf16[2,48,768]{2,1,0:T(8,128)(2,1)S(1)}, bf16[2,48,768]{2,1,0:T(8,128)(2,1)S(1)}, u32[]{:S(2)}, u32[]{:S(2)}) collective-permute-start(bf16[2,48,768]{2,1,0:T(8,128)(2,1)S(1)} %get-tuple-element.78), channel_id=1, source_target_pairs={{0,3},{1,2},{2,1},{3,0},{4,7},{5,6},{6,5},{7,4},{8,11},{9,10},{10,... | collective-permute-start | bytes 442376 | tf_op jit(solution)/shard_map/ppermute | solution.py:444
  80.3 16.7 %collective-permute-start.21 = (bf16[2,96,768]{2,1,0:T(8,128)(2,1)S(1)}, bf16[2,96,768]{2,1,0:T(8,128)(2,1)S(1)}, u32[]{:S(2)}, u32[]{:S(2)}) collective-permute-start(bf16[2,96,768]{2,1,0:T(8,128)(2,1)S(1)} %get-tuple-element.80), channel_id=1, source_target_pairs={{0,1},{1,0},{2,3},{3,2},{4,5},{5,4},{6,7},{7,6},{8,9},{9,8},{10,11... | collective-permute-start | bytes 884744 | tf_op jit(solution)/shard_map/ppermute | solution.py:444
  81.0 16.1 %collective-permute-start.22 = (bf16[2,96,768]{2,1,0:T(8,128)(2,1)S(1)}, bf16[2,96,768]{2,1,0:T(8,128)(2,1)S(1)}, u32[]{:S(2)}, u32[]{:S(2)}) collective-permute-start(bf16[2,96,768]{2,1,0:T(8,128)(2,1)S(1)} %get-tuple-element.81), channel_id=1, source_target_pairs={{0,2},{1,3},{2,0},{3,1},{4,6},{5,7},{6,4},{7,5},{8,10},{9,11},{10,... | collective-permute-start | bytes 884744 | tf_op jit(solution)/shard_map/ppermute | solution.py:444
  82.6 15.7 %collective-permute-start.23 = (bf16[2,96,768]{2,1,0:T(8,128)(2,1)S(1)}, bf16[2,96,768]{2,1,0:T(8,128)(2,1)S(1)}, u32[]{:S(2)}, u32[]{:S(2)}) collective-permute-start(bf16[2,96,768]{2,1,0:T(8,128)(2,1)S(1)} %get-tuple-element.82), channel_id=1, source_target_pairs={{0,3},{1,2},{2,1},{3,0},{4,7},{5,6},{6,5},{7,4},{8,11},{9,10},{10,... | collective-permute-start | bytes 884744 | tf_op jit(solution)/shard_map/ppermute | solution.py:444
